TPU v7x, 32 devices: a whole 2x2x4 slice. The times are simulated.
32 devices in a mesh: dp: 16 (over z, y, x), seq: 2 (over core).
Axes of the slice: x: 2, y: 2, z: 4, core: 2. Of those that a mesh axis runs over, the one named last changes fastest.
Arguments:
- tokens: bfloat16 [16384, 768], P(('dp', 'seq')), may hold values from -6 to 6
- doc_lengths: int32 [16, 4], P('dp'), may hold values from 0 to 1024, as said below
- w_query: bfloat16 [768, 768], replicated, may hold values from -0.21875 to 0.21875
- w_key: bfloat16 [768, 768], replicated, may hold values from -0.21875 to 0.21875
- w_value: bfloat16 [768, 768], replicated, may hold values from -0.21875 to 0.21875
- w_out: bfloat16 [768, 768], replicated, may hold values from -0.875 to 0.875
- w_gate: bfloat16 [768, 2560], replicated, may hold values from -0.21875 to 0.21875
- w_up: bfloat16 [768, 2560], replicated, may hold values from -0.21875 to 0.21875
- w_down: bfloat16 [2560, 768], replicated, may hold values from -0.125 to 0.125
- gain_attn: float32 [768], replicated, may hold values from 0.5 to 1.5
- gain_ffn: float32 [768], replicated, may hold values from 0.5 to 1.5
- cotangent: bfloat16 [16384, 768], P(('dp', 'seq')), may hold values from -6 to 6
Outputs:
- output: bfloat16 [16384, 768], P(('dp', 'seq'))
- grad_tokens: bfloat16 [16384, 768], P(('dp', 'seq'))
- grad_query: float32 [768, 768], P('dp', 'seq')
- grad_key: float32 [768, 768], P('dp', 'seq')
- grad_value: float32 [768, 768], P('dp', 'seq')
- grad_out: float32 [768, 768], P('seq', 'dp')
- grad_gate: float32 [768, 2560], P('dp', 'seq')
- grad_up: float32 [768, 2560], P('dp', 'seq')
- grad_down: float32 [2560, 768], P('seq', 'dp')
- grad_gain_attn: float32 [768], replicated
- grad_gain_ffn: float32 [768], replicated
- rms_stats: float32 [3], replicated
Inputs may be any that keep to these rules, and one draw needn't show every extreme that they name: `doc_lengths`: each row lists the documents of one pack: lengths of 1, 2 or 4 times 1024//4, nonzero ones first, summing to 1024 or 768; the first pack is one document of 1024 tokens.
All inputs are finite; a program needn't handle non-finite values.
Results may differ from a plain program's by a relative error of at most 0.014.
Values may be sent and summed in bfloat16 or wider, within the bound.
No kernel may reach another device: no remote copies, remote signals or barrier semaphores. Data moves between devices by JAX's collectives and lax.ppermute only.
A program may use at most 256 MiB of HBM per device.

v0:
```python
import math

import jax
import jax.numpy as jnp
from jax import lax
from jax.sharding import PartitionSpec as P

HDIM = 48


def rms_norm(stream, gain_vector):
    return (
        stream * lax.rsqrt(jnp.mean(stream * stream, axis=-1, keepdims=True) + 1e-06) * gain_vector
    )


def swiglu(gate_proj, up_proj):
    return jax.nn.silu(gate_proj) * up_proj


def rotate(values, cosine_table, sine_table):
    middle = values.shape[-1] // 2
    front_half = values[..., :middle]
    back_half = values[..., middle:]
    return jnp.concatenate(
        [
            front_half * cosine_table - back_half * sine_table,
            back_half * cosine_table + front_half * sine_table,
        ],
        axis=-1,
    )


def angles(position, head_size):
    middle = head_size // 2
    frequency = jnp.exp(jnp.arange(middle, dtype=jnp.float32) * (-math.log(10000.0) / middle))
    phases = position.astype(jnp.float32)[:, None] * frequency[None, :]
    return (jnp.cos(phases)[:, None, :], jnp.sin(phases)[:, None, :])


def layout(lengths, span):
    finish = jnp.cumsum(lengths, dtype=jnp.int32)
    begins = jnp.concatenate([finish - lengths, finish[-1:]])
    places = jnp.arange(span, dtype=jnp.int32)
    segment = jnp.sum(
        (places[:, None] >= finish[None, :]).astype(jnp.int32), axis=1, dtype=jnp.int32
    )
    chosen = segment[:, None] == jnp.arange(begins.shape[0], dtype=jnp.int32)[None, :]
    opening = jnp.sum(jnp.where(chosen, begins[None, :], 0), axis=1, dtype=jnp.int32)
    return (segment, places - opening, places < finish[-1])


def shards(
    tokens,
    doc_lengths,
    w_query,
    w_key,
    w_value,
    w_out,
    w_gate,
    w_up,
    w_down,
    gain_attn,
    gain_ffn,
    cotangent,
):
    row_count = tokens.shape[0]
    width = tokens.shape[1]
    seq_index = lax.axis_index("seq")
    seq_parts = lax.axis_size("seq")
    pack_rows = row_count * seq_parts
    head_cols = w_query.shape[1] // seq_parts
    local_heads = head_cols // HDIM
    score_scale = 1.0 / math.sqrt(HDIM)
    segment, position, valid_rows = layout(doc_lengths[0], pack_rows)
    own_valid = lax.dynamic_slice_in_dim(valid_rows, seq_index * row_count, row_count, 0).astype(
        jnp.float32
    )[:, None]
    col_start = seq_index * head_cols
    w_qkv = jnp.concatenate(
        [
            lax.dynamic_slice_in_dim(w_query, col_start, head_cols, 1),
            lax.dynamic_slice_in_dim(w_key, col_start, head_cols, 1),
            lax.dynamic_slice_in_dim(w_value, col_start, head_cols, 1),
        ],
        axis=1,
    )
    w_out_rows = lax.dynamic_slice_in_dim(w_out, col_start, head_cols, 0)
    stream = tokens.astype(jnp.float32)
    gathered = lax.all_gather(tokens, "seq", axis=0, tiled=True)
    projected = jnp.dot(gathered, w_qkv, preferred_element_type=jnp.float32)
    cosine_table, sine_table = angles(position, HDIM)
    head_shape = (pack_rows, local_heads, HDIM)
    query_proj = projected[:, :head_cols].reshape(head_shape)
    key_proj = projected[:, head_cols : 2 * head_cols].reshape(head_shape)
    query_rot, rope_back = jax.vjp(
        lambda values_in: rotate(values_in, cosine_table, sine_table), query_proj
    )
    key_rot = rotate(key_proj, cosine_table, sine_table)
    query_low = query_rot.astype(jnp.bfloat16)
    key_low = key_rot.astype(jnp.bfloat16)
    value_low = projected[:, 2 * head_cols :].reshape(head_shape).astype(jnp.bfloat16)
    block_rows = min(512, pack_rows)
    block_total = pack_rows // block_rows
    places = jnp.arange(pack_rows, dtype=jnp.int32)

    def scores_of(block_index):
        query_from = block_index * block_rows
        key_end = query_from + block_rows
        raw_scores = jnp.einsum(
            "qhd,khd->hqk",
            query_low[query_from:key_end],
            key_low[:key_end],
            preferred_element_type=jnp.float32,
        )
        allowed = (segment[query_from:key_end, None] == segment[None, :key_end]) & (
            places[query_from:key_end, None] >= places[None, :key_end]
        )
        return jnp.where(allowed[None], raw_scores * score_scale, -1e30)

    contexts = []
    lse_parts = []
    for block_index in range(block_total):
        key_end = (block_index + 1) * block_rows
        scores = scores_of(block_index)
        row_max = jnp.max(scores, axis=-1, keepdims=True)
        exp_scores = jnp.exp(scores - row_max)
        row_total = jnp.sum(exp_scores, axis=-1, keepdims=True)
        attn_probs = (exp_scores / row_total).astype(jnp.bfloat16)
        lse_parts.append(row_max + jnp.log(row_total))
        contexts.append(
            jnp.einsum(
                "hqk,khd->qhd", attn_probs, value_low[:key_end], preferred_element_type=jnp.float32
            )
        )
    context_low = (
        jnp.concatenate(contexts, axis=0).reshape(pack_rows, head_cols).astype(jnp.bfloat16)
    )
    attn_out = lax.psum_scatter(
        jnp.dot(context_low, w_out_rows, preferred_element_type=jnp.float32),
        "seq",
        scatter_dimension=0,
        tiled=True,
    )
    normed, norm_one_back = jax.vjp(rms_norm, stream + attn_out, gain_attn)
    normed_low = normed.astype(jnp.bfloat16)
    gate_cols, up_cols, down_rows = (w_gate, w_up, w_down)
    gate_proj = jnp.dot(normed_low, gate_cols, preferred_element_type=jnp.float32)
    up_proj = jnp.dot(normed_low, up_cols, preferred_element_type=jnp.float32)
    hidden, swiglu_back = jax.vjp(swiglu, gate_proj, up_proj)
    hidden_low = hidden.astype(jnp.bfloat16)
    ffn_out = jnp.dot(hidden_low, down_rows, preferred_element_type=jnp.float32)
    result, norm_two_back = jax.vjp(rms_norm, normed + ffn_out, gain_ffn)
    stat_terms = jnp.stack(
        [
            jnp.sum(own_valid * stream * stream),
            jnp.sum(own_valid * attn_out * attn_out),
            jnp.sum(own_valid * ffn_out * ffn_out),
            jnp.sum(own_valid),
        ]
    )
    stat_totals = lax.psum(stat_terms, ("dp", "seq"))
    grad_result = cotangent.astype(jnp.float32) * own_valid
    grad_mix, grad_gain_two = norm_two_back(grad_result)
    grad_ffn_low = grad_mix.astype(jnp.bfloat16)
    grad_hidden = jnp.dot(grad_ffn_low, down_rows.T, preferred_element_type=jnp.float32)
    grad_gate_f, grad_up_f = swiglu_back(grad_hidden)
    grad_gate_low = grad_gate_f.astype(jnp.bfloat16)
    grad_up_low = grad_up_f.astype(jnp.bfloat16)
    grad_normed_ffn = jnp.dot(
        grad_gate_low, gate_cols.T, preferred_element_type=jnp.float32
    ) + jnp.dot(grad_up_low, up_cols.T, preferred_element_type=jnp.float32)
    weight_gate = jnp.dot(normed_low.T, grad_gate_low, preferred_element_type=jnp.float32)
    weight_up = jnp.dot(normed_low.T, grad_up_low, preferred_element_type=jnp.float32)
    weight_down_t = jnp.dot(grad_ffn_low.T, hidden_low, preferred_element_type=jnp.float32)
    weight_gate, weight_up, weight_down_t = (
        lax.psum_scatter(
            weight_gate.astype(jnp.bfloat16), "seq", scatter_dimension=1, tiled=True
        ).astype(jnp.float32),
        lax.psum_scatter(
            weight_up.astype(jnp.bfloat16), "seq", scatter_dimension=1, tiled=True
        ).astype(jnp.float32),
        lax.psum_scatter(
            weight_down_t.astype(jnp.bfloat16), "seq", scatter_dimension=1, tiled=True
        ).astype(jnp.float32),
    )
    grad_stream_one, grad_gain_one = norm_one_back(grad_mix + grad_normed_ffn)
    grad_attn_low = grad_stream_one.astype(jnp.bfloat16)
    grad_attn_all = lax.all_gather(grad_attn_low, "seq", axis=0, tiled=True)
    grad_context_low = jnp.dot(
        grad_attn_all, w_out_rows.T, preferred_element_type=jnp.float32
    ).astype(jnp.bfloat16)
    weight_out_t = jnp.dot(grad_attn_all.T, context_low, preferred_element_type=jnp.float32)
    grad_context_heads = grad_context_low.reshape(head_shape)
    grad_query_rot = jnp.zeros(head_shape, jnp.float32)
    grad_key_rot = jnp.zeros(head_shape, jnp.float32)
    grad_value = jnp.zeros(head_shape, jnp.float32)
    for block_index in range(block_total):
        query_from = block_index * block_rows
        key_end = query_from + block_rows
        scores = scores_of(block_index)
        attn_probs = jnp.exp(scores - lse_parts[block_index])
        probs_low = attn_probs.astype(jnp.bfloat16)
        context_block = grad_context_heads[query_from:key_end]
        grad_probs = jnp.einsum(
            "qhd,khd->hqk", context_block, value_low[:key_end], preferred_element_type=jnp.float32
        )
        grad_scores = (
            attn_probs
            * (grad_probs - jnp.sum(attn_probs * grad_probs, axis=-1, keepdims=True))
            * score_scale
        ).astype(jnp.bfloat16)
        grad_query_rot = grad_query_rot.at[query_from:key_end].set(
            jnp.einsum(
                "hqk,khd->qhd", grad_scores, key_low[:key_end], preferred_element_type=jnp.float32
            )
        )
        grad_key_rot = grad_key_rot.at[:key_end].add(
            jnp.einsum(
                "hqk,qhd->khd",
                grad_scores,
                query_low[query_from:key_end],
                preferred_element_type=jnp.float32,
            )
        )
        grad_value = grad_value.at[:key_end].add(
            jnp.einsum("hqk,qhd->khd", probs_low, context_block, preferred_element_type=jnp.float32)
        )
    grad_query_f = rope_back(grad_query_rot)[0]
    grad_key_f = rope_back(grad_key_rot)[0]
    grad_qkv_low = jnp.concatenate(
        [
            grad_query_f.reshape(pack_rows, head_cols),
            grad_key_f.reshape(pack_rows, head_cols),
            grad_value.reshape(pack_rows, head_cols),
        ],
        axis=1,
    ).astype(jnp.bfloat16)
    weight_qkv = jnp.dot(gathered.T, grad_qkv_low, preferred_element_type=jnp.float32)
    grad_stream_proj = lax.psum_scatter(
        jnp.dot(grad_qkv_low, w_qkv.T, preferred_element_type=jnp.float32).astype(jnp.bfloat16),
        "seq",
        scatter_dimension=0,
        tiled=True,
    ).astype(jnp.float32)
    grad_tokens = (grad_stream_one + grad_stream_proj).astype(jnp.bfloat16)
    summed_qkv, summed_out_t, summed_gate, summed_up, summed_down_t = (
        lax.psum_scatter(weight_qkv, "dp", scatter_dimension=0, tiled=True),
        lax.psum_scatter(weight_out_t, "dp", scatter_dimension=0, tiled=True),
        lax.psum_scatter(weight_gate, "dp", scatter_dimension=0, tiled=True),
        lax.psum_scatter(weight_up, "dp", scatter_dimension=0, tiled=True),
        lax.psum_scatter(weight_down_t, "dp", scatter_dimension=0, tiled=True),
    )
    total_gain_one, total_gain_two = lax.psum((grad_gain_one, grad_gain_two), ("dp", "seq"))
    rms_values = jnp.sqrt(stat_totals[:3] / (stat_totals[3] * width))
    return (
        result.astype(jnp.bfloat16),
        grad_tokens,
        summed_qkv[:, :head_cols],
        summed_qkv[:, head_cols : 2 * head_cols],
        summed_qkv[:, 2 * head_cols :],
        summed_out_t.T,
        summed_gate,
        summed_up,
        summed_down_t.T,
        total_gain_one,
        total_gain_two,
        rms_values,
    )


def solution(mesh):
    return jax.shard_map(
        shards,
        mesh=mesh,
        in_specs=(
            P(("dp", "seq"), None),
            P("dp", None),
            P(),
            P(),
            P(),
            P(),
            P(),
            P(),
            P(),
            P(),
            P(),
            P(("dp", "seq"), None),
        ),
        out_specs=(
            P(("dp", "seq"), None),
            P(("dp", "seq"), None),
            P("dp", "seq"),
            P("dp", "seq"),
            P("dp", "seq"),
            P("seq", "dp"),
            P("dp", "seq"),
            P("dp", "seq"),
            P("seq", "dp"),
            P(),
            P(),
            P(),
        ),
        check_vma=False,
    )
```

profile of v0, /device:TPU:0, one launch (start us, length us, event | category | flops | bytes accessed | tf_op | source)
XLA Modules:
  0.0 968.8 jit_solution(959750205616758648)
XLA Ops:
  16.6 5.5 all-gather.3.cloned.1.call-done
  22.1 3.5 fusion.132
  33.9 4.5 fusion.83
  38.3 3.5 fusion.5
  41.9 3.8 fusion.84
  51.3 10.6 %reduce-scatter.13.cloned.1.call-done = f32[512,768]{1,0:T(8,128)} async-done(((f32[1024,768]{1,0:T(8,128)}), f32[512,768]{1,0:T(8,128)}) %reduce-scatter.13.cloned.1.call-update) | async-done | bytes 1572880 | tf_op jit(solution)/shard_map/reduce_scatter | solution.py:139
  67.1 4.8 multiply_convert_fusion.3
  76.7 7.5 multiply_convert_fusion.2
  84.1 4.1 fusion.135
  94.2 6.0 convolution_convert_fusion.2
  100.2 6.0 convolution_convert_fusion.1
  107.3 6.6 convolution_convert_fusion
  119.3 8.1 fusion.137
  127.4 37.8 %fusion.78 = f32[512,8,48]{0,2,1:T(8,128)} fusion(f32[8,512,1024]{2,1,0:T(8,128)} %fusion.137, f32[8,512,1024]{2,1,0:T(8,128)} %copy-done.1, f32[8,512]{1,0:T(8,128)S(1)} %log_add_fusion, bf16[1024,8,24]{0,2,1:T(8,128)(2,1)S(1)} %copy-done.14, bf16[1024,8,24]{0,2,1:T(8,128)(2,1)S(1)} %copy-done.16), kind=kOutput, calls=%fused_computation.94 | convolution fusion | flops 433591296 | bytes 35143680 | tf_op jit(solution)/shard_map/hqk,khd->qhd/dot_general | solution.py:214
  165.2 5.6 fusion.136
  170.9 16.9 %fusion.72 = f32[512,8,48]{0,2,1:T(8,128)} fusion(f32[8,512,512]{1,2,0:T(8,128)} %fusion.136, f32[8,512,512]{1,2,0:T(8,128)} %copy-done.2, f32[8,512]{1,0:T(8,128)} %log_add_fusion.1, pred[512,512]{0,1:T(8,128)(4,1)} %compare_and_fusion, bf16[1024,8,24]{0,2,1:T(8,128)(2,1)} %copy-done.13, bf16[1024,8,24]{0,2,1:T(8,128)(2,1)} %copy-done.15), kind=kOutput, calls=%fused_computation.92 | convolution fusion | flops 225186304 | bytes 18628608 | tf_op jit(solution)/shard_map/hqk,khd->qhd/dot_general | solution.py:214
  187.8 17.0 %fusion.75 = f32[512,8,48]{0,2,1:T(8,128)} fusion(f32[8,512,512]{1,2,0:T(8,128)} %fusion.136, f32[8,512,512]{1,2,0:T(8,128)} %copy-done.2, f32[8,512]{1,0:T(8,128)} %log_add_fusion.1, pred[512,512]{0,1:T(8,128)(4,1)} %compare_and_fusion, bf16[1024,8,24]{0,2,1:T(8,128)(2,1)S(1)} %copy-done.10, bf16[1024,8,24]{0,2,1:T(8,128)(2,1)S(1)} %copy-done.12), kind=kOutput, calls=%fused_computation.93 | convolution fusion | flops 225186304 | bytes 35684352 | tf_op jit(solution)/shard_map/hqk,qhd->khd/dot_general | solution.py:219
  204.8 30.6 %bitcast_add_fusion.1 = f32[1024,8,48]{0,2,1:T(8,128)} fusion(f32[512,8,48]{0,2,1:T(8,128)} %fusion.75, f32[8,512,1024]{2,1,0:T(8,128)} %fusion.137, f32[8,512,1024]{2,1,0:T(8,128)} %copy-done.1, f32[8,512]{1,0:T(8,128)S(1)} %log_add_fusion, bf16[1024,8,24]{0,2,1:T(8,128)(2,1)S(1)} %copy-done.12, bf16[1024,8,24]{0,2,1:T(8,128)(2,1)S(1)} %copy-done.10), kind=kOutput, calls=%fused_computation.74 | convolution fusion | flops 433198080 | bytes 36716544 | tf_op jit(solution)/shard_map/hqk,qhd->khd/dot_general | solution.py:219
  239.3 5.8 fusion.69
  245.1 7.5 fusion.63
  257.0 5.6 convolution_bitcast_fusion.1
  262.6 5.2 copy.49
  268.9 3.5 fusion.138
  272.5 3.7 convert_element_type.124
  276.3 3.7 convert_element_type.126
  280.2 3.8 convert_element_type.128
  287.4 41.0 %all-reduce.6 = (f32[768]{0:T(1024)}, f32[768]{0:T(1024)}, f32[4]{0:T(128)S(1)}) all-reduce(f32[768]{0:T(1024)S(1)} %copy-done.59, f32[768]{0:T(1024)S(1)} %copy-done.54, f32[4]{0:T(128)S(1)} %pad_maximum_fusion.17), channel_id=1, replica_groups=mesh['dp'=16,'seq'=2] {'dp','seq'}, use_global_device_ids=true, to_apply=%region_24.25 | all-reduce | flops 1540 | bytes 12320 | tf_op jit(solution)/shard_map/psum | solution.py:254
  333.2 75.8 %reduce-scatter.31.cloned.1.call-done = f32[48,1152]{1,0:T(8,128)} async-done(((f32[768,1152]{1,0:T(8,128)}), f32[48,1152]{1,0:T(8,128)}) %reduce-scatter.31.cloned.1.call-update) | async-done | bytes 221200
  410.6 127.7 %reduce-scatter.17.cloned.1.call-done = f32[48,384]{1,0:T(8,128)} async-done(((f32[768,384]{1,0:T(8,128)}), f32[48,384]{1,0:T(8,128)}) %reduce-scatter.17.cloned.1.call-update) | async-done | bytes 73744 | tf_op jit(solution)/shard_map/reduce_scatter | solution.py:249
  538.3 141.1 %reduce-scatter.21.cloned.1.call-done = f32[48,1280]{1,0:T(8,128)} async-done(((f32[768,1280]{1,0:T(8,128)}), f32[48,1280]{1,0:T(8,128)}) %reduce-scatter.21.cloned.1.call-update) | async-done | bytes 245776 | tf_op jit(solution)/shard_map/reduce_scatter | solution.py:250
  679.4 141.5 %reduce-scatter.25.cloned.1.call-done = f32[48,1280]{1,0:T(8,128)} async-done(((f32[768,1280]{1,0:T(8,128)}), f32[48,1280]{1,0:T(8,128)}) %reduce-scatter.25.cloned.1.call-update) | async-done | bytes 245776 | tf_op jit(solution)/shard_map/reduce_scatter | solution.py:251
  820.8 141.0 %reduce-scatter.29.cloned.1.call-done = f32[48,1280]{1,0:T(8,128)} async-done(((f32[768,1280]{1,0:T(8,128)}), f32[48,1280]{1,0:T(8,128)}) %reduce-scatter.29.cloned.1.call-update) | async-done | bytes 245776 | tf_op jit(solution)/shard_map/reduce_scatter | solution.py:252
  (219 shorter events, 63.6 us)
Async XLA Ops:
  7.2 39.6 %copy-start = (bf16[768,768]{1,0:T(8,128)(2,1)S(1)}, bf16[768,768]{1,0:T(8,128)(2,1)}, u32[]{:S(2)}) copy-start(bf16[768,768]{1,0:T(8,128)(2,1)} %param.33) | copy-start | bytes 3538948
  7.2 14.9 %all-gather.3.cloned.1.call-start = ((), (), s32[]{:S(2)}) async-start(), calls=%async_computation.10 | async-start | bytes 2359296 | tf_op jit(solution)/shard_map/all_gather | solution.py:90
  7.9 54.0 %reduce-scatter.13.cloned.1.call-start = ((), (), s32[]{:S(2)}) async-start(), calls=%async_computation.11 | async-start | bytes 4718592 | tf_op jit(solution)/shard_map/reduce_scatter | solution.py:139
  12.1 13.5 %copy-start.39 = (bf16[768,384]{1,0:T(8,128)(2,1)}, bf16[768,384]{1,0:T(8,128)(2,1)S(1)}, u32[]{:S(2)}) copy-start(bf16[768,384]{1,0:T(8,128)(2,1)S(1)} %constant_dynamic-slice_fusion.2) | copy-start | bytes 1769476
  13.7 11.9 %copy-start.35 = (bf16[768,384]{1,0:T(8,128)(2,1)}, bf16[768,384]{1,0:T(8,128)(2,1)S(1)}, u32[]{:S(2)}) copy-start(bf16[768,384]{1,0:T(8,128)(2,1)S(1)} %get-tuple-element.188) | copy-start | bytes 1769476
  13.7 11.9 %copy-start.37 = (bf16[768,384]{1,0:T(8,128)(2,1)}, bf16[768,384]{1,0:T(8,128)(2,1)S(1)}, u32[]{:S(2)}) copy-start(bf16[768,384]{1,0:T(8,128)(2,1)S(1)} %get-tuple-element.189) | copy-start | bytes 1769476
  14.2 11.8 %copy-start.29 = (f32[1024,24]{0,1:T(8,128)}, f32[1024,24]{0,1:T(8,128)S(1)}, u32[]{:S(2)}) copy-start(f32[1024,24]{0,1:T(8,128)S(1)} %get-tuple-element.174) | copy-start | bytes 294916
  14.2 11.8 %copy-start.30 = (f32[1024,24]{0,1:T(8,128)}, f32[1024,24]{0,1:T(8,128)S(1)}, u32[]{:S(2)}) copy-start(f32[1024,24]{0,1:T(8,128)S(1)} %get-tuple-element.175) | copy-start | bytes 294916
  25.7 16.2 %copy-start.19 = (bf16[1024,384]{0,1:T(8,128)(2,1)}, bf16[1024,384]{0,1:T(8,128)(2,1)S(1)}, u32[]{:S(2)}) copy-start(bf16[1024,384]{0,1:T(8,128)(2,1)S(1)} %slice.258) | copy-start | bytes 2359300
  32.1 9.8 %copy-start.1 = (f32[8,512,1024]{2,1,0:T(8,128)}, f32[8,512,1024]{2,1,0:T(8,128)S(1)}, u32[]{:S(2)}) copy-start(f32[8,512,1024]{2,1,0:T(8,128)S(1)} %get-tuple-element.181) | copy-start | bytes 50331652
  32.1 9.8 %copy-start.42 = (f32[8,512]{1,0:T(8,128)}, f32[8,512]{1,0:T(8,128)S(1)}, u32[]{:S(2)}) copy-start(f32[8,512]{1,0:T(8,128)S(1)} %get-tuple-element.180) | copy-start | bytes 49156
  46.7 15.1 %copy-start.3 = (bf16[512,768]{1,0:T(8,128)(2,1)S(1)}, bf16[512,768]{1,0:T(8,128)(2,1)}, u32[]{:S(2)}) copy-start(bf16[512,768]{1,0:T(8,128)(2,1)} %param.28) | copy-start | bytes 2359300
  49.4 65.9 %all-gather.5.cloned.1.call-start = ((), (), s32[]{:S(2)}) async-start(), calls=%async_computation.12 | async-start | bytes 2359296 | tf_op jit(solution)/shard_map/all_gather | solution.py:189
  63.7 27.9 %copy-start.50 = (f32[512]{0:T(512)}, f32[512]{0:T(512)S(1)}, u32[]{:S(2)}) copy-start(f32[512]{0:T(512)S(1)} %fusion.94) | copy-start | bytes 6148
  74.2 14.0 %copy-start.28 = (f32[512,768]{1,0:T(8,128)}, f32[512,768]{1,0:T(8,128)S(1)}, u32[]{:S(2)}) copy-start(f32[512,768]{1,0:T(8,128)S(1)} %get-tuple-element.149) | copy-start | bytes 4718596
  74.3 14.0 %copy-start.57 = (f32[512]{0:T(512)}, f32[512]{0:T(512)S(1)}, u32[]{:S(2)}) copy-start(f32[512]{0:T(512)S(1)} %fusion.95) | copy-start | bytes 6148
  76.6 11.6 %copy-start.60 = (f32[512]{0:T(512)}, f32[512]{0:T(512)S(1)}, u32[]{:S(2)}) copy-start(f32[512]{0:T(512)S(1)} %multiply_multiply_fusion.4) | copy-start | bytes 6148
  94.1 178.4 %reduce-scatter.19.cloned.1.call-start = ((), (), s32[]{:S(2)}) async-start(), calls=%async_computation.15 | async-start | bytes 5898240 | tf_op jit(solution)/shard_map/reduce_scatter | solution.py:177
  100.1 176.2 %reduce-scatter.23.cloned.1.call-start = ((), (), s32[]{:S(2)}) async-start(), calls=%async_computation.17 | async-start | bytes 5898240 | tf_op jit(solution)/shard_map/reduce_scatter | solution.py:180
  106.2 174.0 %reduce-scatter.27.cloned.1.call-start = ((), (), s32[]{:S(2)}) async-start(), calls=%async_computation.19 | async-start | bytes 5898240 | tf_op jit(solution)/shard_map/reduce_scatter | solution.py:183
  114.0 216.2 %reduce-scatter.15.cloned.1.call-start = ((), (), s32[]{:S(2)}) async-start(), calls=%async_computation.13 | async-start | bytes 2359296 | tf_op jit(solution)/shard_map/reduce_scatter | solution.py:240
  170.9 16.9 %copy-start.10 = (bf16[1024,8,24]{0,2,1:T(8,128)(2,1)S(1)}, bf16[1024,8,24]{0,2,1:T(8,128)(2,1)}, u32[]{:S(2)}) copy-start(bf16[1024,8,24]{0,2,1:T(8,128)(2,1)} %copy-done.9) | copy-start | bytes 1179652
  170.9 16.9 %copy-start.12 = (bf16[1024,8,24]{0,2,1:T(8,128)(2,1)S(1)}, bf16[1024,8,24]{0,2,1:T(8,128)(2,1)}, u32[]{:S(2)}) copy-start(bf16[1024,8,24]{0,2,1:T(8,128)(2,1)} %copy-done.11) | copy-start | bytes 1179652
  239.3 13.4 %copy-start.33 = (bf16[1024,8,48]{0,2,1:T(8,128)(2,1)}, bf16[1024,8,48]{0,2,1:T(8,128)(2,1)S(1)}, u32[]{:S(2)}) copy-start(bf16[1024,8,48]{0,2,1:T(8,128)(2,1)S(1)} %add_convert_fusion.1) | copy-start | bytes 2359300
  256.9 152.0 %reduce-scatter.31.cloned.1.call-start = ((), (), s32[]{:S(2)}) async-start(), calls=%async_computation.21 | async-start | bytes 3760128
  267.8 270.4 %reduce-scatter.17.cloned.1.call-start = ((), (), s32[]{:S(2)}) async-start(), calls=%async_computation.14 | async-start | bytes 1253376 | tf_op jit(solution)/shard_map/reduce_scatter | solution.py:249
  272.4 406.9 %reduce-scatter.21.cloned.1.call-start = ((), (), s32[]{:S(2)}) async-start(), calls=%async_computation.16 | async-start | bytes 4177920 | tf_op jit(solution)/shard_map/reduce_scatter | solution.py:250
  276.2 544.6 %reduce-scatter.25.cloned.1.call-start = ((), (), s32[]{:S(2)}) async-start(), calls=%async_computation.18 | async-start | bytes 4177920 | tf_op jit(solution)/shard_map/reduce_scatter | solution.py:251
  280.1 50.1 %copy-start.49 = (f32[768]{0:T(1024)S(1)}, f32[768]{0:T(1024)}, u32[]{:S(2)}) copy-start(f32[768]{0:T(1024)} %param.37) | copy-start | bytes 9220
  280.1 50.1 %copy-start.51 = (f32[512]{0:T(512)S(1)}, f32[512]{0:T(512)}, u32[]{:S(2)}) copy-start(f32[512]{0:T(512)} %copy-done.50) | copy-start | bytes 6148
  280.1 50.1 %copy-start.53 = (f32[512]{0:T(512)S(1)}, f32[512]{0:T(512)}, u32[]{:S(2)}) copy-start(f32[512]{0:T(512)} %copy-done.52) | copy-start | bytes 6148
  280.1 681.7 %reduce-scatter.29.cloned.1.call-start = ((), (), s32[]{:S(2)}) async-start(), calls=%async_computation.20 | async-start | bytes 4177920 | tf_op jit(solution)/shard_map/reduce_scatter | solution.py:252
  (48 other events, 161.2 us)
Sparse Core Ops, SparseCore 0:
  9.5 12.5 all-gather.2
  49.5 12.3 reduce-scatter.12
  94.2 11.0 all-gather.4
  107.4 13.1 reduce-scatter.18
  122.7 13.2 reduce-scatter.22
  138.1 13.2 reduce-scatter.26
  257.0 10.3 reduce-scatter.14
  272.5 136.3 reduce-scatter.30
  414.3 123.9 reduce-scatter.16
  543.8 135.5 reduce-scatter.20
  685.1 135.7 reduce-scatter.24
  826.4 135.4 reduce-scatter.28
where the time goes:
time: 978 us; the launch traced here: 969 us
  waiting for transfers between devices  644 us (66%)
  matrix products  206 us (21%)
  blocking collectives  41 us (4%)
  other arithmetic  40.2 us (4%)
  local copies, waits for them, and re-layouts  20.7 us (2%)
  between operations  15.9 us (2%)
    reduce_scatter x1, waiting for transfers between devices, shards(): lax.psum_scatter(weight_up, 'dp', scatter_dimension=0, tiled=True)  141 us
    reduce_scatter x1, waiting for transfers between devices, shards(): lax.psum_scatter(weight_gate, 'dp', scatter_dimension=0, tiled=True)  141 us
    reduce_scatter x1, waiting for transfers between devices, shards(): lax.psum_scatter(weight_down_t, 'dp', scatter_dimension=0, tiled=True)  141 us
    reduce_scatter x1, waiting for transfers between devices, shards(): lax.psum_scatter(weight_out_t, 'dp', scatter_dimension=0, tiled=True)  128 us
    unnamed x13, waiting for transfers between devices  76.6 us
    dot_general x2, matrix products, shards(): jnp.einsum('hqk,khd->qhd', grad_scores, key_low[:key_end], preferred_elem...  54.7 us
    dot_general x2, matrix products, shards(): jnp.einsum('hqk,qhd->khd', grad_scores, query_low[query_from:key_end], pr...  47.7 us
    psum x1, blocking collectives, shards(): lax.psum((grad_gain_one, grad_gain_two), ('dp', 'seq'))  41 us
  transfers between devices with their start and end apart: 12, of which 7 were waited for; matrix products, arithmetic and copies ran while one was open for 21% of the time, Pallas kernels for 0%

commit v1 on v0

v1 whole, which is shorter than its diff:
```python
import functools
import math

import jax
import jax.numpy as jnp
import numpy as np
from jax import lax
from jax.experimental import pallas as pl
from jax.experimental.pallas import tpu as pltpu
from jax.sharding import PartitionSpec as P

HDIM = 48
HALF = HDIM // 2
SCORE = 1.0 / math.sqrt(HDIM)
LOG2E = 1.0 / math.log(2.0)
NEG = -1e30
BF16 = jnp.bfloat16
F32 = jnp.float32
CHUNK = 256
WIDE = 512
ROWS = 64
SPANS = 4
MIB = 1 << 20


def call(kernel, name, scalars, arrays, out_shape, flops, scratch=(), room=16, aliases=None):
    moved = sum(math.prod(o.shape) * o.dtype.itemsize for o in out_shape)
    return pl.pallas_call(
        kernel,
        in_specs=[pl.BlockSpec(memory_space=pltpu.SMEM)] * len(scalars)
        + [pl.BlockSpec(memory_space=pltpu.VMEM)] * len(arrays),
        out_specs=[pl.BlockSpec(memory_space=pltpu.VMEM)] * len(out_shape),
        out_shape=out_shape,
        scratch_shapes=list(scratch),
        input_output_aliases=aliases or {},
        cost_estimate=pl.CostEstimate(flops=flops, bytes_accessed=2 * moved, transcendentals=0),
        compiler_params=pltpu.CompilerParams(vmem_limit_bytes=room * MIB),
        name=name,
    )(*scalars, *arrays)


def shape(dtype, *dims):
    return jax.ShapeDtypeStruct(dims, dtype)


def at(start, size):
    return pl.ds(pl.multiple_of(start, size), size)


def dot(a, b, ca, cb):
    return lax.dot_general(a, b, (((ca,), (cb,)), ((), ())), preferred_element_type=F32)


def rope_tables(span):
    freq = 10000.0 ** (-np.arange(HALF, dtype=np.float64) / HALF)
    phase = freq[:, None] * np.arange(span, dtype=np.float64)[None, :]
    return np.cos(phase).astype(np.float32), np.sin(phase).astype(np.float32)


def block_facts(len_ref, block):
    ends = []
    total = 0
    for index in range(len_ref.shape[0]):
        total = total + len_ref[index]
        ends.append(total)
    segments, openings = [], []
    for number in range(SPANS):
        segment = 0
        opening = 0
        for index, end in enumerate(ends):
            done = number * block >= end
            segment = segment + done.astype(jnp.int32)
            opening = opening + jnp.where(done, len_ref[index], 0)
        segments.append(segment)
        openings.append(opening)
    return segments, openings


def causal(block):
    key = lax.broadcasted_iota(jnp.int32, (block, block), 0)
    return key <= lax.broadcasted_iota(jnp.int32, (block, block), 1)


def attention_forward_kernel(
    info_ref, len_ref, own_ref, oth_ref, wq_ref, wk_ref, wv_ref, cos_ref, sin_ref,
    x_ref, q_ref, k_ref, v_ref, ctx_ref, mine_ref, away_ref, lse_ref,
):
    rows = own_ref.shape[0]
    cols, pack = q_ref.shape
    heads = cols // HDIM
    block = pack // SPANS
    segments, openings = block_facts(len_ref, block)
    side = info_ref[0]
    x_ref[at(side * rows, rows), :] = own_ref[...]
    x_ref[at((1 - side) * rows, rows), :] = oth_ref[...]
    for w_ref, to_ref, scale in ((wq_ref, q_ref, SCORE * LOG2E), (wk_ref, k_ref, 1.0), (wv_ref, v_ref, None)):
        weight = w_ref[:, at(side * cols, cols)].T
        for number in range(SPANS):
            lanes = slice(number * block, (number + 1) * block)
            part = dot(weight, x_ref[lanes, :], 1, 1)
            if scale is None:
                to_ref[:, lanes] = part.astype(BF16)
                continue
            here = at(number * block - openings[number], block)
            cos = cos_ref[:, here] * scale
            sin = sin_ref[:, here] * scale
            for head in range(heads):
                a = part[head * HDIM : head * HDIM + HALF]
                b = part[head * HDIM + HALF : (head + 1) * HDIM]
                turned = jnp.concatenate([a * cos - b * sin, b * cos + a * sin], axis=0)
                to_ref[head * HDIM : (head + 1) * HDIM, lanes] = turned.astype(BF16)
    below = causal(block)

    @pl.loop(0, heads)
    def _(head):
        here = at(head * HDIM, HDIM)
        keys = k_ref[here, :].T
        value = v_ref[here, :]
        for i in range(SPANS):
            lanes = slice(i * block, (i + 1) * block)
            query = q_ref[here, lanes]
            scores, biases, tops = [], [], []
            for j in range(i + 1):
                score = dot(keys[j * block : (j + 1) * block], query, 1, 0)
                bias = 0.0
                if j == i:
                    score = jnp.where(below, score, NEG)
                else:
                    bias = jnp.where(segments[i] == segments[j], 0.0, NEG)
                scores.append(score)
                biases.append(bias)
                tops.append(jnp.max(score, axis=0, keepdims=True) + bias)
            top = functools.reduce(jnp.maximum, tops)
            total = jnp.zeros((1, block), F32)
            context = jnp.zeros((HDIM, block), F32)
            for j in range(i + 1):
                prob = jnp.exp2(scores[j] - (top - biases[j]))
                total = total + jnp.sum(prob, axis=0, keepdims=True)
                context = context + dot(value[:, j * block : (j + 1) * block], prob.astype(BF16), 1, 0)
            ctx_ref[here, lanes] = (context * (1.0 / total)).astype(BF16)
            lse_ref[head, :, lanes] = top + jnp.log2(total)
        mine_ref[here, :] = ctx_ref[here, at(side * rows, rows)]
        away_ref[here, :] = ctx_ref[here, at((1 - side) * rows, rows)]


def attention_forward(info, lengths, own, oth, weights):
    rows, width = own.shape
    pack = 2 * rows
    cols = weights[0].shape[1] // 2
    heads = cols // HDIM
    half = shape(BF16, cols, rows)
    return call(
        attention_forward_kernel, "attention_forward", (info, lengths),
        (own, oth, *weights, *rope_tables(pack)),
        [shape(BF16, pack, width)] + [shape(BF16, cols, pack)] * 4 + [half, half, shape(F32, heads, 1, pack)],
        15_000_000_000,
    )


def attention_backward_kernel(
    info_ref, len_ref, q_ref, k_ref, v_ref, ctx_ref, own_ref, oth_ref, lse_ref, cos_ref, sin_ref, *rest,
    first, heads,
):
    dq_ref, dk_ref, dv_ref, dctx_ref, dk_acc, dv_acc = rest[-6:]
    rows = own_ref.shape[1]
    pack = q_ref.shape[1]
    block = pack // SPANS
    segments, openings = block_facts(len_ref, block)
    side = info_ref[0]
    below = causal(block)

    def unturn(value, number, scale):
        here = at(number * block - openings[number], block)
        cos = cos_ref[:, here] * scale
        sin = sin_ref[:, here] * scale
        a, b = value[:HALF], value[HALF:]
        return jnp.concatenate([a * cos + b * sin, b * cos - a * sin], axis=0).astype(BF16)

    @pl.loop(first, first + heads)
    def _(head):
        here = at(head * HDIM, HDIM)
        dctx_ref[:, at(side * rows, rows)] = own_ref[here, :]
        dctx_ref[:, at((1 - side) * rows, rows)] = oth_ref[here, :]
        key = k_ref[here, :]
        keys = key.T
        values = v_ref[here, :].T
        for i in range(SPANS):
            lanes = slice(i * block, (i + 1) * block)
            query = q_ref[here, lanes]
            grad = dctx_ref[:, lanes]
            delta = jnp.sum(grad.astype(F32) * ctx_ref[here, lanes].astype(F32), axis=0, keepdims=True)
            lse = lse_ref[head, :, lanes]
            dq = jnp.zeros((HDIM, block), F32)
            for j in range(i + 1):
                span = slice(j * block, (j + 1) * block)
                score = dot(keys[span], query, 1, 0)
                if j == i:
                    prob = jnp.exp2(jnp.where(below, score, NEG) - lse)
                else:
                    prob = jnp.exp2(score - (lse - jnp.where(segments[i] == segments[j], 0.0, NEG)))
                slope = dot(values[span], grad, 1, 0)
                dscore = (prob * (slope - delta)).astype(BF16)
                dq = dq + dot(key[:, span], dscore, 1, 0)
                dk = dot(query, dscore, 1, 1)
                dv = dot(grad, prob.astype(BF16), 1, 1)
                if j == i:
                    dk_acc[:, span] = dk
                    dv_acc[:, span] = dv
                else:
                    dk_acc[:, span] += dk
                    dv_acc[:, span] += dv
            dq_ref[here, lanes] = unturn(dq, i, SCORE)
        for number in range(SPANS):
            lanes = slice(number * block, (number + 1) * block)
            dk_ref[here, lanes] = unturn(dk_acc[:, lanes], number, 1.0 / LOG2E)
            dv_ref[here, lanes] = dv_acc[:, lanes].astype(BF16)


def attention_backward(info, lengths, kept, own, oth, first, heads, sofar):
    query, key, value, context, lse = kept
    cols, pack = query.shape
    arrays = (query, key, value, context, own, oth, lse, *rope_tables(pack), *sofar)
    base = 2 + len(arrays) - len(sofar)
    return call(
        functools.partial(attention_backward_kernel, first=first, heads=heads),
        "attention_backward", (info, lengths), arrays, [shape(BF16, cols, pack)] * 3,
        heads * 3_000_000_000,
        [pltpu.VMEM((HDIM, pack), BF16)] + [pltpu.VMEM((HDIM, pack), F32)] * 2,
        aliases={base + index: index for index in range(len(sofar))},
    )


def inverse_rms(value):
    return lax.rsqrt(jnp.mean(value * value, axis=-1, keepdims=True) + 1e-06)


def norm_back(value, gain, grad):
    inv = inverse_rms(value)
    scaled = grad * gain
    slope = jnp.mean(scaled * value, axis=-1, keepdims=True) * (inv * inv * inv)
    return scaled * inv - value * slope, grad * value * inv


def relative_rows(to_ref, from_ref, place, blocks):
    size = from_ref.shape[0] // blocks
    for block in range(blocks):
        to_ref[block * size : (block + 1) * size, :] = from_ref[at((block ^ place) * size, size), :]


def position(block, order):
    last = len(order) - 1
    return sum(((block >> bit) & 1) << (last - step) for step, bit in enumerate(order))


def ffn_forward_kernel(
    info_ref, len_ref, x_ref, mine_ref, came_ref, wo_ref, g1_ref, g2_ref, wg_ref, wu_ref, wd_ref, cot_ref,
    act_ref, s_ref, t_ref, out_ref, dm_ref, dmt_ref, hbt_ref, dr2_ref, r1_ref, small_ref,
    hb_ref, h_ref, m_ref, turn_ref, *, blocks,
):
    rows, width = x_ref.shape
    part = mine_ref.shape[0]
    total = len_ref[0] + len_ref[1] + len_ref[2] + len_ref[3]
    side = info_ref[0]
    first = side * rows

    def valid_of(start):
        places = lax.broadcasted_iota(jnp.int32, (ROWS, 1), 0) + (start + first)
        return (places < total).astype(F32)

    def squares(row, value, valid):
        small_ref[row : row + 1, :] += jnp.sum(value * value * valid, axis=0, keepdims=True)

    small_ref[...] = jnp.zeros_like(small_ref)
    m_ref[...] = dot(mine_ref[...].T, wo_ref[at(side * part, part), :], 1, 0) + dot(
        came_ref[...].T, wo_ref[at((1 - side) * part, part), :], 1, 0
    )

    @pl.loop(0, rows // ROWS)
    def _(index):
        here = at(index * ROWS, ROWS)
        valid = valid_of(index * ROWS)
        x = x_ref[here, :].astype(F32)
        a = m_ref[here, :]
        r1 = x + a
        h = r1 * inverse_rms(r1) * g1_ref[...]
        r1_ref[here, :] = r1
        h_ref[here, :] = h
        hb_ref[here, :] = h.astype(BF16)
        squares(2, x, valid)
        squares(3, a, valid)

    turn_ref[...] = hb_ref[...].T
    relative_rows(hbt_ref, turn_ref, info_ref[1], blocks)
    m_ref[...] = jnp.zeros_like(m_ref)

    @pl.loop(0, act_ref.shape[1] // WIDE)
    def _(step):
        cols = at(step * WIDE, WIDE)
        gate = dot(hb_ref[...], wg_ref[:, cols], 1, 0)
        up = dot(hb_ref[...], wu_ref[:, cols], 1, 0)
        sig = 1.0 / (1.0 + jnp.exp(-gate))
        silu = gate * sig
        act = (silu * up).astype(BF16)
        act_ref[:, cols] = act
        s_ref[:, cols] = silu.astype(BF16)
        t_ref[:, cols] = (up * (sig + silu * (1.0 - sig))).astype(BF16)
        m_ref[...] += dot(act, wd_ref[cols, :], 1, 0)

    @pl.loop(0, rows // ROWS)
    def _(index):
        here = at(index * ROWS, ROWS)
        valid = valid_of(index * ROWS)
        m = m_ref[here, :]
        r2 = h_ref[here, :] + m
        gain = g2_ref[...]
        dr2, dgain = norm_back(r2, gain, cot_ref[here, :].astype(F32) * valid)
        out_ref[here, :] = (r2 * inverse_rms(r2) * gain).astype(BF16)
        dr2_ref[here, :] = dr2
        dm_ref[here, :] = dr2.astype(BF16)
        small_ref[1:2, :] += jnp.sum(dgain, axis=0, keepdims=True)
        squares(4, m, valid)

    small_ref[5:6, :] = jnp.full((1, width), jnp.clip(total - first, 0, rows).astype(F32))
    turn_ref[...] = dm_ref[...].T
    relative_rows(dmt_ref, turn_ref, info_ref[1], blocks)


def ffn_forward(info, lengths, x, mine, came, w_out, g1, g2, wg, wu, wd, cot, blocks):
    rows, width = x.shape
    ff = wg.shape[1]
    return call(
        functools.partial(ffn_forward_kernel, blocks=blocks), "ffn_forward", (info, lengths),
        (x, mine, came, w_out, g1, g2, wg, wu, wd, cot),
        [shape(BF16, rows, ff)] * 3 + [shape(BF16, rows, width)] * 2 + [shape(BF16, width, rows)] * 2
        + [shape(F32, rows, width)] * 2 + [shape(F32, 8, width)],
        6 * rows * width * ff,
        [
            pltpu.VMEM((rows, width), BF16), pltpu.VMEM((rows, width), F32),
            pltpu.VMEM((rows, width), F32), pltpu.VMEM((width, rows), BF16),
        ],
    )


def split_store(product, came, to_refs, order, blocks):
    size = product.shape[0] // blocks
    for block in range(blocks):
        place = position(block, order)
        rows = product[block * size : (block + 1) * size]
        if came is not None:
            rows = rows + came[place * size : (place + 1) * size].astype(F32)
        half = blocks // len(to_refs)
        start = (place % half) * size
        to_refs[place // half][start : start + size, :] = rows.astype(BF16)


def weight_kernel(info_ref, left_ref, right_ref, *rest, order, blocks):
    side = info_ref[0]
    mine = len(rest) == 3
    to_refs = rest[-2:] if mine else rest
    cols = to_refs[0].shape[1]
    start = (side if mine else 1 - side) * cols

    @pl.loop(0, cols // CHUNK)
    def _(step):
        here = at(step * CHUNK, CHUNK)
        right = right_ref[:, at(start + step * CHUNK, CHUNK)]
        came = rest[0][:, here] if mine else None
        split_store(dot(left_ref[...], right, 1, 0), came, [ref.at[:, here] for ref in to_refs], order, blocks)


def weight_grad(info, left, right, order, blocks, came=None):
    width, rows = left.shape
    cols = right.shape[1] // 2
    kernel = functools.partial(weight_kernel, order=order, blocks=blocks)
    flops = 2 * width * rows * cols
    if came is None:
        return call(kernel, "weight_away", (info,), (left, right), [shape(BF16, width, cols)], flops)[0]
    return call(
        kernel, "weight_mine", (info,), (left, right, came), [shape(BF16, width // 2, cols)] * 2, flops
    )


def swiglu_back_kernel(
    info_ref, dm_ref, wd_ref, s_ref, t_ref, hbt_ref, dgt_ref, dup_ref, gate_ref, up_ref, *, orders, blocks
):
    half = gate_ref.shape[1]

    def grads(start):
        cols = at(start, CHUNK)
        grad = dot(dm_ref[...], wd_ref[cols, :], 1, 1)
        dup = (grad * s_ref[:, cols].astype(F32)).astype(BF16)
        dgt = (grad * t_ref[:, cols].astype(F32)).astype(BF16)
        dup_ref[:, cols] = dup
        dgt_ref[:, cols] = dgt
        return dgt, dup

    @pl.loop(0, half // CHUNK)
    def _(step):
        here = at(step * CHUNK, CHUNK)
        dgt, dup = grads((1 - info_ref[0]) * half + step * CHUNK)
        split_store(dot(hbt_ref[...], dgt, 1, 0), None, [gate_ref.at[:, here]], orders[0], blocks)
        split_store(dot(hbt_ref[...], dup, 1, 0), None, [up_ref.at[:, here]], orders[1], blocks)

    @pl.loop(0, half // CHUNK)
    def _(step):
        grads(info_ref[0] * half + step * CHUNK)


def swiglu_back(info, dm, wd, s, t, hbt, orders, blocks):
    rows, width = dm.shape
    ff = wd.shape[0]
    return call(
        functools.partial(swiglu_back_kernel, orders=orders, blocks=blocks), "swiglu_back", (info,),
        (dm, wd, s, t, hbt),
        [shape(BF16, rows, ff)] * 2 + [shape(BF16, width, ff // 2)] * 2,
        4 * rows * width * ff,
    )


def norm_one_kernel(
    info_ref, dgt_ref, dup_ref, wg_ref, wu_ref, r1_ref, dr2_ref, g1_ref, wo_ref, part_ref,
    dr1_ref, dat_ref, own_ref, away_ref, small_ref, acc_ref, da_ref, turn_ref, *, blocks,
):
    rows = r1_ref.shape[0]
    cols = own_ref.shape[0]
    side = info_ref[0]
    acc_ref[...] = dr2_ref[...]

    @pl.loop(0, wg_ref.shape[1] // WIDE)
    def _(step):
        here = at(step * WIDE, WIDE)
        acc_ref[...] += dot(dgt_ref[:, here], wg_ref[:, here], 1, 1) + dot(dup_ref[:, here], wu_ref[:, here], 1, 1)

    small_ref[...] = part_ref[...]

    @pl.loop(0, rows // ROWS)
    def _(index):
        here = at(index * ROWS, ROWS)
        dr1, dgain = norm_back(r1_ref[here, :], g1_ref[...], acc_ref[here, :])
        dr1_ref[here, :] = dr1
        da_ref[here, :] = dr1.astype(BF16)
        small_ref[0:1, :] += jnp.sum(dgain, axis=0, keepdims=True)

    away_ref[...] = dot(wo_ref[at((1 - side) * cols, cols), :], da_ref[...], 1, 1).astype(BF16)
    own_ref[...] = dot(wo_ref[at(side * cols, cols), :], da_ref[...], 1, 1).astype(BF16)
    turn_ref[...] = da_ref[...].T
    relative_rows(dat_ref, turn_ref, info_ref[1], blocks)


def norm_one(info, dgt, dup, wg, wu, r1, dr2, g1, w_out, part, blocks):
    rows, width = r1.shape
    ff = wg.shape[1]
    cols = w_out.shape[0] // 2
    return call(
        functools.partial(norm_one_kernel, blocks=blocks), "norm_one_back", (info,),
        (dgt, dup, wg, wu, r1, dr2, g1, w_out, part),
        [
            shape(F32, rows, width), shape(BF16, width, rows), shape(BF16, cols, rows),
            shape(BF16, cols, rows), shape(F32, 8, width),
        ],
        4 * rows * width * ff,
        [pltpu.VMEM((rows, width), F32), pltpu.VMEM((rows, width), BF16), pltpu.VMEM((width, rows), BF16)],
    )


def out_grad_kernel(dat_ref, mine_ref, came_ref, keep_ref, away_ref):
    away_ref[...] = dot(dat_ref[...], came_ref[...], 1, 1).astype(BF16)
    keep_ref[...] = dot(dat_ref[...], mine_ref[...], 1, 1).astype(BF16)


def out_grad(dat, mine, came):
    width, rows = dat.shape
    cols = mine.shape[0]
    return call(
        out_grad_kernel, "out_grad", (), (dat, mine, came), [shape(BF16, width, cols)] * 2,
        4 * width * rows * cols,
    )


def project_grad_kernel(info_ref, x_ref, dq_ref, dk_ref, dv_ref, mine_ref, came_ref, *rest, orders, blocks):
    out_refs, (turn_ref, left_ref) = rest[:-2], rest[-2:]
    turn_ref[...] = x_ref[...].T
    relative_rows(left_ref, turn_ref, info_ref[1], blocks)
    left = left_ref[...]
    cols = dq_ref.shape[0]
    piece = cols // 3
    for index, grad_ref in enumerate((dq_ref, dk_ref, dv_ref)):
        lanes = slice(index * piece, (index + 1) * piece)
        pair = out_refs[2 * index : 2 * index + 2]
        main = [ref.at[:, 0:cols] for ref in pair]
        tail = [ref.at[:, cols : cols + piece] for ref in pair]
        split_store(dot(left, grad_ref[...], 1, 1), None, main, orders[index], blocks)
        both = mine_ref[:, lanes].astype(F32) + came_ref[:, lanes].astype(F32)
        split_store(both, None, tail, orders[index], blocks)


def project_grad(info, x, grads, mine, came, orders, blocks):
    rows, width = x.shape
    cols = grads[0].shape[0]
    wide = cols + cols // 3
    return call(
        functools.partial(project_grad_kernel, orders=orders, blocks=blocks), "project_grad", (info,),
        (x, *grads, mine, came), [shape(BF16, width // 2, wide)] * 6, 6 * rows * width * cols,
        [pltpu.VMEM((width, rows), BF16)] * 2,
    )


def stream_grad_kernel(info_ref, dq_ref, dk_ref, dv_ref, wq_ref, wk_ref, wv_ref, *rest):
    cols, pack = dq_ref.shape
    rows = pack // 2
    side = info_ref[0]
    mine = len(rest) == 3
    lanes = at((side if mine else 1 - side) * rows, rows)
    total = sum(
        dot(w_ref[:, at(side * cols, cols)], g_ref[:, lanes], 1, 0)
        for w_ref, g_ref in ((wq_ref, dq_ref), (wk_ref, dk_ref), (wv_ref, dv_ref))
    )
    if mine:
        came_ref, dr1_ref, out_ref = rest
        total = total + came_ref[...].astype(F32)
        out_ref[...] = (dr1_ref[...] + total.T).astype(BF16)
    else:
        rest[0][...] = total.astype(BF16)


def stream_grad(info, grads, weights, *others):
    cols, pack = grads[0].shape
    width = weights[0].shape[0]
    rows = pack // 2
    out = (rows, width) if others else (width, rows)
    return call(
        stream_grad_kernel, "stream_grad", (info,), (*grads, *weights, *others), [shape(BF16, *out)],
        6 * rows * width * cols,
    )[0]


def stage_order(bits, turn):
    last = bits - 1
    return [(turn + step) % last for step in range(last)] + [last]


def swap_seq(value):
    return lax.ppermute(value, "seq", [(0, 1), (1, 0)])


def swap_dp(value, bit):
    size = lax.axis_size("dp")
    return lax.ppermute(value, "dp", [(i, i ^ (1 << bit)) for i in range(size)])


def sum_everywhere(value):
    value = value + swap_seq(value)
    for bit in range(lax.axis_size("dp").bit_length() - 1):
        value = value + swap_dp(value, bit)
    return value


class Halving:
    def __init__(self, keep, away, order, shift):
        self.keep, self.order, self.shift = keep, order, shift
        self.sent, self.step = away, 0

    def send(self):
        self.came = swap_dp(self.sent, self.order[self.step] + self.shift)
        self.step += 1

    def receive(self):
        rows = self.keep.shape[0] // 2
        if self.step < len(self.order):
            self.sent = self.add(rows, 2 * rows)
            self.keep = self.add(0, rows)
        else:
            self.keep = self.keep.astype(F32) + self.came.astype(F32)

    def add(self, low, high):
        return (self.keep[low:high].astype(F32) + self.came[low:high].astype(F32)).astype(BF16)

    def rest(self):
        value = self.keep
        for bit in reversed(range(self.shift)):
            half = value.shape[0] // 2
            mine = (lax.axis_index("dp") >> bit) & 1
            keep = lax.dynamic_slice_in_dim(value, mine * half, half, 0)
            away = lax.dynamic_slice_in_dim(value, (1 - mine) * half, half, 0)
            value = keep + swap_dp(away.astype(BF16), bit).astype(F32)
        return value


def after(values, *others):
    return lax.optimization_barrier((values, others))[0]


def shards(
    tokens,
    doc_lengths,
    w_query,
    w_key,
    w_value,
    w_out,
    w_gate,
    w_up,
    w_down,
    gain_attn,
    gain_ffn,
    cotangent,
):
    row_count, width = tokens.shape
    head_cols = w_query.shape[1] // lax.axis_size("seq")
    dp_size = lax.axis_size("dp")
    blocks = min(dp_size, 16)
    bits = blocks.bit_length() - 1
    shift = (dp_size // blocks).bit_length() - 1
    orders = [stage_order(bits, turn) for turn in range(3)]
    lengths = doc_lengths[0]
    seq_index = lax.axis_index("seq")
    info = jnp.stack([seq_index, lax.axis_index("dp") >> shift]).astype(jnp.int32)
    gain_one, gain_two = gain_attn.reshape(1, width), gain_ffn.reshape(1, width)

    weights = (w_query, w_key, w_value)
    gathered, query, key, value, context, mine, away, lse = attention_forward(
        info, lengths, tokens, swap_seq(tokens), weights
    )
    kept = (query, key, value, context, lse)
    came = swap_seq(away)
    act, silu, slope, result, dm, dm_turned, hb_turned, dr2, r1, small = ffn_forward(
        info, lengths, tokens, mine, came, w_out, gain_one, gain_two, w_gate, w_up, w_down, cotangent, blocks
    )
    down_came = swap_seq(weight_grad(info, dm_turned, act, orders[2], blocks))
    dgt, dup, gate_away, up_away = swiglu_back(
        info, dm, w_down, silu, slope, hb_turned, orders[:2], blocks
    )
    gate_came, up_came = swap_seq(gate_away), swap_seq(up_away)
    down = Halving(*weight_grad(info, dm_turned, after(act, gate_away), orders[2], blocks, down_came), orders[2], shift)
    down.send()
    gate = Halving(*weight_grad(info, after(hb_turned, down.sent), dgt, orders[0], blocks, gate_came), orders[0], shift)
    gate.send()
    up = Halving(*weight_grad(info, after(hb_turned, gate.sent), dup, orders[1], blocks, up_came), orders[1], shift)
    up.send()
    dr1, da_turned, own_rows, away_rows, small = norm_one(
        info, after(dgt, up.sent), dup, w_gate, w_up, r1, dr2, gain_one, w_out, small, blocks
    )
    came_rows = swap_seq(away_rows)
    out_keep, out_away = out_grad(da_turned, mine, came)
    out_came = swap_seq(out_away)
    small = sum_everywhere(small)
    steps = 4
    each = head_cols // HDIM // steps
    grads = ()
    ffn = [down, gate, up]
    for step in range(steps):
        if step >= 2:
            for part in ffn:
                part.receive()
                part.send()
            own_rows = after(own_rows, *[part.sent for part in ffn])
        grads = attention_backward(
            info, lengths, kept, own_rows, came_rows, step * each, each, grads
        )
    sides = project_grad(info, gathered, grads, out_keep, out_came, orders, blocks)
    attn = [
        Halving(sides[2 * index], sides[2 * index + 1], orders[index], shift) for index in range(3)
    ]
    for part in attn:
        part.send()
    stream_away = stream_grad(info, after(grads, *sides), weights)
    grad_tokens = stream_grad(info, grads, weights, swap_seq(stream_away), dr1)
    while ffn[0].step < bits:
        for part in ffn:
            part.receive()
            part.send()
    for part in ffn:
        part.receive()
    while attn[0].step < bits:
        for part in attn:
            part.receive()
            part.send()
    for part in attn:
        part.receive()
    summed_down, summed_gate, summed_up = (part.rest() for part in ffn)
    sums = [part.rest() for part in attn]
    summed_out = jnp.concatenate([total[:, head_cols:] for total in sums], axis=1)
    squares = jnp.sum(small[2:5], axis=1)
    rms_values = jnp.sqrt(squares / (small[5, 0] * width))
    return (
        result,
        grad_tokens,
        sums[0][:, :head_cols],
        sums[1][:, :head_cols],
        sums[2][:, :head_cols],
        summed_out.T,
        summed_gate,
        summed_up,
        summed_down.T,
        small[0],
        small[1],
        rms_values,
    )


def solution(mesh):
    return jax.shard_map(
        shards,
        mesh=mesh,
        in_specs=(
            P(("dp", "seq"), None),
            P("dp", None),
            P(),
            P(),
            P(),
            P(),
            P(),
            P(),
            P(),
            P(),
            P(),
            P(("dp", "seq"), None),
        ),
        out_specs=(
            P(("dp", "seq"), None),
            P(("dp", "seq"), None),
            P("dp", "seq"),
            P("dp", "seq"),
            P("dp", "seq"),
            P("seq", "dp"),
            P("dp", "seq"),
            P("dp", "seq"),
            P("seq", "dp"),
            P(),
            P(),
            P(),
        ),
        check_vma=False,
    )
```

time: 978 us -> 208 us (0.21)
  waiting for transfers between devices: 644 us -> 58.6 us
  matrix products: 206 us -> 0 us
  Pallas kernels: 0 us -> 90.4 us
  blocking collectives: 41 us -> 0 us
  starting transfers between devices: 0.49 us -> 38.1 us
  other arithmetic: 40.2 us -> 5.36 us
  between operations: 15.9 us -> 1.85 us
    reduce_scatter x9 -> x0, waiting for transfers between devices: 562 us -> none  [the longest x1 141 us: shards(): lax.psum_scatter(weight_up, 'dp', scatter_dimension=0, tiled=True)]
    dot_general x27 -> x0, matrix products: 206 us -> none  [the longest x2 54.7 us: shards(): jnp.einsum('hqk,khd->qhd', grad_scores, key_low[:key_end], preferred_elem...]
    pallas_call x0 -> x16, Pallas kernels: none -> 90.4 us  [call(): pl.pallas_call(kernel, in_specs=[pl.BlockSpec(memory_space=pltpu.SMEM)] *...]
    unnamed x13 -> x0, waiting for transfers between devices: 76.6 us -> none
    ppermute x0 -> x37, waiting for transfers between devices: none -> 58.6 us  [the longest x28 52.7 us: swap_dp(): return lax.ppermute(value, 'dp', [(i, i ^ 1 << bit) for i in range(size)])]
    psum x1 -> x0, blocking collectives: 41 us -> none  [shards(): lax.psum((grad_gain_one, grad_gain_two), ('dp', 'seq'))]
    ppermute x0 -> x37, starting transfers between devices: none -> 38.1 us  [the longest x28 35.9 us: swap_dp(): return lax.ppermute(value, 'dp', [(i, i ^ 1 << bit) for i in range(size)])]
    convert_element_type x8 -> x18, other arithmetic: 16.9 us -> 1.7 us  [add(): (self.keep[low:high].astype(F32) + self.came[low:high].astype(F32)).astyp...]
  transfers between devices with their start and end apart: 12 -> 37, of which waited for: 7 -> 20; matrix products, arithmetic and copies ran while one was open for 21% -> 4% of each run, Pallas kernels for 0% -> 22%
where the time goes in v1:
time: 208 us; the launch traced here: 207 us
  Pallas kernels  90.4 us (43%)
  waiting for transfers between devices  58.6 us (28%)
  starting transfers between devices  38.1 us (18%)
  local copies, waits for them, and re-layouts  13.2 us (6%)
  other arithmetic  5.36 us (3%)
    pallas_call x16, Pallas kernels, call(): pl.pallas_call(kernel, in_specs=[pl.BlockSpec(memory_space=pltpu.SMEM)] *...  90.4 us
    ppermute x28, waiting for transfers between devices, swap_dp(): return lax.ppermute(value, 'dp', [(i, i ^ 1 << bit) for i in range(size)])  52.7 us
    ppermute x28, starting transfers between devices, swap_dp(): return lax.ppermute(value, 'dp', [(i, i ^ 1 << bit) for i in range(size)])  35.9 us
    unnamed x60, local copies, waits for them, and re-layouts  10.1 us
    ppermute x9, waiting for transfers between devices, swap_seq(): return lax.ppermute(value, 'seq', [(0, 1), (1, 0)])  5.85 us
  transfers between devices with their start and end apart: 37, of which 20 were waited for; matrix products, arithmetic and copies ran while one was open for 4% of the time, Pallas kernels for 22%

profile of v1, /device:TPU:0, one launch (start us, length us, event | category | flops | bytes accessed | tf_op | source)
XLA Modules:
  0.0 207.5 jit_solution(18187807430348027594)
XLA Ops:
  1.3 2.0 collective-permute-done.oth_ref
  10.8 15.8 %attention_forward.1 = (bf16[1024,768]{1,0:T(8,128)(2,1)S(1)}, bf16[384,1024]{1,0:T(8,128)(2,1)S(1)}, bf16[384,1024]{1,0:T(8,128)(2,1)S(1)}, bf16[384,1024]{1,0:...) custom-call(s32[2]{0:T(128)S(1)} %pad_add_fusion.info_ref, ...), custom_call_target="tpu_custom_call" | custom-call | flops 15000000512 | bytes 11075584 | tf_op jit(solution)/shard_map/attention_forward/pallas_call | solution.py:28
  29.3 13.6 %ffn_forward.1 = (bf16[512,2560]{1,0:T(8,128)(2,1)S(1)}, bf16[512,2560]{1,0:T(8,128)(2,1)S(1)}, bf16[512,2560]{1,0:T(8,128)(2,1)S(1)}, bf16[512,768]{1,0:T(8,128...) custom-call(s32[2]{0:T(128)S(1)} %pad_add_fusion.info_ref, ...), custom_call_target="tpu_custom_call" | custom-call | flops 6039797760 | bytes 28360704 | tf_op jit(solution)/shard_map/ffn_forward/pallas_call | solution.py:28
  42.9 2.4 %weight_away.1 = bf16[768,1280]{1,0:T(8,128)(2,1)S(1)} custom-call(s32[2]{0:T(128)S(1)} %pad_add_fusion.info_ref, bf16[768,512]{1,0:T(8,128)(2,1)S(1)} %get-tuple-element.86.left_ref, bf16[512,2560]{1,0:T(8,128)(2,1)S(1)} %get-tuple-element.89.right_ref), custom_call_target="tpu_custom_call" | custom-call | flops 1006632960 | bytes 3932160 | tf_op jit(solution)/shard_map/weight_away/pallas_call | solution.py:28
  47.6 8.9 %swiglu_back.1 = (bf16[512,2560]{1,0:T(8,128)(2,1)S(1)}, bf16[512,2560]{1,0:T(8,128)(2,1)S(1)}, bf16[768,1280]{1,0:T(8,128)(2,1)S(1)}, bf16[768,1280]{1,0:T(8,128)(2,1)S(1)}) custom-call(s32[2]{0:T(128)S(1)} %pad_add_fusion.info_ref, bf16[512,768]{1,0:T(8,128)(2,1)S(1)} %get-tuple-element.81.dm_ref, bf16[2560,768]{1,0:T(8,128)(2,1)S(1)} %copy-done.9, ...), custom_call_target="tpu_custom_call" | custom-call | flops 4026531840 | bytes 18350080 | tf_op jit(solution)/shard_map/swiglu_back/pallas_call | solution.py:28
  57.1 2.4 %weight_mine.3 = (bf16[384,1280]{1,0:T(8,128)(2,1)S(1)}, bf16[384,1280]{1,0:T(8,128)(2,1)S(1)}) custom-call(s32[2]{0:T(128)S(1)} %pad_add_fusion.info_ref, bf16[768,512]{1,0:T(8,128)(2,1)S(1)} %get-tuple-element.86.left_ref, bf16[512,2560]{1,0:T(8,128)(2,1)S(1)} %get-tuple-element.89.right_ref, bf16[768,1280]{1,0:T(8,128)(2,1)S(1)} %collective-permute-done.2.rest_0_), custom_call_target="tpu_custom_call" | custom-call | flops 1006632960 | bytes 3932160 | tf_op jit(solution)/shard_map/weight_mine/pallas_call | solution.py:28
  60.5 2.4 %weight_mine.4 = (bf16[384,1280]{1,0:T(8,128)(2,1)S(1)}, bf16[384,1280]{1,0:T(8,128)(2,1)S(1)}) custom-call(s32[2]{0:T(128)S(1)} %pad_add_fusion.info_ref, bf16[768,512]{1,0:T(8,128)(2,1)S(1)} %get-tuple-element.93.hbt_ref.left_ref, bf16[512,2560]{1,0:T(8,128)(2,1)S(1)} %get-tuple-element.97.right_ref.dgt_ref, ...), custom_call_target="tpu_custom_call" | custom-call | flops 1006632960 | bytes 3932160 | tf_op jit(solution)/shard_map/weight_mine/pallas_call | solution.py:28
  63.4 2.4 %weight_mine.5 = (bf16[384,1280]{1,0:T(8,128)(2,1)S(1)}, bf16[384,1280]{1,0:T(8,128)(2,1)S(1)}) custom-call(s32[2]{0:T(128)S(1)} %pad_add_fusion.info_ref, bf16[768,512]{1,0:T(8,128)(2,1)S(1)} %get-tuple-element.93.hbt_ref.left_ref, bf16[512,2560]{1,0:T(8,128)(2,1)S(1)} %get-tuple-element.94.right_ref.dup_ref, ...), custom_call_target="tpu_custom_call" | custom-call | flops 1006632960 | bytes 3932160 | tf_op jit(solution)/shard_map/weight_mine/pallas_call | solution.py:28
  65.8 7.7 %norm_one_back.1 = (f32[512,768]{1,0:T(8,128)S(1)}, bf16[768,512]{1,0:T(8,128)(2,1)S(1)}, bf16[384,512]{1,0:T(8,128)(2,1)S(1)}, bf16[384,512]{1,0:T(8,128)(2,1)S(1)}, f32[8,768]{1,0:T(8,128)S(1)}) custom-call(s32[2]{0:T(128)S(1)} %pad_add_fusion.info_ref, bf16[512,2560]{1,0:T(8,128)(2,1)S(1)} %get-tuple-element.97.right_ref.dgt_ref, ...), custom_call_target="tpu_custom_call" | custom-call | flops 4026531840 | bytes 6340608 | tf_op jit(solution)/shard_map/norm_one_back/pallas_call | solution.py:28
  74.8 2.6 %collective-permute-start.33 = (f32[8,768]{1,0:T(8,128)S(1)}, f32[8,768]{1,0:T(8,128)S(1)}, u32[]{:S(2)}, u32[]{:S(2)}) collective-permute-start(f32[8,768]{1,0:T(8,128)S(1)} %add.183), channel_id=1, source_target_pairs={{0,2},{2,0},{4,6},{6,4},{8,10},{10,8},{12,14},{14,12},{16,18},{18,... | collective-permute-start | bytes 73736 | tf_op jit(solution)/shard_map/ppermute | solution.py:548
  79.2 2.0 collective-permute-start.34
  83.1 2.1 %collective-permute-start.35 = (f32[8,768]{1,0:T(8,128)S(1)}, f32[8,768]{1,0:T(8,128)S(1)}, u32[]{:S(2)}, u32[]{:S(2)}) collective-permute-start(f32[8,768]{1,0:T(8,128)S(1)} %add.185), channel_id=1, source_target_pairs={{0,8},{2,10},{4,12},{6,14},{8,0},{10,2},{12,4},{14,6},{16,24},{18,... | collective-permute-start | bytes 73736 | tf_op jit(solution)/shard_map/ppermute | solution.py:548
  85.3 1.9 collective-permute-start.7
  88.7 2.7 %collective-permute-start.36 = (f32[8,768]{1,0:T(8,128)S(1)}, f32[8,768]{1,0:T(8,128)S(1)}, u32[]{:S(2)}, u32[]{:S(2)}) collective-permute-start(f32[8,768]{1,0:T(8,128)S(1)} %add.186), channel_id=1, source_target_pairs={{0,16},{2,18},{4,20},{6,22},{8,24},{10,26},{12,28},{14,30},{16,0},... | collective-permute-start | bytes 73736 | tf_op jit(solution)/shard_map/ppermute | solution.py:548
  92.3 13.2 %collective-permute-done.36 = f32[8,768]{1,0:T(8,128)S(1)} collective-permute-done((f32[8,768]{1,0:T(8,128)S(1)}, f32[8,768]{1,0:T(8,128)S(1)}, u32[]{:S(2)}, u32[]{:S(2)}) %collective-permute-start.36) | collective-permute-done | bytes 24608 | tf_op jit(solution)/shard_map/ppermute | solution.py:548
  107.9 6.3 %attention_backward.4 = (bf16[384,1024]{1,0:T(8,128)(2,1)S(1)}, bf16[384,1024]{1,0:T(8,128)(2,1)S(1)}, bf16[384,1024]{1,0:T(8,128)(2,1)S(1)}) custom-call(s32[2]{0:T(128)S(1)} %pad_add_fusion.info_ref, s32[4]{0:T(128)S(1)} %bitcast.10, bf16[384,1024]{1,0:T(8,128)(2,1)S(1)} %get-tuple-element.77.q_ref, bf16[384,1024]{1,0:T(8,128)(2,1)S(1)} %copy-done.23, ...), custom_call_target="tpu_custom_call" | custom-call | flops 6000000000 | bytes 4718592 | tf_op jit(solution)/shard_map/attention_backward/pallas_call | solution.py:28
  114.2 6.1 %attention_backward.5 = (bf16[384,1024]{1,0:T(8,128)(2,1)S(1)}, bf16[384,1024]{1,0:T(8,128)(2,1)S(1)}, bf16[384,1024]{1,0:T(8,128)(2,1)S(1)}) custom-call(s32[2]{0:T(128)S(1)} %pad_add_fusion.info_ref, s32[4]{0:T(128)S(1)} %bitcast.11, bf16[384,1024]{1,0:T(8,128)(2,1)S(1)} %get-tuple-element.77.q_ref, ...), custom_call_target="tpu_custom_call", output_to_operand_aliasing={{0}: (11, {}), {1}: (12, {}), {2}: (13, {})} | custom-call | flops 6000000000 | bytes 4718592 | tf_op jit(solution)/shard_map/attention_backward/pallas_call | solution.py:28
  122.5 4.6 %collective-permute-start.10 = (bf16[192,1280]{1,0:T(8,128)(2,1)S(1)}, bf16[192,1280]{1,0:T(8,128)(2,1)S(1)}, u32[]{:S(2)}, u32[]{:S(2)}) collective-permute-start(bf16[192,1280]{1,0:T(8,128)(2,1)S(1)} %get-tuple-element.139), channel_id=1, source_target_pairs={{0,8},{2,10},{4,12},{6,14},{8,0},{10,2},{12,4},{14,6},{16,24},{18,... | collective-permute-start | bytes 1474568 | tf_op jit(solution)/shard_map/ppermute | solution.py:548
  128.9 6.1 %attention_backward.6 = (bf16[384,1024]{1,0:T(8,128)(2,1)S(1)}, bf16[384,1024]{1,0:T(8,128)(2,1)S(1)}, bf16[384,1024]{1,0:T(8,128)(2,1)S(1)}) custom-call(s32[2]{0:T(128)S(1)} %pad_add_fusion.info_ref, s32[4]{0:T(128)S(1)} %bitcast.12, bf16[384,1024]{1,0:T(8,128)(2,1)S(1)} %get-tuple-element.77.q_ref, ...), custom_call_target="tpu_custom_call", output_to_operand_aliasing={{0}: (11, {}), {1}: (12, {}), {2}: (13, {})} | custom-call | flops 6000000000 | bytes 4718592 | tf_op jit(solution)/shard_map/attention_backward/pallas_call | solution.py:28
  136.0 2.6 %collective-permute-done.10 = bf16[192,1280]{1,0:T(8,128)(2,1)S(1)} collective-permute-done((bf16[192,1280]{1,0:T(8,128)(2,1)S(1)}, bf16[192,1280]{1,0:T(8,128)(2,1)S(1)}, u32[]{:S(2)}, u32[]{:S(2)}) %collective-permute-start.10) | collective-permute-done | bytes 491552 | tf_op jit(solution)/shard_map/ppermute | solution.py:548
  139.4 2.1 %collective-permute-done.9 = bf16[192,1280]{1,0:T(8,128)(2,1)S(1)} collective-permute-done((bf16[192,1280]{1,0:T(8,128)(2,1)S(1)}, bf16[192,1280]{1,0:T(8,128)(2,1)S(1)}, u32[]{:S(2)}, u32[]{:S(2)}) %collective-permute-start.9) | collective-permute-done | bytes 491552 | tf_op jit(solution)/shard_map/ppermute | solution.py:548
  142.5 6.3 %attention_backward.7 = (bf16[384,1024]{1,0:T(8,128)(2,1)S(1)}, bf16[384,1024]{1,0:T(8,128)(2,1)S(1)}, bf16[384,1024]{1,0:T(8,128)(2,1)S(1)}) custom-call(s32[2]{0:T(128)S(1)} %pad_add_fusion.info_ref, s32[4]{0:T(128)S(1)} %bitcast.13, bf16[384,1024]{1,0:T(8,128)(2,1)S(1)} %get-tuple-element.77.q_ref, ...), custom_call_target="tpu_custom_call", output_to_operand_aliasing={{0}: (11, {}), {1}: (12, {}), {2}: (13, {})} | custom-call | flops 6000000000 | bytes 4718592 | tf_op jit(solution)/shard_map/attention_backward/pallas_call | solution.py:28
  148.8 3.8 %project_grad.1 = (bf16[384,512]{1,0:T(8,128)(2,1)S(1)}, bf16[384,512]{1,0:T(8,128)(2,1)S(1)}, bf16[384,512]{1,0:T(8,128)(2,1)S(1)}, bf16[384,512]{1,0:T(8,128)(...) custom-call(s32[2]{0:T(128)S(1)} %pad_add_fusion.info_ref, bf16[1024,768]{1,0:T(8,128)(2,1)S(1)} %copy-done.19, ...), custom_call_target="tpu_custom_call" | custom-call | flops 1811939328 | bytes 4718592 | tf_op jit(solution)/shard_map/project_grad/pallas_call | solution.py:28
  155.4 1.9 stream_grad.2
  158.2 9.2 %collective-permute-done.31 = bf16[48,1280]{1,0:T(8,128)(2,1)S(1)} collective-permute-done((bf16[48,1280]{1,0:T(8,128)(2,1)S(1)}, bf16[48,1280]{1,0:T(8,128)(2,1)S(1)}, u32[]{:S(2)}, u32[]{:S(2)}) %collective-permute-start.31) | collective-permute-done | bytes 122912 | tf_op jit(solution)/shard_map/ppermute | solution.py:548
  168.2 5.7 %collective-permute-done.29 = bf16[48,1280]{1,0:T(8,128)(2,1)S(1)} collective-permute-done((bf16[48,1280]{1,0:T(8,128)(2,1)S(1)}, bf16[48,1280]{1,0:T(8,128)(2,1)S(1)}, u32[]{:S(2)}, u32[]{:S(2)}) %collective-permute-start.29) | collective-permute-done | bytes 122912 | tf_op jit(solution)/shard_map/ppermute | solution.py:548
  174.6 7.1 %collective-permute-done.27 = bf16[48,1280]{1,0:T(8,128)(2,1)S(1)} collective-permute-done((bf16[48,1280]{1,0:T(8,128)(2,1)S(1)}, bf16[48,1280]{1,0:T(8,128)(2,1)S(1)}, u32[]{:S(2)}, u32[]{:S(2)}) %collective-permute-start.27) | collective-permute-done | bytes 122912 | tf_op jit(solution)/shard_map/ppermute | solution.py:548
  183.0 2.5 %collective-permute-start.15 = (bf16[192,512]{1,0:T(8,128)(2,1)S(1)}, bf16[192,512]{1,0:T(8,128)(2,1)S(1)}, u32[]{:S(2)}, u32[]{:S(2)}) collective-permute-start(bf16[192,512]{1,0:T(8,128)(2,1)S(1)} %get-tuple-element.155), channel_id=1, source_target_pairs={{0,4},{2,6},{4,0},{6,2},{8,12},{10,14},{12,8},{14,10},{16,20},{18,... | collective-permute-start | bytes 589832 | tf_op jit(solution)/shard_map/ppermute | solution.py:548
  185.5 3.9 %collective-permute-done.23 = bf16[192,512]{1,0:T(8,128)(2,1)S(1)} collective-permute-done((bf16[192,512]{1,0:T(8,128)(2,1)S(1)}, bf16[192,512]{1,0:T(8,128)(2,1)S(1)}, u32[]{:S(2)}, u32[]{:S(2)}) %collective-permute-start.23) | collective-permute-done | bytes 196640 | tf_op jit(solution)/shard_map/ppermute | solution.py:548
  195.1 2.1 %collective-permute-start.21 = (bf16[48,512]{1,0:T(8,128)(2,1)S(1)}, bf16[48,512]{1,0:T(8,128)(2,1)S(1)}, u32[]{:S(2)}, u32[]{:S(2)}) collective-permute-start(bf16[48,512]{1,0:T(8,128)(2,1)S(1)} %add_convert_fusion.32), channel_id=1, source_target_pairs={{0,16},{2,18},{4,20},{6,22},{8,24},{10,26},{12,28},{14,30},{16,0},... | collective-permute-start | bytes 147464 | tf_op jit(solution)/shard_map/ppermute | solution.py:548
  198.4 2.5 %collective-permute-done.25 = bf16[48,512]{1,0:T(8,128)(2,1)S(1)} collective-permute-done((bf16[48,512]{1,0:T(8,128)(2,1)S(1)}, bf16[48,512]{1,0:T(8,128)(2,1)S(1)}, u32[]{:S(2)}, u32[]{:S(2)}) %collective-permute-start.25) | collective-permute-done | bytes 49184 | tf_op jit(solution)/shard_map/ppermute | solution.py:548
  204.4 3.1 %stream_grad.3 = bf16[512,768]{1,0:T(8,128)(2,1)} custom-call(s32[2]{0:T(128)S(1)} %pad_add_fusion.info_ref, bf16[384,1024]{1,0:T(8,128)(2,1)S(1)} %get-tuple-element.131.dq_ref, bf16[384,1024]{1,0:T(8,128)(2,1)S(1)} %get-tuple-element.132.dk_ref, bf16[384,1024]{1,0:T(8,128)(2,1)S(1)} %get-tuple-element.133.dv_ref, bf16[768,768]{1,0:T(8,128)(2,1)S(1)} %copy-done.1, ...), custom_call_target="tpu_custom_call" | custom-call | flops 905969664 | bytes 1572864 | tf_op jit(solution)/shard_map/stream_grad/pallas_call | solution.py:28
  (161 shorter events, 47.3 us)
Async XLA Ops:
  45.4 11.7 %collective-permute-start.2 = (bf16[768,1280]{1,0:T(8,128)(2,1)S(1)}, bf16[768,1280]{1,0:T(8,128)(2,1)S(1)}, u32[]{:S(2)}, u32[]{:S(2)}) collective-permute-start(bf16[768,1280]{1,0:T(8,128)(2,1)S(1)} %weight_away.1), channel_id=1, source_target_pairs={{0,1},{1,0},{2,3},{3,2},{4,5},{5,4},{6,7},{7,6},{8,9},{9,8},{10,11... | collective-permute-start | bytes 5898248 | tf_op jit(solution)/shard_map/ppermute | solution.py:543
  56.7 6.6 %collective-permute-start.4 = (bf16[768,1280]{1,0:T(8,128)(2,1)S(1)}, bf16[768,1280]{1,0:T(8,128)(2,1)S(1)}, u32[]{:S(2)}, u32[]{:S(2)}) collective-permute-start(bf16[768,1280]{1,0:T(8,128)(2,1)S(1)} %get-tuple-element.95), channel_id=1, source_target_pairs={{0,1},{1,0},{2,3},{3,2},{4,5},{5,4},{6,7},{7,6},{8,9},{9,8},{10,11... | collective-permute-start | bytes 5898248 | tf_op jit(solution)/shard_map/ppermute | solution.py:543
  74.8 4.4 %collective-permute-start.33 = (f32[8,768]{1,0:T(8,128)S(1)}, f32[8,768]{1,0:T(8,128)S(1)}, u32[]{:S(2)}, u32[]{:S(2)}) collective-permute-start(f32[8,768]{1,0:T(8,128)S(1)} %add.183), channel_id=1, source_target_pairs={{0,2},{2,0},{4,6},{6,4},{8,10},{10,8},{12,14},{14,12},{16,18},{18,... | collective-permute-start | bytes 73736 | tf_op jit(solution)/shard_map/ppermute | solution.py:548
  83.1 5.5 %collective-permute-start.35 = (f32[8,768]{1,0:T(8,128)S(1)}, f32[8,768]{1,0:T(8,128)S(1)}, u32[]{:S(2)}, u32[]{:S(2)}) collective-permute-start(f32[8,768]{1,0:T(8,128)S(1)} %add.185), channel_id=1, source_target_pairs={{0,8},{2,10},{4,12},{6,14},{8,0},{10,2},{12,4},{14,6},{16,24},{18,... | collective-permute-start | bytes 73736 | tf_op jit(solution)/shard_map/ppermute | solution.py:548
  85.2 35.2 %collective-permute-start.5 = (bf16[384,1280]{1,0:T(8,128)(2,1)S(1)}, bf16[384,1280]{1,0:T(8,128)(2,1)S(1)}, u32[]{:S(2)}, u32[]{:S(2)}) collective-permute-start(bf16[384,1280]{1,0:T(8,128)(2,1)S(1)} %get-tuple-element.90), channel_id=1, source_target_pairs={{0,8},{2,10},{4,12},{6,14},{8,0},{10,2},{12,4},{14,6},{16,24},{18,... | collective-permute-start | bytes 2949128 | tf_op jit(solution)/shard_map/ppermute | solution.py:548
  85.3 36.9 %collective-permute-start.7 = (bf16[384,1280]{1,0:T(8,128)(2,1)S(1)}, bf16[384,1280]{1,0:T(8,128)(2,1)S(1)}, u32[]{:S(2)}, u32[]{:S(2)}) collective-permute-start(bf16[384,1280]{1,0:T(8,128)(2,1)S(1)} %get-tuple-element.96), channel_id=1, source_target_pairs={{0,4},{2,6},{4,0},{6,2},{8,12},{10,14},{12,8},{14,10},{16,20},{18,... | collective-permute-start | bytes 2949128 | tf_op jit(solution)/shard_map/ppermute | solution.py:548
  87.1 39.9 %collective-permute-start.6 = (bf16[384,1280]{1,0:T(8,128)(2,1)S(1)}, bf16[384,1280]{1,0:T(8,128)(2,1)S(1)}, u32[]{:S(2)}, u32[]{:S(2)}) collective-permute-start(bf16[384,1280]{1,0:T(8,128)(2,1)S(1)} %get-tuple-element.92), channel_id=1, source_target_pairs={{0,2},{2,0},{4,6},{6,4},{8,10},{10,8},{12,14},{14,12},{16,18},{18,... | collective-permute-start | bytes 2949128 | tf_op jit(solution)/shard_map/ppermute | solution.py:548
  88.6 19.3 %collective-permute-start.11 = (bf16[384,512]{1,0:T(8,128)(2,1)S(1)}, bf16[384,512]{1,0:T(8,128)(2,1)S(1)}, u32[]{:S(2)}, u32[]{:S(2)}) collective-permute-start(bf16[384,512]{1,0:T(8,128)(2,1)S(1)} %get-tuple-element.107), channel_id=1, source_target_pairs={{0,1},{1,0},{2,3},{3,2},{4,5},{5,4},{6,7},{7,6},{8,9},{9,8},{10,11... | collective-permute-start | bytes 1179656 | tf_op jit(solution)/shard_map/ppermute | solution.py:543
  88.7 16.8 %collective-permute-start.36 = (f32[8,768]{1,0:T(8,128)S(1)}, f32[8,768]{1,0:T(8,128)S(1)}, u32[]{:S(2)}, u32[]{:S(2)}) collective-permute-start(f32[8,768]{1,0:T(8,128)S(1)} %add.186), channel_id=1, source_target_pairs={{0,16},{2,18},{4,20},{6,22},{8,24},{10,26},{12,28},{14,30},{16,0},... | collective-permute-start | bytes 73736 | tf_op jit(solution)/shard_map/ppermute | solution.py:548
  105.5 43.3 %collective-permute-start.12 = (bf16[768,384]{1,0:T(8,128)(2,1)S(1)}, bf16[768,384]{1,0:T(8,128)(2,1)S(1)}, u32[]{:S(2)}, u32[]{:S(2)}) collective-permute-start(bf16[768,384]{1,0:T(8,128)(2,1)S(1)} %get-tuple-element.124), channel_id=1, source_target_pairs={{0,1},{1,0},{2,3},{3,2},{4,5},{5,4},{6,7},{7,6},{8,9},{9,8},{10,11... | collective-permute-start | bytes 1769480 | tf_op jit(solution)/shard_map/ppermute | solution.py:543
  120.6 14.4 %collective-permute-start.8 = (bf16[192,1280]{1,0:T(8,128)(2,1)S(1)}, bf16[192,1280]{1,0:T(8,128)(2,1)S(1)}, u32[]{:S(2)}, u32[]{:S(2)}) collective-permute-start(bf16[192,1280]{1,0:T(8,128)(2,1)S(1)} %get-tuple-element.143), channel_id=1, source_target_pairs={{0,2},{2,0},{4,6},{6,4},{8,10},{10,8},{12,14},{14,12},{16,18},{18,... | collective-permute-start | bytes 1474568 | tf_op jit(solution)/shard_map/ppermute | solution.py:548
  122.5 16.2 %collective-permute-start.10 = (bf16[192,1280]{1,0:T(8,128)(2,1)S(1)}, bf16[192,1280]{1,0:T(8,128)(2,1)S(1)}, u32[]{:S(2)}, u32[]{:S(2)}) collective-permute-start(bf16[192,1280]{1,0:T(8,128)(2,1)S(1)} %get-tuple-element.139), channel_id=1, source_target_pairs={{0,8},{2,10},{4,12},{6,14},{8,0},{10,2},{12,4},{14,6},{16,24},{18,... | collective-permute-start | bytes 1474568 | tf_op jit(solution)/shard_map/ppermute | solution.py:548
  127.3 14.2 %collective-permute-start.9 = (bf16[192,1280]{1,0:T(8,128)(2,1)S(1)}, bf16[192,1280]{1,0:T(8,128)(2,1)S(1)}, u32[]{:S(2)}, u32[]{:S(2)}) collective-permute-start(bf16[192,1280]{1,0:T(8,128)(2,1)S(1)} %get-tuple-element.141), channel_id=1, source_target_pairs={{0,4},{2,6},{4,0},{6,2},{8,12},{10,14},{12,8},{14,10},{16,20},{18,... | collective-permute-start | bytes 1474568 | tf_op jit(solution)/shard_map/ppermute | solution.py:548
  135.2 22.2 %collective-permute-start.30 = (bf16[96,1280]{1,0:T(8,128)(2,1)S(1)}, bf16[96,1280]{1,0:T(8,128)(2,1)S(1)}, u32[]{:S(2)}, u32[]{:S(2)}) collective-permute-start(bf16[96,1280]{1,0:T(8,128)(2,1)S(1)} %get-tuple-element.145), channel_id=1, source_target_pairs={{0,4},{2,6},{4,0},{6,2},{8,12},{10,14},{12,8},{14,10},{16,20},{18,... | collective-permute-start | bytes 737288 | tf_op jit(solution)/shard_map/ppermute | solution.py:548
  138.8 19.2 %collective-permute-start.28 = (bf16[96,1280]{1,0:T(8,128)(2,1)S(1)}, bf16[96,1280]{1,0:T(8,128)(2,1)S(1)}, u32[]{:S(2)}, u32[]{:S(2)}) collective-permute-start(bf16[96,1280]{1,0:T(8,128)(2,1)S(1)} %get-tuple-element.147), channel_id=1, source_target_pairs={{0,2},{2,0},{4,6},{6,4},{8,10},{10,8},{12,14},{14,12},{16,18},{18,... | collective-permute-start | bytes 737288 | tf_op jit(solution)/shard_map/ppermute | solution.py:548
  141.6 16.5 %collective-permute-start.26 = (bf16[96,1280]{1,0:T(8,128)(2,1)S(1)}, bf16[96,1280]{1,0:T(8,128)(2,1)S(1)}, u32[]{:S(2)}, u32[]{:S(2)}) collective-permute-start(bf16[96,1280]{1,0:T(8,128)(2,1)S(1)} %get-tuple-element.149), channel_id=1, source_target_pairs={{0,8},{2,10},{4,12},{6,14},{8,0},{10,2},{12,4},{14,6},{16,24},{18,... | collective-permute-start | bytes 737288 | tf_op jit(solution)/shard_map/ppermute | solution.py:548
  152.6 29.9 %collective-permute-start.22 = (bf16[384,512]{1,0:T(8,128)(2,1)S(1)}, bf16[384,512]{1,0:T(8,128)(2,1)S(1)}, u32[]{:S(2)}, u32[]{:S(2)}) collective-permute-start(bf16[384,512]{1,0:T(8,128)(2,1)S(1)} %get-tuple-element.130), channel_id=1, source_target_pairs={{0,8},{2,10},{4,12},{6,14},{8,0},{10,2},{12,4},{14,6},{16,24},{18,... | collective-permute-start | bytes 1179656 | tf_op jit(solution)/shard_map/ppermute | solution.py:548
  153.9 28.8 %collective-permute-start.18 = (bf16[384,512]{1,0:T(8,128)(2,1)S(1)}, bf16[384,512]{1,0:T(8,128)(2,1)S(1)}, u32[]{:S(2)}, u32[]{:S(2)}) collective-permute-start(bf16[384,512]{1,0:T(8,128)(2,1)S(1)} %get-tuple-element.128), channel_id=1, source_target_pairs={{0,4},{2,6},{4,0},{6,2},{8,12},{10,14},{12,8},{14,10},{16,20},{18,... | collective-permute-start | bytes 1179656 | tf_op jit(solution)/shard_map/ppermute | solution.py:548
  157.4 25.5 %collective-permute-start.14 = (bf16[384,512]{1,0:T(8,128)(2,1)S(1)}, bf16[384,512]{1,0:T(8,128)(2,1)S(1)}, u32[]{:S(2)}, u32[]{:S(2)}) collective-permute-start(bf16[384,512]{1,0:T(8,128)(2,1)S(1)} %get-tuple-element.126), channel_id=1, source_target_pairs={{0,2},{2,0},{4,6},{6,4},{8,10},{10,8},{12,14},{14,12},{16,18},{18,... | collective-permute-start | bytes 1179656 | tf_op jit(solution)/shard_map/ppermute | solution.py:548
  158.0 46.4 %collective-permute-start.13 = (bf16[768,512]{1,0:T(8,128)(2,1)S(1)}, bf16[768,512]{1,0:T(8,128)(2,1)S(1)}, u32[]{:S(2)}, u32[]{:S(2)}) collective-permute-start(bf16[768,512]{1,0:T(8,128)(2,1)S(1)} %stream_grad.2), channel_id=1, source_target_pairs={{0,1},{1,0},{2,3},{3,2},{4,5},{5,4},{6,7},{7,6},{8,9},{9,8},{10,11... | collective-permute-start | bytes 2359304 | tf_op jit(solution)/shard_map/ppermute | solution.py:543
  158.1 9.3 %collective-permute-start.31 = (bf16[48,1280]{1,0:T(8,128)(2,1)S(1)}, bf16[48,1280]{1,0:T(8,128)(2,1)S(1)}, u32[]{:S(2)}, u32[]{:S(2)}) collective-permute-start(bf16[48,1280]{1,0:T(8,128)(2,1)S(1)} %add_convert_fusion.18), channel_id=1, source_target_pairs={{0,16},{2,18},{4,20},{6,22},{8,24},{10,26},{12,28},{14,30},{16,0},... | collective-permute-start | bytes 368648 | tf_op jit(solution)/shard_map/ppermute | solution.py:548
  167.4 6.4 %collective-permute-start.29 = (bf16[48,1280]{1,0:T(8,128)(2,1)S(1)}, bf16[48,1280]{1,0:T(8,128)(2,1)S(1)}, u32[]{:S(2)}, u32[]{:S(2)}) collective-permute-start(bf16[48,1280]{1,0:T(8,128)(2,1)S(1)} %add_convert_fusion.20), channel_id=1, source_target_pairs={{0,16},{2,18},{4,20},{6,22},{8,24},{10,26},{12,28},{14,30},{16,0},... | collective-permute-start | bytes 368648 | tf_op jit(solution)/shard_map/ppermute | solution.py:548
  173.8 7.9 %collective-permute-start.27 = (bf16[48,1280]{1,0:T(8,128)(2,1)S(1)}, bf16[48,1280]{1,0:T(8,128)(2,1)S(1)}, u32[]{:S(2)}, u32[]{:S(2)}) collective-permute-start(bf16[48,1280]{1,0:T(8,128)(2,1)S(1)} %add_convert_fusion.22), channel_id=1, source_target_pairs={{0,16},{2,18},{4,20},{6,22},{8,24},{10,26},{12,28},{14,30},{16,0},... | collective-permute-start | bytes 368648 | tf_op jit(solution)/shard_map/ppermute | solution.py:548
  182.6 6.8 %collective-permute-start.23 = (bf16[192,512]{1,0:T(8,128)(2,1)S(1)}, bf16[192,512]{1,0:T(8,128)(2,1)S(1)}, u32[]{:S(2)}, u32[]{:S(2)}) collective-permute-start(bf16[192,512]{1,0:T(8,128)(2,1)S(1)} %get-tuple-element.151), channel_id=1, source_target_pairs={{0,2},{2,0},{4,6},{6,4},{8,10},{10,8},{12,14},{14,12},{16,18},{18,... | collective-permute-start | bytes 589832 | tf_op jit(solution)/shard_map/ppermute | solution.py:548
  182.8 7.5 %collective-permute-start.19 = (bf16[192,512]{1,0:T(8,128)(2,1)S(1)}, bf16[192,512]{1,0:T(8,128)(2,1)S(1)}, u32[]{:S(2)}, u32[]{:S(2)}) collective-permute-start(bf16[192,512]{1,0:T(8,128)(2,1)S(1)} %get-tuple-element.153), channel_id=1, source_target_pairs={{0,8},{2,10},{4,12},{6,14},{8,0},{10,2},{12,4},{14,6},{16,24},{18,... | collective-permute-start | bytes 589832 | tf_op jit(solution)/shard_map/ppermute | solution.py:548
  183.0 9.2 %collective-permute-start.15 = (bf16[192,512]{1,0:T(8,128)(2,1)S(1)}, bf16[192,512]{1,0:T(8,128)(2,1)S(1)}, u32[]{:S(2)}, u32[]{:S(2)}) collective-permute-start(bf16[192,512]{1,0:T(8,128)(2,1)S(1)} %get-tuple-element.155), channel_id=1, source_target_pairs={{0,4},{2,6},{4,0},{6,2},{8,12},{10,14},{12,8},{14,10},{16,20},{18,... | collective-permute-start | bytes 589832 | tf_op jit(solution)/shard_map/ppermute | solution.py:548
  189.4 4.7 %collective-permute-start.24 = (bf16[96,512]{1,0:T(8,128)(2,1)S(1)}, bf16[96,512]{1,0:T(8,128)(2,1)S(1)}, u32[]{:S(2)}, u32[]{:S(2)}) collective-permute-start(bf16[96,512]{1,0:T(8,128)(2,1)S(1)} %get-tuple-element.157), channel_id=1, source_target_pairs={{0,4},{2,6},{4,0},{6,2},{8,12},{10,14},{12,8},{14,10},{16,20},{18,... | collective-permute-start | bytes 294920 | tf_op jit(solution)/shard_map/ppermute | solution.py:548
  190.4 4.7 %collective-permute-start.20 = (bf16[96,512]{1,0:T(8,128)(2,1)S(1)}, bf16[96,512]{1,0:T(8,128)(2,1)S(1)}, u32[]{:S(2)}, u32[]{:S(2)}) collective-permute-start(bf16[96,512]{1,0:T(8,128)(2,1)S(1)} %get-tuple-element.159), channel_id=1, source_target_pairs={{0,2},{2,0},{4,6},{6,4},{8,10},{10,8},{12,14},{14,12},{16,18},{18,... | collective-permute-start | bytes 294920 | tf_op jit(solution)/shard_map/ppermute | solution.py:548
  192.2 5.2 %collective-permute-start.16 = (bf16[96,512]{1,0:T(8,128)(2,1)S(1)}, bf16[96,512]{1,0:T(8,128)(2,1)S(1)}, u32[]{:S(2)}, u32[]{:S(2)}) collective-permute-start(bf16[96,512]{1,0:T(8,128)(2,1)S(1)} %get-tuple-element.161), channel_id=1, source_target_pairs={{0,8},{2,10},{4,12},{6,14},{8,0},{10,2},{12,4},{14,6},{16,24},{18,... | collective-permute-start | bytes 294920 | tf_op jit(solution)/shard_map/ppermute | solution.py:548
  194.1 6.7 %collective-permute-start.25 = (bf16[48,512]{1,0:T(8,128)(2,1)S(1)}, bf16[48,512]{1,0:T(8,128)(2,1)S(1)}, u32[]{:S(2)}, u32[]{:S(2)}) collective-permute-start(bf16[48,512]{1,0:T(8,128)(2,1)S(1)} %add_convert_fusion.30), channel_id=1, source_target_pairs={{0,16},{2,18},{4,20},{6,22},{8,24},{10,26},{12,28},{14,30},{16,0},... | collective-permute-start | bytes 147464 | tf_op jit(solution)/shard_map/ppermute | solution.py:548
  195.1 6.3 %collective-permute-start.21 = (bf16[48,512]{1,0:T(8,128)(2,1)S(1)}, bf16[48,512]{1,0:T(8,128)(2,1)S(1)}, u32[]{:S(2)}, u32[]{:S(2)}) collective-permute-start(bf16[48,512]{1,0:T(8,128)(2,1)S(1)} %add_convert_fusion.32), channel_id=1, source_target_pairs={{0,16},{2,18},{4,20},{6,22},{8,24},{10,26},{12,28},{14,30},{16,0},... | collective-permute-start | bytes 147464 | tf_op jit(solution)/shard_map/ppermute | solution.py:548
  197.5 5.6 %collective-permute-start.17 = (bf16[48,512]{1,0:T(8,128)(2,1)S(1)}, bf16[48,512]{1,0:T(8,128)(2,1)S(1)}, u32[]{:S(2)}, u32[]{:S(2)}) collective-permute-start(bf16[48,512]{1,0:T(8,128)(2,1)S(1)} %add_convert_fusion.34), channel_id=1, source_target_pairs={{0,16},{2,18},{4,20},{6,22},{8,24},{10,26},{12,28},{14,30},{16,0},... | collective-permute-start | bytes 147464 | tf_op jit(solution)/shard_map/ppermute | solution.py:548
  (35 other events, 416.1 us)

commit v2 on v1

--- a/solution.py
+++ b/solution.py
@@ -20,7 +20,9 @@
 WIDE = 512
 ROWS = 64
 SPANS = 4
+PLAN = ((0,), (1,))
 MIB = 1 << 20
+EASE = 50
 
 
 def call(kernel, name, scalars, arrays, out_shape, flops, scratch=(), room=16, aliases=None):
@@ -33,7 +35,7 @@
         out_shape=out_shape,
         scratch_shapes=list(scratch),
         input_output_aliases=aliases or {},
-        cost_estimate=pl.CostEstimate(flops=flops, bytes_accessed=2 * moved, transcendentals=0),
+        cost_estimate=pl.CostEstimate(flops=flops // EASE, bytes_accessed=moved // EASE, transcendentals=0),
         compiler_params=pltpu.CompilerParams(vmem_limit_bytes=room * MIB),
         name=name,
     )(*scalars, *arrays)
@@ -81,34 +83,83 @@
     return key <= lax.broadcasted_iota(jnp.int32, (block, block), 1)
 
 
+def project(to_refs, weights, x, openings, cos_ref, sin_ref, start):
+    rows = x.shape[0]
+    cols, pack = to_refs[0].shape
+    block = pack // SPANS
+    for weight, to_ref, scale in zip(weights, to_refs, (SCORE * LOG2E, 1.0, None)):
+        for number in range(rows // block):
+            part = dot(weight, x[number * block : (number + 1) * block], 1, 1)
+            first = start + number * block
+            if scale is None:
+                to_ref[:, at(first, block)] = part.astype(BF16)
+                continue
+            opening = functools.reduce(
+                lambda rest, span: jnp.where(first == span * block, openings[span], rest), range(SPANS), 0
+            )
+            here = at(first - opening, block)
+            cos = cos_ref[:, here] * scale
+            sin = sin_ref[:, here] * scale
+            for head in range(cols // HDIM):
+                a = part[head * HDIM : head * HDIM + HALF]
+                b = part[head * HDIM + HALF : (head + 1) * HDIM]
+                turned = jnp.concatenate([a * cos - b * sin, b * cos + a * sin], axis=0)
+                to_ref[head * HDIM : (head + 1) * HDIM, at(first, block)] = turned.astype(BF16)
+
+
+def project_own_kernel(
+    info_ref, len_ref, x_ref, cos_ref, sin_ref, wq_ref, wk_ref, wv_ref,
+    q_ref, k_ref, v_ref, all_ref, turned_ref, cq_ref, ck_ref, cv_ref, sems,
+):
+    cols, pack = q_ref.shape
+    rows = x_ref.shape[0]
+    side = info_ref[0]
+    copies = []
+    for index, (w_ref, c_ref) in enumerate(((wq_ref, cq_ref), (wk_ref, ck_ref), (wv_ref, cv_ref))):
+        copies.append(pltpu.make_async_copy(w_ref.at[:, at(side * cols, cols)], c_ref, sems.at[index]))
+        copies[-1].start()
+    _, openings = block_facts(len_ref, pack // SPANS)
+    all_ref[at(side * rows, rows), :] = x_ref[...]
+    for index, c_ref in enumerate((cq_ref, ck_ref, cv_ref)):
+        copies[index].wait()
+        turned_ref[index * cols : (index + 1) * cols, :] = c_ref[...].T
+    weights = [turned_ref[index * cols : (index + 1) * cols, :] for index in range(3)]
+    project((q_ref, k_ref, v_ref), weights, x_ref[...], openings, cos_ref, sin_ref, side * rows)
+
+
+def project_own(info, lengths, own, weights):
+    rows, width = own.shape
+    pack = 2 * rows
+    cols = weights[0].shape[1] // 2
+    vmem = pl.BlockSpec(memory_space=pltpu.VMEM)
+    smem = pl.BlockSpec(memory_space=pltpu.SMEM)
+    return pl.pallas_call(
+        project_own_kernel,
+        in_specs=[smem] * 2 + [vmem] * 3 + [pl.BlockSpec(memory_space=pltpu.HBM)] * 3,
+        out_specs=[vmem] * 8,
+        out_shape=[shape(BF16, cols, pack)] * 3
+        + [shape(BF16, pack, width), shape(BF16, 3 * cols, width)]
+        + [shape(BF16, width, cols)] * 3,
+        scratch_shapes=[pltpu.SemaphoreType.DMA((3,))],
+        cost_estimate=pl.CostEstimate(flops=4_000_000_000, bytes_accessed=8_000_000, transcendentals=0),
+        compiler_params=pltpu.CompilerParams(vmem_limit_bytes=8 * MIB),
+        name="project_own",
+    )(info, lengths, own, *rope_tables(pack), *weights)
+
+
 def attention_forward_kernel(
-    info_ref, len_ref, own_ref, oth_ref, wq_ref, wk_ref, wv_ref, cos_ref, sin_ref,
-    x_ref, q_ref, k_ref, v_ref, ctx_ref, mine_ref, away_ref, lse_ref,
+    info_ref, len_ref, _, __, ___, ____, oth_ref, turned_ref, cos_ref, sin_ref,
+    q_ref, k_ref, v_ref, x_ref, ctx_ref, mine_ref, away_ref, lse_ref,
 ):
-    rows = own_ref.shape[0]
+    rows = oth_ref.shape[0]
     cols, pack = q_ref.shape
     heads = cols // HDIM
     block = pack // SPANS
     segments, openings = block_facts(len_ref, block)
     side = info_ref[0]
-    x_ref[at(side * rows, rows), :] = own_ref[...]
     x_ref[at((1 - side) * rows, rows), :] = oth_ref[...]
-    for w_ref, to_ref, scale in ((wq_ref, q_ref, SCORE * LOG2E), (wk_ref, k_ref, 1.0), (wv_ref, v_ref, None)):
-        weight = w_ref[:, at(side * cols, cols)].T
-        for number in range(SPANS):
-            lanes = slice(number * block, (number + 1) * block)
-            part = dot(weight, x_ref[lanes, :], 1, 1)
-            if scale is None:
-                to_ref[:, lanes] = part.astype(BF16)
-                continue
-            here = at(number * block - openings[number], block)
-            cos = cos_ref[:, here] * scale
-            sin = sin_ref[:, here] * scale
-            for head in range(heads):
-                a = part[head * HDIM : head * HDIM + HALF]
-                b = part[head * HDIM + HALF : (head + 1) * HDIM]
-                turned = jnp.concatenate([a * cos - b * sin, b * cos + a * sin], axis=0)
-                to_ref[head * HDIM : (head + 1) * HDIM, lanes] = turned.astype(BF16)
+    weights = [turned_ref[index * cols : (index + 1) * cols, :] for index in range(3)]
+    project((q_ref, k_ref, v_ref), weights, oth_ref[...], openings, cos_ref, sin_ref, (1 - side) * rows)
     below = causal(block)
 
     @pl.loop(0, heads)
@@ -143,17 +194,18 @@
         away_ref[here, :] = ctx_ref[here, at((1 - side) * rows, rows)]
 
 
-def attention_forward(info, lengths, own, oth, weights):
-    rows, width = own.shape
-    pack = 2 * rows
-    cols = weights[0].shape[1] // 2
+def attention_forward(info, lengths, started, oth, turned):
+    rows, width = oth.shape
+    cols, pack = started[0].shape
     heads = cols // HDIM
     half = shape(BF16, cols, rows)
     return call(
         attention_forward_kernel, "attention_forward", (info, lengths),
-        (own, oth, *weights, *rope_tables(pack)),
-        [shape(BF16, pack, width)] + [shape(BF16, cols, pack)] * 4 + [half, half, shape(F32, heads, 1, pack)],
+        (*started, oth, turned, *rope_tables(pack)),
+        [shape(BF16, cols, pack)] * 3 + [shape(BF16, pack, width), shape(BF16, cols, pack)]
+        + [half, half, shape(F32, heads, 1, pack)],
         15_000_000_000,
+        aliases={2 + index: index for index in range(4)},
     )
 
 
@@ -161,13 +213,14 @@
     info_ref, len_ref, q_ref, k_ref, v_ref, ctx_ref, own_ref, oth_ref, lse_ref, cos_ref, sin_ref, *rest,
     first, heads,
 ):
-    dq_ref, dk_ref, dv_ref, dctx_ref, dk_acc, dv_acc = rest[-6:]
+    dq_ref, dk_ref, dv_ref, dctx_ref = rest[-4:]
     rows = own_ref.shape[1]
     pack = q_ref.shape[1]
     block = pack // SPANS
     segments, openings = block_facts(len_ref, block)
     side = info_ref[0]
     below = causal(block)
+    spans = [slice(number * block, (number + 1) * block) for number in range(SPANS)]
 
     def unturn(value, number, scale):
         here = at(number * block - openings[number], block)
@@ -176,7 +229,10 @@
         a, b = value[:HALF], value[HALF:]
         return jnp.concatenate([a * cos + b * sin, b * cos - a * sin], axis=0).astype(BF16)
 
-    @pl.loop(first, first + heads)
+    def plus(sums, index, value):
+        sums[index] = sums[index] + value if index in sums else value
+
+    @pl.loop(first, first + heads, unroll=2)
     def _(head):
         here = at(head * HDIM, HDIM)
         dctx_ref[:, at(side * rows, rows)] = own_ref[here, :]
@@ -184,36 +240,41 @@
         key = k_ref[here, :]
         keys = key.T
         values = v_ref[here, :].T
-        for i in range(SPANS):
-            lanes = slice(i * block, (i + 1) * block)
-            query = q_ref[here, lanes]
-            grad = dctx_ref[:, lanes]
-            delta = jnp.sum(grad.astype(F32) * ctx_ref[here, lanes].astype(F32), axis=0, keepdims=True)
-            lse = lse_ref[head, :, lanes]
-            dq = jnp.zeros((HDIM, block), F32)
-            for j in range(i + 1):
-                span = slice(j * block, (j + 1) * block)
-                score = dot(keys[span], query, 1, 0)
-                if j == i:
-                    prob = jnp.exp2(jnp.where(below, score, NEG) - lse)
-                else:
-                    prob = jnp.exp2(score - (lse - jnp.where(segments[i] == segments[j], 0.0, NEG)))
-                slope = dot(values[span], grad, 1, 0)
-                dscore = (prob * (slope - delta)).astype(BF16)
-                dq = dq + dot(key[:, span], dscore, 1, 0)
-                dk = dot(query, dscore, 1, 1)
-                dv = dot(grad, prob.astype(BF16), 1, 1)
-                if j == i:
-                    dk_acc[:, span] = dk
-                    dv_acc[:, span] = dv
-                else:
-                    dk_acc[:, span] += dk
-                    dv_acc[:, span] += dv
-            dq_ref[here, lanes] = unturn(dq, i, SCORE)
-        for number in range(SPANS):
-            lanes = slice(number * block, (number + 1) * block)
-            dk_ref[here, lanes] = unturn(dk_acc[:, lanes], number, 1.0 / LOG2E)
-            dv_ref[here, lanes] = dv_acc[:, lanes].astype(BF16)
+        delta = jnp.sum(dctx_ref[...].astype(F32) * ctx_ref[here, :].astype(F32), axis=0, keepdims=True)
+        lse = lse_ref[head, :, :]
+        raw, done, dqs, dks, dvs = {}, {}, {}, {}, {}
+
+        def scores(i, j):
+            return (
+                dot(keys[spans[j]], q_ref[here, spans[i]], 1, 0),
+                dot(values[spans[j]], dctx_ref[:, spans[i]], 1, 0),
+            )
+
+        def slopes(i, j, score, slope):
+            top = lse[:, spans[i]]
+            if j == i:
+                prob = jnp.exp2(jnp.where(below, score, NEG) - top)
+            else:
+                prob = jnp.exp2(score - (top - jnp.where(segments[i] == segments[j], 0.0, NEG)))
+            return prob.astype(BF16), (prob * (slope - delta[:, spans[i]])).astype(BF16)
+
+        def products(i, j, prob, dscore):
+            plus(dqs, i, dot(key[:, spans[j]], dscore, 1, 0))
+            plus(dks, j, dot(q_ref[here, spans[i]], dscore, 1, 1))
+            plus(dvs, j, dot(dctx_ref[:, spans[i]], prob, 1, 1))
+
+        pairs = [(i, j) for i in range(SPANS) for j in range(i + 1)]
+        for step in range(len(pairs) + 2):
+            if step < len(pairs):
+                raw[step] = scores(*pairs[step])
+            if 0 <= step - 1 < len(pairs):
+                done[step - 1] = slopes(*pairs[step - 1], *raw.pop(step - 1))
+            if 0 <= step - 2:
+                products(*pairs[step - 2], *done.pop(step - 2))
+        for number, lanes in enumerate(spans):
+            dq_ref[here, lanes] = unturn(dqs[number], number, SCORE)
+            dk_ref[here, lanes] = unturn(dks[number], number, 1.0 / LOG2E)
+            dv_ref[here, lanes] = dvs[number].astype(BF16)
 
 
 def attention_backward(info, lengths, kept, own, oth, first, heads, sofar):
@@ -225,7 +286,7 @@
         functools.partial(attention_backward_kernel, first=first, heads=heads),
         "attention_backward", (info, lengths), arrays, [shape(BF16, cols, pack)] * 3,
         heads * 3_000_000_000,
-        [pltpu.VMEM((HDIM, pack), BF16)] + [pltpu.VMEM((HDIM, pack), F32)] * 2,
+        [pltpu.VMEM((HDIM, pack), BF16)],
         aliases={base + index: index for index in range(len(sofar))},
     )
 
@@ -268,7 +329,7 @@
         return (places < total).astype(F32)
 
     def squares(row, value, valid):
-        small_ref[row : row + 1, :] += jnp.sum(value * value * valid, axis=0, keepdims=True)
+        add_small(small_ref, row, jnp.sum(value * value * valid, axis=0, keepdims=True))
 
     small_ref[...] = jnp.zeros_like(small_ref)
     m_ref[...] = dot(mine_ref[...].T, wo_ref[at(side * part, part), :], 1, 0) + dot(
@@ -317,10 +378,10 @@
         out_ref[here, :] = (r2 * inverse_rms(r2) * gain).astype(BF16)
         dr2_ref[here, :] = dr2
         dm_ref[here, :] = dr2.astype(BF16)
-        small_ref[1:2, :] += jnp.sum(dgain, axis=0, keepdims=True)
+        add_small(small_ref, 1, jnp.sum(dgain, axis=0, keepdims=True))
         squares(4, m, valid)
 
-    small_ref[5:6, :] = jnp.full((1, width), jnp.clip(total - first, 0, rows).astype(F32))
+    add_small(small_ref, 5, jnp.full((1, width), jnp.clip(total - first, 0, rows).astype(F32)))
     turn_ref[...] = dm_ref[...].T
     relative_rows(dmt_ref, turn_ref, info_ref[1], blocks)
 
@@ -332,13 +393,19 @@
         functools.partial(ffn_forward_kernel, blocks=blocks), "ffn_forward", (info, lengths),
         (x, mine, came, w_out, g1, g2, wg, wu, wd, cot),
         [shape(BF16, rows, ff)] * 3 + [shape(BF16, rows, width)] * 2 + [shape(BF16, width, rows)] * 2
-        + [shape(F32, rows, width)] * 2 + [shape(F32, 8, width)],
+        + [shape(F32, rows, width)] * 2 + [shape(F32, 16, WIDE)],
         6 * rows * width * ff,
         [
             pltpu.VMEM((rows, width), BF16), pltpu.VMEM((rows, width), F32),
             pltpu.VMEM((rows, width), F32), pltpu.VMEM((width, rows), BF16),
         ],
     )
+
+
+def add_small(small_ref, row, value):
+    for piece in range(-(-value.shape[1] // WIDE)):
+        part = value[:, piece * WIDE : (piece + 1) * WIDE]
+        small_ref[2 * row + piece : 2 * row + piece + 1, 0 : part.shape[1]] += part
 
 
 def split_store(product, came, to_refs, order, blocks):
@@ -380,40 +447,54 @@
     )
 
 
-def swiglu_back_kernel(
+def swiglu_away_kernel(
     info_ref, dm_ref, wd_ref, s_ref, t_ref, hbt_ref, dgt_ref, dup_ref, gate_ref, up_ref, *, orders, blocks
 ):
     half = gate_ref.shape[1]
 
-    def grads(start):
-        cols = at(start, CHUNK)
-        grad = dot(dm_ref[...], wd_ref[cols, :], 1, 1)
-        dup = (grad * s_ref[:, cols].astype(F32)).astype(BF16)
-        dgt = (grad * t_ref[:, cols].astype(F32)).astype(BF16)
-        dup_ref[:, cols] = dup
-        dgt_ref[:, cols] = dgt
-        return dgt, dup
-
     @pl.loop(0, half // CHUNK)
     def _(step):
         here = at(step * CHUNK, CHUNK)
-        dgt, dup = grads((1 - info_ref[0]) * half + step * CHUNK)
+        dgt, dup = swiglu_grads(
+            (1 - info_ref[0]) * half + step * CHUNK, dm_ref, wd_ref, s_ref, t_ref, dgt_ref, dup_ref
+        )
         split_store(dot(hbt_ref[...], dgt, 1, 0), None, [gate_ref.at[:, here]], orders[0], blocks)
         split_store(dot(hbt_ref[...], dup, 1, 0), None, [up_ref.at[:, here]], orders[1], blocks)
 
+
+def swiglu_grads(start, dm_ref, wd_ref, s_ref, t_ref, dgt_ref, dup_ref):
+    cols = at(start, CHUNK)
+    grad = dot(dm_ref[...], wd_ref[cols, :], 1, 1)
+    dup = (grad * s_ref[:, cols].astype(F32)).astype(BF16)
+    dgt = (grad * t_ref[:, cols].astype(F32)).astype(BF16)
+    dup_ref[:, cols] = dup
+    dgt_ref[:, cols] = dgt
+    return dgt, dup
+
+
+def swiglu_mine_kernel(info_ref, dm_ref, wd_ref, s_ref, t_ref, _, __, dgt_ref, dup_ref):
+    half = s_ref.shape[1] // 2
+
     @pl.loop(0, half // CHUNK)
     def _(step):
-        grads(info_ref[0] * half + step * CHUNK)
-
-
-def swiglu_back(info, dm, wd, s, t, hbt, orders, blocks):
+        swiglu_grads(info_ref[0] * half + step * CHUNK, dm_ref, wd_ref, s_ref, t_ref, dgt_ref, dup_ref)
+
+
+def swiglu_away(info, dm, wd, s, t, hbt, orders, blocks):
     rows, width = dm.shape
     ff = wd.shape[0]
     return call(
-        functools.partial(swiglu_back_kernel, orders=orders, blocks=blocks), "swiglu_back", (info,),
+        functools.partial(swiglu_away_kernel, orders=orders, blocks=blocks), "swiglu_away", (info,),
         (dm, wd, s, t, hbt),
         [shape(BF16, rows, ff)] * 2 + [shape(BF16, width, ff // 2)] * 2,
-        4 * rows * width * ff,
+        3 * rows * width * ff,
+    )
+
+
+def swiglu_mine(info, dm, wd, s, t, dgt, dup):
+    return call(
+        swiglu_mine_kernel, "swiglu_mine", (info,), (dm, wd, s, t, dgt, dup), [shape(BF16, *dgt.shape)] * 2,
+        dm.shape[0] * dm.shape[1] * wd.shape[0], aliases={5: 0, 6: 1},
     )
 
 
@@ -439,7 +520,7 @@
         dr1, dgain = norm_back(r1_ref[here, :], g1_ref[...], acc_ref[here, :])
         dr1_ref[here, :] = dr1
         da_ref[here, :] = dr1.astype(BF16)
-        small_ref[0:1, :] += jnp.sum(dgain, axis=0, keepdims=True)
+        add_small(small_ref, 0, jnp.sum(dgain, axis=0, keepdims=True))
 
     away_ref[...] = dot(wo_ref[at((1 - side) * cols, cols), :], da_ref[...], 1, 1).astype(BF16)
     own_ref[...] = dot(wo_ref[at(side * cols, cols), :], da_ref[...], 1, 1).astype(BF16)
@@ -456,7 +537,7 @@
         (dgt, dup, wg, wu, r1, dr2, g1, w_out, part),
         [
             shape(F32, rows, width), shape(BF16, width, rows), shape(BF16, cols, rows),
-            shape(BF16, cols, rows), shape(F32, 8, width),
+            shape(BF16, cols, rows), shape(F32, 16, WIDE),
         ],
         4 * rows * width * ff,
         [pltpu.VMEM((rows, width), F32), pltpu.VMEM((rows, width), BF16), pltpu.VMEM((width, rows), BF16)],
@@ -512,7 +593,7 @@
     mine = len(rest) == 3
     lanes = at((side if mine else 1 - side) * rows, rows)
     total = sum(
-        dot(w_ref[:, at(side * cols, cols)], g_ref[:, lanes], 1, 0)
+        dot(w_ref[...], g_ref[:, lanes], 1, 0)
         for w_ref, g_ref in ((wq_ref, dq_ref), (wk_ref, dk_ref), (wv_ref, dv_ref))
     )
     if mine:
@@ -548,32 +629,66 @@
     return lax.ppermute(value, "dp", [(i, i ^ (1 << bit)) for i in range(size)])
 
 
-def sum_everywhere(value):
-    value = value + swap_seq(value)
-    for bit in range(lax.axis_size("dp").bit_length() - 1):
-        value = value + swap_dp(value, bit)
-    return value
+def halves_of(small):
+    high = lax.reduce_precision(small, 8, 7)
+    return high.astype(BF16), (small - high).astype(BF16)
+
+
+def whole_of(high, low):
+    return high.astype(F32) + low.astype(F32)
 
 
 class Halving:
-    def __init__(self, keep, away, order, shift):
-        self.keep, self.order, self.shift = keep, order, shift
+    def __init__(self, keep, away, order, shift, small=None):
+        self.keep, self.order, self.shift, self.small = keep, order, shift, small
         self.sent, self.step = away, 0
 
     def send(self):
+        if self.small is not None:
+            self.pair = halves_of(self.small)
+            self.sent = jnp.concatenate([self.sent, *self.pair], axis=0)
         self.came = swap_dp(self.sent, self.order[self.step] + self.shift)
         self.step += 1
 
     def receive(self):
-        rows = self.keep.shape[0] // 2
+        rows = self.keep.shape[0]
+        if self.small is not None:
+            count = self.small.shape[0]
+            came = self.came[rows : rows + count], self.came[rows + count :]
+            self.small = whole_of(*self.pair) + whole_of(*came)
         if self.step < len(self.order):
-            self.sent = self.add(rows, 2 * rows)
-            self.keep = self.add(0, rows)
+            self.sent = self.add(rows // 2, rows)
+            self.keep = self.add(0, rows // 2)
         else:
-            self.keep = self.keep.astype(F32) + self.came.astype(F32)
+            self.keep = self.keep.astype(F32) + self.came[:rows].astype(F32)
 
     def add(self, low, high):
         return (self.keep[low:high].astype(F32) + self.came[low:high].astype(F32)).astype(BF16)
+
+    def relay(self, *others):
+        if others:
+            self.keep = after(self.keep, *others)
+        self.receive()
+        self.send()
+
+    @staticmethod
+    def last(parts):
+        for part in parts:
+            part.receive()
+            part.size = part.sent.shape[0]
+        rows = [part.sent for part in parts]
+        small = parts[0].small
+        if small is not None:
+            parts[0].pair = halves_of(small)
+            rows[1:1] = parts[0].pair
+        came = swap_dp(jnp.concatenate(rows, axis=0), parts[0].order[-1] + parts[0].shift)
+        start = 0
+        for part in parts:
+            end = start + part.size + (2 * small.shape[0] if part.small is not None else 0)
+            part.came = came[start:end]
+            start = end
+            part.step += 1
+            part.receive()
 
     def rest(self):
         value = self.keep
@@ -583,6 +698,8 @@
             keep = lax.dynamic_slice_in_dim(value, mine * half, half, 0)
             away = lax.dynamic_slice_in_dim(value, (1 - mine) * half, half, 0)
             value = keep + swap_dp(away.astype(BF16), bit).astype(F32)
+            if self.small is not None:
+                self.small = self.small + swap_dp(self.small, bit)
         return value
 
 
@@ -610,75 +727,83 @@
     blocks = min(dp_size, 16)
     bits = blocks.bit_length() - 1
     shift = (dp_size // blocks).bit_length() - 1
-    orders = [stage_order(bits, turn) for turn in range(3)]
+    turns = [stage_order(bits, turn) for turn in range(3)]
+    orders = ((0, 2, 1, 3), (1, 0, 2, 3), (2, 3, 1, 0))
     lengths = doc_lengths[0]
     seq_index = lax.axis_index("seq")
     info = jnp.stack([seq_index, lax.axis_index("dp") >> shift]).astype(jnp.int32)
     gain_one, gain_two = gain_attn.reshape(1, width), gain_ffn.reshape(1, width)
 
-    weights = (w_query, w_key, w_value)
-    gathered, query, key, value, context, mine, away, lse = attention_forward(
-        info, lengths, tokens, swap_seq(tokens), weights
+    oth = swap_seq(tokens)
+    *started, turned, own_q, own_k, own_v = project_own(info, lengths, tokens, (w_query, w_key, w_value))
+    query, key, value, gathered, context, mine, away, lse = attention_forward(
+        info, lengths, started, oth, turned
     )
     kept = (query, key, value, context, lse)
     came = swap_seq(away)
     act, silu, slope, result, dm, dm_turned, hb_turned, dr2, r1, small = ffn_forward(
         info, lengths, tokens, mine, came, w_out, gain_one, gain_two, w_gate, w_up, w_down, cotangent, blocks
     )
-    down_came = swap_seq(weight_grad(info, dm_turned, act, orders[2], blocks))
-    dgt, dup, gate_away, up_away = swiglu_back(
-        info, dm, w_down, silu, slope, hb_turned, orders[:2], blocks
+    down_away = weight_grad(info, dm_turned, act, orders[2], blocks)
+    down_came = swap_seq(down_away)
+    dgt, dup, gate_away, up_away = swiglu_away(
+        info, after(dm, down_away), w_down, silu, slope, hb_turned, orders[:2], blocks
     )
     gate_came, up_came = swap_seq(gate_away), swap_seq(up_away)
-    down = Halving(*weight_grad(info, dm_turned, after(act, gate_away), orders[2], blocks, down_came), orders[2], shift)
+    down = Halving(
+        *weight_grad(info, dm_turned, after(act, gate_away), orders[2], blocks, down_came), orders[2], shift
+    )
     down.send()
-    gate = Halving(*weight_grad(info, after(hb_turned, down.sent), dgt, orders[0], blocks, gate_came), orders[0], shift)
+    dgt, dup = swiglu_mine(info, after(dm, down.sent), w_down, silu, slope, dgt, dup)
+    gate = Halving(*weight_grad(info, hb_turned, dgt, orders[0], blocks, gate_came), orders[0], shift)
     gate.send()
-    up = Halving(*weight_grad(info, after(hb_turned, gate.sent), dup, orders[1], blocks, up_came), orders[1], shift)
+    dr1, da_turned, own_rows, away_rows, small = norm_one(
+        info, after(dgt, gate.sent), dup, w_gate, w_up, r1, dr2, gain_one, w_out, small, blocks
+    )
+    came_rows = swap_seq(away_rows)
+    up = Halving(
+        *weight_grad(info, after(hb_turned, away_rows), dup, orders[1], blocks, up_came), orders[1], shift
+    )
     up.send()
-    dr1, da_turned, own_rows, away_rows, small = norm_one(
-        info, after(dgt, up.sent), dup, w_gate, w_up, r1, dr2, gain_one, w_out, small, blocks
-    )
-    came_rows = swap_seq(away_rows)
-    out_keep, out_away = out_grad(da_turned, mine, came)
+    out_keep, out_away = out_grad(after(da_turned, up.sent), mine, came)
     out_came = swap_seq(out_away)
-    small = sum_everywhere(small)
-    steps = 4
-    each = head_cols // HDIM // steps
+    small = small + swap_seq(small)
     grads = ()
+    each = head_cols // HDIM // len(PLAN)
     ffn = [down, gate, up]
-    for step in range(steps):
-        if step >= 2:
-            for part in ffn:
-                part.receive()
-                part.send()
-            own_rows = after(own_rows, *[part.sent for part in ffn])
+    for number, relays in enumerate(PLAN):
+        for part in relays:
+            ffn[part].relay(*grads)
+        own_rows = after(own_rows, out_away, *[ffn[part].sent for part in relays], *grads)
         grads = attention_backward(
-            info, lengths, kept, own_rows, came_rows, step * each, each, grads
+            info, lengths, kept, own_rows, came_rows, number * each, each, grads
         )
-    sides = project_grad(info, gathered, grads, out_keep, out_came, orders, blocks)
+    sides = project_grad(info, gathered, grads, out_keep, out_came, turns, blocks)
     attn = [
-        Halving(sides[2 * index], sides[2 * index + 1], orders[index], shift) for index in range(3)
+        Halving(sides[2 * index], sides[2 * index + 1], turns[index], shift, None if index else small)
+        for index in range(3)
     ]
+    up.relay(*sides)
+    down.relay(*sides)
     for part in attn:
         part.send()
+    weights = (own_q, own_k, own_v)
     stream_away = stream_grad(info, after(grads, *sides), weights)
     grad_tokens = stream_grad(info, grads, weights, swap_seq(stream_away), dr1)
-    while ffn[0].step < bits:
-        for part in ffn:
-            part.receive()
-            part.send()
-    for part in ffn:
-        part.receive()
-    while attn[0].step < bits:
-        for part in attn:
-            part.receive()
-            part.send()
+    gate.relay()
+    up.relay()
+    down.relay()
     for part in attn:
-        part.receive()
+        part.relay()
+    Halving.last([gate, up])
+    for part in attn:
+        part.relay()
+    down.receive()
+    Halving.last(attn)
     summed_down, summed_gate, summed_up = (part.rest() for part in ffn)
     sums = [part.rest() for part in attn]
     summed_out = jnp.concatenate([total[:, head_cols:] for total in sums], axis=1)
+    small = attn[0].small.reshape(8, 2 * WIDE)[:, :width]
     squares = jnp.sum(small[2:5], axis=1)
     rms_values = jnp.sqrt(squares / (small[5, 0] * width))
     return (

time: 208 us -> 171 us (0.82)
  waiting for transfers between devices: 58.6 us -> 36.8 us
  Pallas kernels: 90.4 us -> 81.8 us
  starting transfers between devices: 38.1 us -> 31 us
    ppermute x28 -> x21, waiting for transfers between devices: 52.7 us -> 35.1 us  [swap_dp(): return lax.ppermute(value, 'dp', [(i, i ^ 1 << bit) for i in range(size)])]
    pallas_call x16 -> x15, Pallas kernels: 90.4 us -> 79.2 us  [call(): pl.pallas_call(kernel, in_specs=[pl.BlockSpec(memory_space=pltpu.SMEM)] *...]
    ppermute x28 -> x21, starting transfers between devices: 35.9 us -> 29 us  [swap_dp(): return lax.ppermute(value, 'dp', [(i, i ^ 1 << bit) for i in range(size)])]
    ppermute x9, waiting for transfers between devices: 5.85 us -> 1.67 us  [swap_seq(): return lax.ppermute(value, 'seq', [(0, 1), (1, 0)])]
    pallas_call x0 -> x1, Pallas kernels: none -> 2.55 us  [project_own(): pl.pallas_call(project_own_kernel, in_specs=[smem] * 2 + [vmem] * 3 + [pl...]
    unnamed x60 -> x66, local copies, waits for them, and re-layouts: 10.1 us -> 11.2 us
  transfers between devices with their start and end apart: 37 -> 30, of which waited for: 20 -> 10; matrix products, arithmetic and copies ran while one was open for 4% -> 4% of each run, Pallas kernels for 22% -> 30%
where the time goes in v2:
time: 171 us
  Pallas kernels  81.8 us (48%)
  waiting for transfers between devices  36.8 us (22%)
  starting transfers between devices  31 us (18%)
  local copies, waits for them, and re-layouts  14.3 us (8%)
  other arithmetic  4.89 us (3%)
  between operations  1.94 us (1%)
    pallas_call x15, Pallas kernels, call(): pl.pallas_call(kernel, in_specs=[pl.BlockSpec(memory_space=pltpu.SMEM)] *...  79.2 us
    ppermute x21, waiting for transfers between devices, swap_dp(): return lax.ppermute(value, 'dp', [(i, i ^ 1 << bit) for i in range(size)])  35.1 us
    ppermute x21, starting transfers between devices, swap_dp(): return lax.ppermute(value, 'dp', [(i, i ^ 1 << bit) for i in range(size)])  29 us
    unnamed x66, local copies, waits for them, and re-layouts  11.2 us
  transfers between devices with their start and end apart: 30, of which 10 were waited for; matrix products, arithmetic and copies ran while one was open for 4% of the time, Pallas kernels for 30%

profile of v2, /device:TPU:0, one launch (start us, length us, event | category | flops | bytes accessed | tf_op | source)
XLA Modules:
  0.0 170.7 jit_solution(2382370692301632871)
XLA Ops:
  8.7 2.6 %project_own.1 = (bf16[384,1024]{1,0:T(8,128)(2,1)S(1)}, bf16[384,1024]{1,0:T(8,128)(2,1)S(1)}, bf16[384,1024]{1,0:T(8,128)(2,1)S(1)}, bf16[1024,768]{1,0:T(8,12...) custom-call(s32[2]{0:T(128)S(1)} %pad_add_fusion.info_ref, ...), custom_call_target="tpu_custom_call" | custom-call | flops 4000000000 | bytes 8000000 | tf_op jit(solution)/shard_map/project_own/pallas_call | solution.py:136
  12.1 14.8 %attention_forward.1 = (bf16[384,1024]{1,0:T(8,128)(2,1)S(1)}, bf16[384,1024]{1,0:T(8,128)(2,1)S(1)}, bf16[384,1024]{1,0:T(8,128)(2,1)S(1)}, bf16[1024,768]{1,0:...) custom-call(s32[2]{0:T(128)S(1)} %pad_add_fusion.info_ref, ...), custom_call_target="tpu_custom_call", output_to_operand_aliasing={{0}: (2, {}), {1}: (3, {}), {2}: (4, {}), {3}: (5, {})} | custom-call | flops 300000000 | bytes 110755 | tf_op jit(solution)/shard_map/attention_forward/pallas_call | solution.py:30
  29.9 1.7 collective-permute-done.1.came_ref
  31.6 13.3 %ffn_forward.1 = (bf16[512,2560]{1,0:T(8,128)(2,1)S(1)}, bf16[512,2560]{1,0:T(8,128)(2,1)S(1)}, bf16[512,2560]{1,0:T(8,128)(2,1)S(1)}, bf16[512,768]{1,0:T(8,128...) custom-call(s32[2]{0:T(128)S(1)} %pad_add_fusion.info_ref, ...), custom_call_target="tpu_custom_call" | custom-call | flops 120795952 | bytes 283770 | tf_op jit(solution)/shard_map/ffn_forward/pallas_call | solution.py:30
  44.9 2.4 %weight_away.1 = bf16[768,1280]{1,0:T(8,128)(2,1)S(1)} custom-call(s32[2]{0:T(128)S(1)} %pad_add_fusion.info_ref, bf16[768,512]{1,0:T(8,128)(2,1)S(1)} %get-tuple-element.96.left_ref, bf16[512,2560]{1,0:T(8,128)(2,1)S(1)} %get-tuple-element.103.right_ref), custom_call_target="tpu_custom_call" | custom-call | flops 20132660 | bytes 39321 | tf_op jit(solution)/shard_map/weight_away/pallas_call | solution.py:30
  47.5 8.2 %swiglu_away.1 = (bf16[512,2560]{1,0:T(8,128)(2,1)S(1)}, bf16[512,2560]{1,0:T(8,128)(2,1)S(1)}, bf16[768,1280]{1,0:T(8,128)(2,1)S(1)}, bf16[768,1280]{1,0:T(8,128)(2,1)}) custom-call(s32[2]{0:T(128)S(1)} %pad_add_fusion.info_ref, bf16[512,768]{1,0:T(8,128)(2,1)S(1)} %get-tuple-element.105.dm_ref, bf16[2560,768]{1,0:T(8,128)(2,1)S(1)} %copy-done, ...), custom_call_target="tpu_custom_call" | custom-call | flops 60397976 | bytes 183500 | tf_op jit(solution)/shard_map/swiglu_away/pallas_call | solution.py:30
  56.2 2.4 %weight_mine.3 = (bf16[384,1280]{1,0:T(8,128)(2,1)S(1)}, bf16[384,1280]{1,0:T(8,128)(2,1)S(1)}) custom-call(s32[2]{0:T(128)S(1)} %pad_add_fusion.info_ref, bf16[768,512]{1,0:T(8,128)(2,1)S(1)} %get-tuple-element.96.left_ref, bf16[512,2560]{1,0:T(8,128)(2,1)S(1)} %get-tuple-element.103.right_ref, bf16[768,1280]{1,0:T(8,128)(2,1)S(1)} %collective-permute-done.2.rest_0_), custom_call_target="tpu_custom_call" | custom-call | flops 20132660 | bytes 39321 | tf_op jit(solution)/shard_map/weight_mine/pallas_call | solution.py:30
  58.6 3.0 %collective-permute-start.5 = (bf16[384,1280]{1,0:T(8,128)(2,1)S(1)}, bf16[384,1280]{1,0:T(8,128)(2,1)S(1)}, u32[]{:S(2)}, u32[]{:S(2)}) collective-permute-start(bf16[384,1280]{1,0:T(8,128)(2,1)S(1)} %get-tuple-element.104), channel_id=1, source_target_pairs={{0,8},{2,10},{4,12},{6,14},{8,0},{10,2},{12,4},{14,6},{16,24},{18,... | collective-permute-start | bytes 2949128 | tf_op jit(solution)/shard_map/ppermute | solution.py:629
  61.6 2.6 %swiglu_mine.1 = (bf16[512,2560]{1,0:T(8,128)(2,1)S(1)}, bf16[512,2560]{1,0:T(8,128)(2,1)S(1)}) custom-call(s32[2]{0:T(128)S(1)} %pad_add_fusion.info_ref, bf16[512,768]{1,0:T(8,128)(2,1)S(1)} %get-tuple-element.105.dm_ref, bf16[2560,768]{1,0:T(8,128)(2,1)S(1)} %copy-done, ...), custom_call_target="tpu_custom_call", output_to_operand_aliasing={{0}: (5, {}), {1}: (6, {})} | custom-call | flops 20132660 | bytes 104857 | tf_op jit(solution)/shard_map/swiglu_mine/pallas_call | solution.py:30
  64.3 2.4 %weight_mine.4 = (bf16[384,1280]{1,0:T(8,128)(2,1)S(1)}, bf16[384,1280]{1,0:T(8,128)(2,1)S(1)}) custom-call(s32[2]{0:T(128)S(1)} %pad_add_fusion.info_ref, bf16[768,512]{1,0:T(8,128)(2,1)S(1)} %get-tuple-element.118.hbt_ref.left_ref, bf16[512,2560]{1,0:T(8,128)(2,1)S(1)} %get-tuple-element.110.right_ref.dgt_ref, ...), custom_call_target="tpu_custom_call" | custom-call | flops 20132660 | bytes 39321 | tf_op jit(solution)/shard_map/weight_mine/pallas_call | solution.py:30
  68.3 7.7 %norm_one_back.1 = (f32[512,768]{1,0:T(8,128)S(1)}, bf16[768,512]{1,0:T(8,128)(2,1)S(1)}, bf16[384,512]{1,0:T(8,128)(2,1)S(1)}, bf16[384,512]{1,0:T(8,128)(2,1)S(1)}, f32[16,512]{1,0:T(8,128)S(1)}) custom-call(s32[2]{0:T(128)S(1)} %pad_add_fusion.info_ref, bf16[512,2560]{1,0:T(8,128)(2,1)S(1)} %get-tuple-element.110.right_ref.dgt_ref, ...), custom_call_target="tpu_custom_call" | custom-call | flops 80530640 | bytes 63569 | tf_op jit(solution)/shard_map/norm_one_back/pallas_call | solution.py:30
  76.6 2.6 %weight_mine.5 = (bf16[384,1280]{1,0:T(8,128)(2,1)S(1)}, bf16[384,1280]{1,0:T(8,128)(2,1)S(1)}) custom-call(s32[2]{0:T(128)S(1)} %pad_add_fusion.info_ref, bf16[768,512]{1,0:T(8,128)(2,1)S(1)} %get-tuple-element.118.hbt_ref.left_ref, bf16[512,2560]{1,0:T(8,128)(2,1)S(1)} %get-tuple-element.111.dup_ref.right_ref, ...), custom_call_target="tpu_custom_call" | custom-call | flops 20132660 | bytes 39321 | tf_op jit(solution)/shard_map/weight_mine/pallas_call | solution.py:30
  79.2 1.6 collective-permute-start.23
  81.9 1.8 %collective-permute-done.5 = bf16[384,1280]{1,0:T(8,128)(2,1)S(1)} collective-permute-done((bf16[384,1280]{1,0:T(8,128)(2,1)S(1)}, bf16[384,1280]{1,0:T(8,128)(2,1)S(1)}, u32[]{:S(2)}, u32[]{:S(2)}) %collective-permute-start.5) | collective-permute-done | bytes 983072 | tf_op jit(solution)/shard_map/ppermute | solution.py:629
  84.0 2.8 %collective-permute-start.27 = (bf16[192,1280]{1,0:T(8,128)(2,1)S(1)}, bf16[192,1280]{1,0:T(8,128)(2,1)S(1)}, u32[]{:S(2)}, u32[]{:S(2)}) collective-permute-start(bf16[192,1280]{1,0:T(8,128)(2,1)S(1)} %get-tuple-element.161), channel_id=1, source_target_pairs={{0,16},{2,18},{4,20},{6,22},{8,24},{10,26},{12,28},{14,30},{16,0},... | collective-permute-start | bytes 1474568 | tf_op jit(solution)/shard_map/ppermute | solution.py:629
  86.8 6.4 %attention_backward.2 = (bf16[384,1024]{1,0:T(8,128)(2,1)S(1)}, bf16[384,1024]{1,0:T(8,128)(2,1)S(1)}, bf16[384,1024]{1,0:T(8,128)(2,1)S(1)}) custom-call(s32[2]{0:T(128)S(1)} %pad_add_fusion.info_ref, s32[4]{0:T(128)S(1)} %bitcast.11, bf16[384,1024]{1,0:T(8,128)(2,1)S(1)} %get-tuple-element.91.q_ref, bf16[384,1024]{1,0:T(8,128)(2,1)S(1)} %get-tuple-element.92.k_ref, ...), custom_call_target="tpu_custom_call" | custom-call | flops 240000000 | bytes 47185 | tf_op jit(solution)/shard_map/attention_backward/pallas_call | solution.py:30
  93.5 1.7 collective-permute-start.21
  95.2 6.7 %attention_backward.3 = (bf16[384,1024]{1,0:T(8,128)(2,1)S(1)}, bf16[384,1024]{1,0:T(8,128)(2,1)S(1)}, bf16[384,1024]{1,0:T(8,128)(2,1)S(1)}) custom-call(s32[2]{0:T(128)S(1)} %pad_add_fusion.info_ref, s32[4]{0:T(128)S(1)} %bitcast.12, bf16[384,1024]{1,0:T(8,128)(2,1)S(1)} %get-tuple-element.91.q_ref, ...), custom_call_target="tpu_custom_call", output_to_operand_aliasing={{0}: (11, {}), {1}: (12, {}), {2}: (13, {})} | custom-call | flops 240000000 | bytes 47185 | tf_op jit(solution)/shard_map/attention_backward/pallas_call | solution.py:30
  101.9 3.8 %project_grad.1 = (bf16[384,512]{1,0:T(8,128)(2,1)S(1)}, bf16[384,512]{1,0:T(8,128)(2,1)S(1)}, bf16[384,512]{1,0:T(8,128)(2,1)S(1)}, bf16[384,512]{1,0:T(8,128)(...) custom-call(s32[2]{0:T(128)S(1)} %pad_add_fusion.info_ref, bf16[1024,768]{1,0:T(8,128)(2,1)S(1)} %copy-done.6, ...), custom_call_target="tpu_custom_call" | custom-call | flops 36238784 | bytes 47185 | tf_op jit(solution)/shard_map/project_grad/pallas_call | solution.py:30
  105.6 1.6 collective-permute-start.14
  109.5 1.9 %stream_grad.2 = bf16[768,512]{1,0:T(8,128)(2,1)S(1)} custom-call(s32[2]{0:T(128)S(1)} %pad_add_fusion.info_ref, bf16[384,1024]{1,0:T(8,128)(2,1)S(1)} %get-tuple-element.146.dq_ref, bf16[384,1024]{1,0:T(8,128)(2,1)S(1)} %get-tuple-element.147.dk_ref, bf16[384,1024]{1,0:T(8,128)(2,1)S(1)} %get-tuple-element.148.dv_ref, ...), custom_call_target="tpu_custom_call" | custom-call | flops 18119392 | bytes 15728 | tf_op jit(solution)/shard_map/stream_grad/pallas_call | solution.py:30
  111.4 4.0 %collective-permute-done.14 = bf16[384,512]{1,0:T(8,128)(2,1)S(1)} collective-permute-done((bf16[384,512]{1,0:T(8,128)(2,1)S(1)}, bf16[384,512]{1,0:T(8,128)(2,1)S(1)}, u32[]{:S(2)}, u32[]{:S(2)}) %collective-permute-start.14) | collective-permute-done | bytes 393248 | tf_op jit(solution)/shard_map/ppermute | solution.py:629
  117.0 6.7 %collective-permute-done.17 = bf16[384,512]{1,0:T(8,128)(2,1)S(1)} collective-permute-done((bf16[384,512]{1,0:T(8,128)(2,1)S(1)}, bf16[384,512]{1,0:T(8,128)(2,1)S(1)}, u32[]{:S(2)}, u32[]{:S(2)}) %collective-permute-start.17) | collective-permute-done | bytes 393248 | tf_op jit(solution)/shard_map/ppermute | solution.py:629
  125.6 4.0 %collective-permute-done.24 = bf16[192,1280]{1,0:T(8,128)(2,1)S(1)} collective-permute-done((bf16[192,1280]{1,0:T(8,128)(2,1)S(1)}, bf16[192,1280]{1,0:T(8,128)(2,1)S(1)}, u32[]{:S(2)}, u32[]{:S(2)}) %collective-permute-start.24) | collective-permute-done | bytes 491552 | tf_op jit(solution)/shard_map/ppermute | solution.py:629
  129.7 2.1 %collective-permute-start.28 = (bf16[96,1280]{1,0:T(8,128)(2,1)S(1)}, bf16[96,1280]{1,0:T(8,128)(2,1)S(1)}, u32[]{:S(2)}, u32[]{:S(2)}) collective-permute-start(bf16[96,1280]{1,0:T(8,128)(2,1)S(1)} %get-tuple-element.167), channel_id=1, source_target_pairs={{0,4},{2,6},{4,0},{6,2},{8,12},{10,14},{12,8},{14,10},{16,20},{18,... | collective-permute-start | bytes 737288 | tf_op jit(solution)/shard_map/ppermute | solution.py:629
  133.7 4.3 %collective-permute-done.12 = bf16[224,512]{1,0:T(8,128)(2,1)S(1)} collective-permute-done((bf16[224,512]{1,0:T(8,128)(2,1)S(1)}, bf16[224,512]{1,0:T(8,128)(2,1)S(1)}, u32[]{:S(2)}, u32[]{:S(2)}) %collective-permute-start.12) | collective-permute-done | bytes 229408 | tf_op jit(solution)/shard_map/ppermute | solution.py:629
  138.1 1.8 %collective-permute-start.16 = (bf16[96,512]{1,0:T(8,128)(2,1)S(1)}, bf16[96,512]{1,0:T(8,128)(2,1)S(1)}, u32[]{:S(2)}, u32[]{:S(2)}) collective-permute-start(bf16[96,512]{1,0:T(8,128)(2,1)S(1)} %get-tuple-element.185), channel_id=1, source_target_pairs={{0,2},{2,0},{4,6},{6,4},{8,10},{10,8},{12,14},{14,12},{16,18},{18,... | collective-permute-start | bytes 294920 | tf_op jit(solution)/shard_map/ppermute | solution.py:629
  139.9 3.1 %collective-permute-done.28 = bf16[96,1280]{1,0:T(8,128)(2,1)S(1)} collective-permute-done((bf16[96,1280]{1,0:T(8,128)(2,1)S(1)}, bf16[96,1280]{1,0:T(8,128)(2,1)S(1)}, u32[]{:S(2)}, u32[]{:S(2)}) %collective-permute-start.28) | collective-permute-done | bytes 245792 | tf_op jit(solution)/shard_map/ppermute | solution.py:629
  147.2 2.6 %collective-permute-done.13 = bf16[128,512]{1,0:T(8,128)(2,1)S(1)} collective-permute-done((bf16[128,512]{1,0:T(8,128)(2,1)S(1)}, bf16[128,512]{1,0:T(8,128)(2,1)S(1)}, u32[]{:S(2)}, u32[]{:S(2)}) %collective-permute-start.13) | collective-permute-done | bytes 131104 | tf_op jit(solution)/shard_map/ppermute | solution.py:629
  150.5 2.4 %collective-permute-start.20 = (bf16[176,512]{1,0:T(8,128)(2,1)S(1)}, bf16[176,512]{1,0:T(8,128)(2,1)S(1)}, u32[]{:S(2)}, u32[]{:S(2)}) collective-permute-start(bf16[176,512]{1,0:T(8,128)(2,1)S(1)} %fusion.2), channel_id=1, source_target_pairs={{0,16},{2,18},{4,20},{6,22},{8,24},{10,26},{12,28},{14,30},{16,0},... | collective-permute-start | bytes 540680 | tf_op jit(solution)/shard_map/ppermute | solution.py:629
  152.9 3.1 %stream_grad.3 = bf16[512,768]{1,0:T(8,128)(2,1)} custom-call(s32[2]{0:T(128)S(1)} %pad_add_fusion.info_ref, bf16[384,1024]{1,0:T(8,128)(2,1)S(1)} %get-tuple-element.146.dq_ref, bf16[384,1024]{1,0:T(8,128)(2,1)S(1)} %get-tuple-element.147.dk_ref, bf16[384,1024]{1,0:T(8,128)(2,1)S(1)} %get-tuple-element.148.dv_ref, ...), custom_call_target="tpu_custom_call" | custom-call | flops 18119392 | bytes 15728 | tf_op jit(solution)/shard_map/stream_grad/pallas_call | solution.py:30
  156.8 7.9 %collective-permute-done.20 = bf16[176,512]{1,0:T(8,128)(2,1)S(1)} collective-permute-done((bf16[176,512]{1,0:T(8,128)(2,1)S(1)}, bf16[176,512]{1,0:T(8,128)(2,1)S(1)}, u32[]{:S(2)}, u32[]{:S(2)}) %collective-permute-start.20) | collective-permute-done | bytes 180256 | tf_op jit(solution)/shard_map/ppermute | solution.py:629
  (156 shorter events, 34.9 us)
Async XLA Ops:
  0.6 11.4 %collective-permute-start = (bf16[512,768]{1,0:T(8,128)(2,1)}, bf16[512,768]{1,0:T(8,128)(2,1)S(1)}, u32[]{:S(2)}, u32[]{:S(2)}) collective-permute-start(bf16[512,768]{1,0:T(8,128)(2,1)} %x_ref.3), channel_id=1, source_target_pairs={{0,1},{1,0},{2,3},{3,2},{4,5},{5,4},{6,7},{7,6},{8,9},{9,8},{10,11... | collective-permute-start | bytes 2359304 | tf_op jit(solution)/shard_map/ppermute | solution.py:624
  8.7 22.9 %copy-start.1 = (bf16[768,2560]{1,0:T(8,128)(2,1)S(1)}, bf16[768,2560]{1,0:T(8,128)(2,1)}, u32[]{:S(2)}) copy-start(bf16[768,2560]{1,0:T(8,128)(2,1)} %wg_ref.3) | copy-start | bytes 11796484
  8.7 22.9 %copy-start.2 = (bf16[768,2560]{1,0:T(8,128)(2,1)S(1)}, bf16[768,2560]{1,0:T(8,128)(2,1)}, u32[]{:S(2)}) copy-start(bf16[768,2560]{1,0:T(8,128)(2,1)} %wu_ref.3) | copy-start | bytes 11796484
  29.9 1.7 %collective-permute-start.1 = (bf16[384,512]{1,0:T(8,128)(2,1)S(1)}, bf16[384,512]{1,0:T(8,128)(2,1)S(1)}, u32[]{:S(2)}, u32[]{:S(2)}) collective-permute-start(bf16[384,512]{1,0:T(8,128)(2,1)S(1)} %get-tuple-element.89), channel_id=1, source_target_pairs={{0,1},{1,0},{2,3},{3,2},{4,5},{5,4},{6,7},{7,6},{8,9},{9,8},{10,11... | collective-permute-start | bytes 1179656 | tf_op jit(solution)/shard_map/ppermute | solution.py:624
  47.3 8.9 %collective-permute-start.2 = (bf16[768,1280]{1,0:T(8,128)(2,1)S(1)}, bf16[768,1280]{1,0:T(8,128)(2,1)S(1)}, u32[]{:S(2)}, u32[]{:S(2)}) collective-permute-start(bf16[768,1280]{1,0:T(8,128)(2,1)S(1)} %weight_away.1), channel_id=1, source_target_pairs={{0,1},{1,0},{2,3},{3,2},{4,5},{5,4},{6,7},{7,6},{8,9},{9,8},{10,11... | collective-permute-start | bytes 5898248 | tf_op jit(solution)/shard_map/ppermute | solution.py:624
  55.7 8.5 %collective-permute-start.3 = (bf16[768,1280]{1,0:T(8,128)(2,1)S(1)}, bf16[768,1280]{1,0:T(8,128)(2,1)S(1)}, u32[]{:S(2)}, u32[]{:S(2)}) collective-permute-start(bf16[768,1280]{1,0:T(8,128)(2,1)S(1)} %get-tuple-element.102), channel_id=1, source_target_pairs={{0,1},{1,0},{2,3},{3,2},{4,5},{5,4},{6,7},{7,6},{8,9},{9,8},{10,11... | collective-permute-start | bytes 5898248 | tf_op jit(solution)/shard_map/ppermute | solution.py:624
  56.1 20.5 %collective-permute-start.4 = (bf16[768,1280]{1,0:T(8,128)(2,1)}, bf16[768,1280]{1,0:T(8,128)(2,1)S(1)}, u32[]{:S(2)}, u32[]{:S(2)}) collective-permute-start(bf16[768,1280]{1,0:T(8,128)(2,1)} %get-tuple-element.119), channel_id=1, source_target_pairs={{0,1},{1,0},{2,3},{3,2},{4,5},{5,4},{6,7},{7,6},{8,9},{9,8},{10,11... | collective-permute-start | bytes 5898248 | tf_op jit(solution)/shard_map/ppermute | solution.py:624
  58.6 25.1 %collective-permute-start.5 = (bf16[384,1280]{1,0:T(8,128)(2,1)S(1)}, bf16[384,1280]{1,0:T(8,128)(2,1)S(1)}, u32[]{:S(2)}, u32[]{:S(2)}) collective-permute-start(bf16[384,1280]{1,0:T(8,128)(2,1)S(1)} %get-tuple-element.104), channel_id=1, source_target_pairs={{0,8},{2,10},{4,12},{6,14},{8,0},{10,2},{12,4},{14,6},{16,24},{18,... | collective-permute-start | bytes 2949128 | tf_op jit(solution)/shard_map/ppermute | solution.py:629
  66.7 26.5 %collective-permute-start.7 = (bf16[384,1280]{1,0:T(8,128)(2,1)S(1)}, bf16[384,1280]{1,0:T(8,128)(2,1)S(1)}, u32[]{:S(2)}, u32[]{:S(2)}) collective-permute-start(bf16[384,1280]{1,0:T(8,128)(2,1)S(1)} %get-tuple-element.109), channel_id=1, source_target_pairs={{0,2},{2,0},{4,6},{6,4},{8,10},{10,8},{12,14},{14,12},{16,18},{18,... | collective-permute-start | bytes 2949128 | tf_op jit(solution)/shard_map/ppermute | solution.py:629
  76.0 5.8 %collective-permute-start.10 = (f32[16,512]{1,0:T(8,128)S(1)}, f32[16,512]{1,0:T(8,128)S(1)}, u32[]{:S(2)}, u32[]{:S(2)}) collective-permute-start(f32[16,512]{1,0:T(8,128)S(1)} %get-tuple-element.150), channel_id=1, source_target_pairs={{0,1},{1,0},{2,3},{3,2},{4,5},{5,4},{6,7},{7,6},{8,9},{9,8},{10,11... | collective-permute-start | bytes 98312 | tf_op jit(solution)/shard_map/ppermute | solution.py:624
  76.1 10.7 %collective-permute-start.6 = (bf16[384,512]{1,0:T(8,128)(2,1)S(1)}, bf16[384,512]{1,0:T(8,128)(2,1)S(1)}, u32[]{:S(2)}, u32[]{:S(2)}) collective-permute-start(bf16[384,512]{1,0:T(8,128)(2,1)S(1)} %get-tuple-element.117), channel_id=1, source_target_pairs={{0,1},{1,0},{2,3},{3,2},{4,5},{5,4},{6,7},{7,6},{8,9},{9,8},{10,11... | collective-permute-start | bytes 1179656 | tf_op jit(solution)/shard_map/ppermute | solution.py:624
  79.2 28.5 %collective-permute-start.23 = (bf16[384,1280]{1,0:T(8,128)(2,1)S(1)}, bf16[384,1280]{1,0:T(8,128)(2,1)S(1)}, u32[]{:S(2)}, u32[]{:S(2)}) collective-permute-start(bf16[384,1280]{1,0:T(8,128)(2,1)S(1)} %get-tuple-element.120), channel_id=1, source_target_pairs={{0,4},{2,6},{4,0},{6,2},{8,12},{10,14},{12,8},{14,10},{16,20},{18,... | collective-permute-start | bytes 2949128 | tf_op jit(solution)/shard_map/ppermute | solution.py:629
  81.8 20.0 %collective-permute-start.8 = (bf16[768,384]{1,0:T(8,128)(2,1)S(1)}, bf16[768,384]{1,0:T(8,128)(2,1)S(1)}, u32[]{:S(2)}, u32[]{:S(2)}) collective-permute-start(bf16[768,384]{1,0:T(8,128)(2,1)S(1)} %get-tuple-element.122), channel_id=1, source_target_pairs={{0,1},{1,0},{2,3},{3,2},{4,5},{5,4},{6,7},{7,6},{8,9},{9,8},{10,11... | collective-permute-start | bytes 1769480 | tf_op jit(solution)/shard_map/ppermute | solution.py:624
  84.0 40.1 %collective-permute-start.27 = (bf16[192,1280]{1,0:T(8,128)(2,1)S(1)}, bf16[192,1280]{1,0:T(8,128)(2,1)S(1)}, u32[]{:S(2)}, u32[]{:S(2)}) collective-permute-start(bf16[192,1280]{1,0:T(8,128)(2,1)S(1)} %get-tuple-element.161), channel_id=1, source_target_pairs={{0,16},{2,18},{4,20},{6,22},{8,24},{10,26},{12,28},{14,30},{16,0},... | collective-permute-start | bytes 1474568 | tf_op jit(solution)/shard_map/ppermute | solution.py:629
  93.5 36.2 %collective-permute-start.21 = (bf16[192,1280]{1,0:T(8,128)(2,1)S(1)}, bf16[192,1280]{1,0:T(8,128)(2,1)S(1)}, u32[]{:S(2)}, u32[]{:S(2)}) collective-permute-start(bf16[192,1280]{1,0:T(8,128)(2,1)S(1)} %get-tuple-element.163), channel_id=1, source_target_pairs={{0,8},{2,10},{4,12},{6,14},{8,0},{10,2},{12,4},{14,6},{16,24},{18,... | collective-permute-start | bytes 1474568 | tf_op jit(solution)/shard_map/ppermute | solution.py:629
  105.6 9.8 %collective-permute-start.14 = (bf16[384,512]{1,0:T(8,128)(2,1)S(1)}, bf16[384,512]{1,0:T(8,128)(2,1)S(1)}, u32[]{:S(2)}, u32[]{:S(2)}) collective-permute-start(bf16[384,512]{1,0:T(8,128)(2,1)S(1)} %get-tuple-element.143), channel_id=1, source_target_pairs={{0,4},{2,6},{4,0},{6,2},{8,12},{10,14},{12,8},{14,10},{16,20},{18,... | collective-permute-start | bytes 1179656 | tf_op jit(solution)/shard_map/ppermute | solution.py:629
  107.2 16.5 %collective-permute-start.17 = (bf16[384,512]{1,0:T(8,128)(2,1)S(1)}, bf16[384,512]{1,0:T(8,128)(2,1)S(1)}, u32[]{:S(2)}, u32[]{:S(2)}) collective-permute-start(bf16[384,512]{1,0:T(8,128)(2,1)S(1)} %get-tuple-element.145), channel_id=1, source_target_pairs={{0,8},{2,10},{4,12},{6,14},{8,0},{10,2},{12,4},{14,6},{16,24},{18,... | collective-permute-start | bytes 1179656 | tf_op jit(solution)/shard_map/ppermute | solution.py:629
  108.0 15.8 %collective-permute-start.11 = (bf16[416,512]{1,0:T(8,128)(2,1)S(1)}, bf16[416,512]{1,0:T(8,128)(2,1)S(1)}, u32[]{:S(2)}, u32[]{:S(2)}) collective-permute-start(bf16[416,512]{1,0:T(8,128)(2,1)S(1)} %pad_maximum_fusion), channel_id=1, source_target_pairs={{0,2},{2,0},{4,6},{6,4},{8,10},{10,8},{12,14},{14,12},{16,18},{18,... | collective-permute-start | bytes 1277960 | tf_op jit(solution)/shard_map/ppermute | solution.py:629
  115.4 14.2 %collective-permute-start.24 = (bf16[192,1280]{1,0:T(8,128)(2,1)S(1)}, bf16[192,1280]{1,0:T(8,128)(2,1)S(1)}, u32[]{:S(2)}, u32[]{:S(2)}) collective-permute-start(bf16[192,1280]{1,0:T(8,128)(2,1)S(1)} %get-tuple-element.165), channel_id=1, source_target_pairs={{0,2},{2,0},{4,6},{6,4},{8,10},{10,8},{12,14},{14,12},{16,18},{18,... | collective-permute-start | bytes 1474568 | tf_op jit(solution)/shard_map/ppermute | solution.py:629
  123.7 29.3 %collective-permute-start.9 = (bf16[768,512]{1,0:T(8,128)(2,1)S(1)}, bf16[768,512]{1,0:T(8,128)(2,1)S(1)}, u32[]{:S(2)}, u32[]{:S(2)}) collective-permute-start(bf16[768,512]{1,0:T(8,128)(2,1)S(1)} %stream_grad.2), channel_id=1, source_target_pairs={{0,1},{1,0},{2,3},{3,2},{4,5},{5,4},{6,7},{7,6},{8,9},{9,8},{10,11... | collective-permute-start | bytes 2359304 | tf_op jit(solution)/shard_map/ppermute | solution.py:624
  123.8 8.2 %collective-permute-start.15 = (bf16[192,512]{1,0:T(8,128)(2,1)S(1)}, bf16[192,512]{1,0:T(8,128)(2,1)S(1)}, u32[]{:S(2)}, u32[]{:S(2)}) collective-permute-start(bf16[192,512]{1,0:T(8,128)(2,1)S(1)} %get-tuple-element.177), channel_id=1, source_target_pairs={{0,8},{2,10},{4,12},{6,14},{8,0},{10,2},{12,4},{14,6},{16,24},{18,... | collective-permute-start | bytes 589832 | tf_op jit(solution)/shard_map/ppermute | solution.py:629
  124.1 9.6 %collective-permute-start.18 = (bf16[192,512]{1,0:T(8,128)(2,1)S(1)}, bf16[192,512]{1,0:T(8,128)(2,1)S(1)}, u32[]{:S(2)}, u32[]{:S(2)}) collective-permute-start(bf16[192,512]{1,0:T(8,128)(2,1)S(1)} %get-tuple-element.175), channel_id=1, source_target_pairs={{0,2},{2,0},{4,6},{6,4},{8,10},{10,8},{12,14},{14,12},{16,18},{18,... | collective-permute-start | bytes 589832 | tf_op jit(solution)/shard_map/ppermute | solution.py:629
  129.6 8.5 %collective-permute-start.12 = (bf16[224,512]{1,0:T(8,128)(2,1)S(1)}, bf16[224,512]{1,0:T(8,128)(2,1)S(1)}, u32[]{:S(2)}, u32[]{:S(2)}) collective-permute-start(bf16[224,512]{1,0:T(8,128)(2,1)S(1)} %pad_maximum_fusion.2), channel_id=1, source_target_pairs={{0,4},{2,6},{4,0},{6,2},{8,12},{10,14},{12,8},{14,10},{16,20},{18,... | collective-permute-start | bytes 688136 | tf_op jit(solution)/shard_map/ppermute | solution.py:629
  129.7 13.3 %collective-permute-start.28 = (bf16[96,1280]{1,0:T(8,128)(2,1)S(1)}, bf16[96,1280]{1,0:T(8,128)(2,1)S(1)}, u32[]{:S(2)}, u32[]{:S(2)}) collective-permute-start(bf16[96,1280]{1,0:T(8,128)(2,1)S(1)} %get-tuple-element.167), channel_id=1, source_target_pairs={{0,4},{2,6},{4,0},{6,2},{8,12},{10,14},{12,8},{14,10},{16,20},{18,... | collective-permute-start | bytes 737288 | tf_op jit(solution)/shard_map/ppermute | solution.py:629
  132.0 11.4 %collective-permute-start.25 = (bf16[96,1280]{1,0:T(8,128)(2,1)S(1)}, bf16[96,1280]{1,0:T(8,128)(2,1)S(1)}, u32[]{:S(2)}, u32[]{:S(2)}) collective-permute-start(bf16[96,1280]{1,0:T(8,128)(2,1)S(1)} %get-tuple-element.171), channel_id=1, source_target_pairs={{0,8},{2,10},{4,12},{6,14},{8,0},{10,2},{12,4},{14,6},{16,24},{18,... | collective-permute-start | bytes 737288 | tf_op jit(solution)/shard_map/ppermute | solution.py:629
  133.6 12.0 %collective-permute-start.22 = (bf16[96,1280]{1,0:T(8,128)(2,1)S(1)}, bf16[96,1280]{1,0:T(8,128)(2,1)S(1)}, u32[]{:S(2)}, u32[]{:S(2)}) collective-permute-start(bf16[96,1280]{1,0:T(8,128)(2,1)S(1)} %get-tuple-element.169), channel_id=1, source_target_pairs={{0,4},{2,6},{4,0},{6,2},{8,12},{10,14},{12,8},{14,10},{16,20},{18,... | collective-permute-start | bytes 737288 | tf_op jit(solution)/shard_map/ppermute | solution.py:629
  138.1 12.3 %collective-permute-start.16 = (bf16[96,512]{1,0:T(8,128)(2,1)S(1)}, bf16[96,512]{1,0:T(8,128)(2,1)S(1)}, u32[]{:S(2)}, u32[]{:S(2)}) collective-permute-start(bf16[96,512]{1,0:T(8,128)(2,1)S(1)} %get-tuple-element.185), channel_id=1, source_target_pairs={{0,2},{2,0},{4,6},{6,4},{8,10},{10,8},{12,14},{14,12},{16,18},{18,... | collective-permute-start | bytes 294920 | tf_op jit(solution)/shard_map/ppermute | solution.py:629
  143.0 7.4 %collective-permute-start.19 = (bf16[96,512]{1,0:T(8,128)(2,1)S(1)}, bf16[96,512]{1,0:T(8,128)(2,1)S(1)}, u32[]{:S(2)}, u32[]{:S(2)}) collective-permute-start(bf16[96,512]{1,0:T(8,128)(2,1)S(1)} %get-tuple-element.183), channel_id=1, source_target_pairs={{0,4},{2,6},{4,0},{6,2},{8,12},{10,14},{12,8},{14,10},{16,20},{18,... | collective-permute-start | bytes 294920 | tf_op jit(solution)/shard_map/ppermute | solution.py:629
  143.4 6.4 %collective-permute-start.13 = (bf16[128,512]{1,0:T(8,128)(2,1)S(1)}, bf16[128,512]{1,0:T(8,128)(2,1)S(1)}, u32[]{:S(2)}, u32[]{:S(2)}) collective-permute-start(bf16[128,512]{1,0:T(8,128)(2,1)S(1)} %pad_maximum_fusion.3), channel_id=1, source_target_pairs={{0,8},{2,10},{4,12},{6,14},{8,0},{10,2},{12,4},{14,6},{16,24},{18,... | collective-permute-start | bytes 393224 | tf_op jit(solution)/shard_map/ppermute | solution.py:629
  145.6 10.4 %collective-permute-start.29 = (bf16[48,1280]{1,0:T(8,128)(2,1)S(1)}, bf16[48,1280]{1,0:T(8,128)(2,1)S(1)}, u32[]{:S(2)}, u32[]{:S(2)}) collective-permute-start(bf16[48,1280]{1,0:T(8,128)(2,1)S(1)} %add_convert_fusion.18), channel_id=1, source_target_pairs={{0,2},{2,0},{4,6},{6,4},{8,10},{10,8},{12,14},{14,12},{16,18},{18,... | collective-permute-start | bytes 368648 | tf_op jit(solution)/shard_map/ppermute | solution.py:629
  149.8 20.0 %collective-permute-start.26 = (bf16[96,1280]{1,0:T(8,128)(2,1)S(1)}, bf16[96,1280]{1,0:T(8,128)(2,1)S(1)}, u32[]{:S(2)}, u32[]{:S(2)}) collective-permute-start(bf16[96,1280]{1,0:T(8,128)(2,1)S(1)} %pad_maximum_fusion.1), channel_id=1, source_target_pairs={{0,16},{2,18},{4,20},{6,22},{8,24},{10,26},{12,28},{14,30},{16,0},... | collective-permute-start | bytes 737288 | tf_op jit(solution)/shard_map/ppermute | solution.py:629
  150.5 14.2 %collective-permute-start.20 = (bf16[176,512]{1,0:T(8,128)(2,1)S(1)}, bf16[176,512]{1,0:T(8,128)(2,1)S(1)}, u32[]{:S(2)}, u32[]{:S(2)}) collective-permute-start(bf16[176,512]{1,0:T(8,128)(2,1)S(1)} %fusion.2), channel_id=1, source_target_pairs={{0,16},{2,18},{4,20},{6,22},{8,24},{10,26},{12,28},{14,30},{16,0},... | collective-permute-start | bytes 540680 | tf_op jit(solution)/shard_map/ppermute | solution.py:629
  (31 other events, 210.9 us)

commit v3 on v2

--- a/solution.py
+++ b/solution.py
@@ -20,9 +20,11 @@
 WIDE = 512
 ROWS = 64
 SPANS = 4
+PAIR = 2
 PLAN = ((0,), (1,))
 MIB = 1 << 20
 EASE = 50
+ROOM = 8
 
 
 def call(kernel, name, scalars, arrays, out_shape, flops, scratch=(), room=16, aliases=None):
@@ -108,21 +110,29 @@
 
 
 def project_own_kernel(
-    info_ref, len_ref, x_ref, cos_ref, sin_ref, wq_ref, wk_ref, wv_ref,
-    q_ref, k_ref, v_ref, all_ref, turned_ref, cq_ref, ck_ref, cv_ref, sems,
+    info_ref, from_len_ref, from_x_ref, from_cos_ref, from_sin_ref, wq_ref, wk_ref, wv_ref,
+    q_ref, k_ref, v_ref, all_ref, turned_ref, cq_ref, ck_ref, cv_ref,
+    len_ref, x_ref, cos_ref, sin_ref, sems,
 ):
     cols, pack = q_ref.shape
     rows = x_ref.shape[0]
     side = info_ref[0]
-    copies = []
-    for index, (w_ref, c_ref) in enumerate(((wq_ref, cq_ref), (wk_ref, ck_ref), (wv_ref, cv_ref))):
-        copies.append(pltpu.make_async_copy(w_ref.at[:, at(side * cols, cols)], c_ref, sems.at[index]))
-        copies[-1].start()
-    _, openings = block_facts(len_ref, pack // SPANS)
+    pairs = [(from_x_ref, x_ref)]
+    pairs += [
+        (w_ref.at[:, at(side * cols, cols)], c_ref)
+        for w_ref, c_ref in ((wq_ref, cq_ref), (wk_ref, ck_ref), (wv_ref, cv_ref))
+    ]
+    pairs += [(from_cos_ref, cos_ref), (from_sin_ref, sin_ref), (from_len_ref, len_ref)]
+    copies = [pltpu.make_async_copy(*pair, sems.at[index]) for index, pair in enumerate(pairs)]
+    for copy in copies:
+        copy.start()
+    for index, c_ref in enumerate((cq_ref, ck_ref, cv_ref)):
+        copies[1 + index].wait()
+        turned_ref[index * cols : (index + 1) * cols, :] = c_ref[...].T
+    for index in (0, 4, 5, 6):
+        copies[index].wait()
+    _, openings = block_facts(len_ref.at[0], pack // SPANS)
     all_ref[at(side * rows, rows), :] = x_ref[...]
-    for index, c_ref in enumerate((cq_ref, ck_ref, cv_ref)):
-        copies[index].wait()
-        turned_ref[index * cols : (index + 1) * cols, :] = c_ref[...].T
     weights = [turned_ref[index * cols : (index + 1) * cols, :] for index in range(3)]
     project((q_ref, k_ref, v_ref), weights, x_ref[...], openings, cos_ref, sin_ref, side * rows)
 
@@ -132,19 +142,22 @@
     pack = 2 * rows
     cols = weights[0].shape[1] // 2
     vmem = pl.BlockSpec(memory_space=pltpu.VMEM)
-    smem = pl.BlockSpec(memory_space=pltpu.SMEM)
+    far = [pltpu.with_memory_space_constraint(jnp.asarray(value), pltpu.HBM) for value in (lengths, own, *rope_tables(pack), *weights)]
     return pl.pallas_call(
         project_own_kernel,
-        in_specs=[smem] * 2 + [vmem] * 3 + [pl.BlockSpec(memory_space=pltpu.HBM)] * 3,
+        in_specs=[pl.BlockSpec(memory_space=pltpu.SMEM)] + [pl.BlockSpec(memory_space=pltpu.HBM)] * 7,
         out_specs=[vmem] * 8,
         out_shape=[shape(BF16, cols, pack)] * 3
         + [shape(BF16, pack, width), shape(BF16, 3 * cols, width)]
         + [shape(BF16, width, cols)] * 3,
-        scratch_shapes=[pltpu.SemaphoreType.DMA((3,))],
+        scratch_shapes=[
+            pltpu.SMEM(lengths.shape, jnp.int32), pltpu.VMEM(own.shape, BF16),
+            pltpu.VMEM((HALF, pack), F32), pltpu.VMEM((HALF, pack), F32), pltpu.SemaphoreType.DMA((7,)),
+        ],
         cost_estimate=pl.CostEstimate(flops=4_000_000_000, bytes_accessed=8_000_000, transcendentals=0),
         compiler_params=pltpu.CompilerParams(vmem_limit_bytes=8 * MIB),
         name="project_own",
-    )(info, lengths, own, *rope_tables(pack), *weights)
+    )(info, *far)
 
 
 def attention_forward_kernel(
@@ -162,34 +175,47 @@
     project((q_ref, k_ref, v_ref), weights, oth_ref[...], openings, cos_ref, sin_ref, (1 - side) * rows)
     below = causal(block)
 
-    @pl.loop(0, heads)
-    def _(head):
-        here = at(head * HDIM, HDIM)
-        keys = k_ref[here, :].T
-        value = v_ref[here, :]
-        for i in range(SPANS):
-            lanes = slice(i * block, (i + 1) * block)
-            query = q_ref[here, lanes]
-            scores, biases, tops = [], [], []
-            for j in range(i + 1):
-                score = dot(keys[j * block : (j + 1) * block], query, 1, 0)
-                bias = 0.0
-                if j == i:
-                    score = jnp.where(below, score, NEG)
-                else:
-                    bias = jnp.where(segments[i] == segments[j], 0.0, NEG)
-                scores.append(score)
-                biases.append(bias)
-                tops.append(jnp.max(score, axis=0, keepdims=True) + bias)
-            top = functools.reduce(jnp.maximum, tops)
-            total = jnp.zeros((1, block), F32)
-            context = jnp.zeros((HDIM, block), F32)
-            for j in range(i + 1):
-                prob = jnp.exp2(scores[j] - (top - biases[j]))
-                total = total + jnp.sum(prob, axis=0, keepdims=True)
-                context = context + dot(value[:, j * block : (j + 1) * block], prob.astype(BF16), 1, 0)
-            ctx_ref[here, lanes] = (context * (1.0 / total)).astype(BF16)
-            lse_ref[head, :, lanes] = top + jnp.log2(total)
+    spans = [slice(number * block, (number + 1) * block) for number in range(SPANS)]
+
+    @pl.loop(0, heads // PAIR)
+    def _(group):
+        units = [(group * PAIR + number, i) for number in range(PAIR) for i in range(SPANS)]
+        keys = [k_ref[at(head * HDIM, HDIM), :].T for head, i in units if i == 0]
+        raw, done = {}, {}
+
+        def scores(step):
+            head, i = units[step]
+            query = q_ref[at(head * HDIM, HDIM), spans[i]]
+            raw[step] = [dot(keys[step // SPANS][spans[j]], query, 1, 0) for j in range(i + 1)]
+
+        def softmax(step):
+            head, i = units[step]
+            parts = raw.pop(step)
+            parts[i] = jnp.where(below, parts[i], NEG)
+            biases = [jnp.where(segments[i] == segments[j], 0.0, NEG) for j in range(i)] + [0.0]
+            top = functools.reduce(
+                jnp.maximum, [jnp.max(part, axis=0, keepdims=True) + bias for part, bias in zip(parts, biases)]
+            )
+            probs = [jnp.exp2(part - (top - bias)) for part, bias in zip(parts, biases)]
+            total = sum(jnp.sum(prob, axis=0, keepdims=True) for prob in probs)
+            lse_ref[head, :, spans[i]] = top + jnp.log2(total)
+            done[step] = [prob.astype(BF16) for prob in probs], 1.0 / total
+
+        def context(step):
+            head, i = units[step]
+            here = at(head * HDIM, HDIM)
+            probs, scale = done.pop(step)
+            total = sum(dot(v_ref[here, spans[j]], prob, 1, 0) for j, prob in enumerate(probs))
+            ctx_ref[here, spans[i]] = (total * scale).astype(BF16)
+
+        for step in range(len(units) + 2):
+            if step < len(units):
+                scores(step)
+            if 0 <= step - 1 < len(units):
+                softmax(step - 1)
+            if 0 <= step - 2:
+                context(step - 2)
+        here = at(group * PAIR * HDIM, PAIR * HDIM)
         mine_ref[here, :] = ctx_ref[here, at(side * rows, rows)]
         away_ref[here, :] = ctx_ref[here, at((1 - side) * rows, rows)]
 
@@ -204,7 +230,7 @@
         (*started, oth, turned, *rope_tables(pack)),
         [shape(BF16, cols, pack)] * 3 + [shape(BF16, pack, width), shape(BF16, cols, pack)]
         + [half, half, shape(F32, heads, 1, pack)],
-        15_000_000_000,
+        15_000_000_000, room=24,
         aliases={2 + index: index for index in range(4)},
     )
 
@@ -232,7 +258,7 @@
     def plus(sums, index, value):
         sums[index] = sums[index] + value if index in sums else value
 
-    @pl.loop(first, first + heads, unroll=2)
+    @pl.loop(first, first + heads)
     def _(head):
         here = at(head * HDIM, HDIM)
         dctx_ref[:, at(side * rows, rows)] = own_ref[here, :]
@@ -336,7 +362,7 @@
         came_ref[...].T, wo_ref[at((1 - side) * part, part), :], 1, 0
     )
 
-    @pl.loop(0, rows // ROWS)
+    @pl.loop(0, rows // ROWS, unroll=2)
     def _(index):
         here = at(index * ROWS, ROWS)
         valid = valid_of(index * ROWS)
@@ -352,22 +378,25 @@
 
     turn_ref[...] = hb_ref[...].T
     relative_rows(hbt_ref, turn_ref, info_ref[1], blocks)
-    m_ref[...] = jnp.zeros_like(m_ref)
-
-    @pl.loop(0, act_ref.shape[1] // WIDE)
-    def _(step):
-        cols = at(step * WIDE, WIDE)
-        gate = dot(hb_ref[...], wg_ref[:, cols], 1, 0)
-        up = dot(hb_ref[...], wu_ref[:, cols], 1, 0)
+
+    def inputs(step):
+        cols = slice(step * CHUNK, (step + 1) * CHUNK)
+        return dot(hb_ref[...], wg_ref[:, cols], 1, 0), dot(hb_ref[...], wu_ref[:, cols], 1, 0)
+
+    count = act_ref.shape[1] // CHUNK
+    ready = inputs(0)
+    for step in range(count):
+        gate, up = ready
+        ready = inputs(step + 1) if step + 1 < count else None
+        cols = slice(step * CHUNK, (step + 1) * CHUNK)
         sig = 1.0 / (1.0 + jnp.exp(-gate))
         silu = gate * sig
-        act = (silu * up).astype(BF16)
-        act_ref[:, cols] = act
+        act_ref[:, cols] = (silu * up).astype(BF16)
         s_ref[:, cols] = silu.astype(BF16)
         t_ref[:, cols] = (up * (sig + silu * (1.0 - sig))).astype(BF16)
-        m_ref[...] += dot(act, wd_ref[cols, :], 1, 0)
-
-    @pl.loop(0, rows // ROWS)
+    m_ref[...] = dot(act_ref[...], wd_ref[...], 1, 0)
+
+    @pl.loop(0, rows // ROWS, unroll=2)
     def _(index):
         here = at(index * ROWS, ROWS)
         valid = valid_of(index * ROWS)
@@ -427,7 +456,7 @@
     cols = to_refs[0].shape[1]
     start = (side if mine else 1 - side) * cols
 
-    @pl.loop(0, cols // CHUNK)
+    @pl.loop(0, cols // CHUNK, unroll=True)
     def _(step):
         here = at(step * CHUNK, CHUNK)
         right = right_ref[:, at(start + step * CHUNK, CHUNK)]
@@ -441,9 +470,9 @@
     kernel = functools.partial(weight_kernel, order=order, blocks=blocks)
     flops = 2 * width * rows * cols
     if came is None:
-        return call(kernel, "weight_away", (info,), (left, right), [shape(BF16, width, cols)], flops)[0]
-    return call(
-        kernel, "weight_mine", (info,), (left, right, came), [shape(BF16, width // 2, cols)] * 2, flops
+        return call(kernel, "weight_away", (info,), (left, right), [shape(BF16, width, cols)], flops, room=ROOM)[0]
+    return call(
+        kernel, "weight_mine", (info,), (left, right, came), [shape(BF16, width // 2, cols)] * 2, flops, room=ROOM
     )
 
 
@@ -451,13 +480,18 @@
     info_ref, dm_ref, wd_ref, s_ref, t_ref, hbt_ref, dgt_ref, dup_ref, gate_ref, up_ref, *, orders, blocks
 ):
     half = gate_ref.shape[1]
-
-    @pl.loop(0, half // CHUNK)
-    def _(step):
-        here = at(step * CHUNK, CHUNK)
-        dgt, dup = swiglu_grads(
+    count = half // CHUNK
+
+    def grads(step):
+        return swiglu_grads(
             (1 - info_ref[0]) * half + step * CHUNK, dm_ref, wd_ref, s_ref, t_ref, dgt_ref, dup_ref
         )
+
+    ready = grads(0)
+    for step in range(count):
+        dgt, dup = ready
+        ready = grads(step + 1) if step + 1 < count else None
+        here = slice(step * CHUNK, (step + 1) * CHUNK)
         split_store(dot(hbt_ref[...], dgt, 1, 0), None, [gate_ref.at[:, here]], orders[0], blocks)
         split_store(dot(hbt_ref[...], dup, 1, 0), None, [up_ref.at[:, here]], orders[1], blocks)
 
@@ -475,7 +509,7 @@
 def swiglu_mine_kernel(info_ref, dm_ref, wd_ref, s_ref, t_ref, _, __, dgt_ref, dup_ref):
     half = s_ref.shape[1] // 2
 
-    @pl.loop(0, half // CHUNK)
+    @pl.loop(0, half // CHUNK, unroll=True)
     def _(step):
         swiglu_grads(info_ref[0] * half + step * CHUNK, dm_ref, wd_ref, s_ref, t_ref, dgt_ref, dup_ref)
 
@@ -487,7 +521,7 @@
         functools.partial(swiglu_away_kernel, orders=orders, blocks=blocks), "swiglu_away", (info,),
         (dm, wd, s, t, hbt),
         [shape(BF16, rows, ff)] * 2 + [shape(BF16, width, ff // 2)] * 2,
-        3 * rows * width * ff,
+        3 * rows * width * ff, room=ROOM,
     )
 
 
@@ -514,7 +548,7 @@
 
     small_ref[...] = part_ref[...]
 
-    @pl.loop(0, rows // ROWS)
+    @pl.loop(0, rows // ROWS, unroll=2)
     def _(index):
         here = at(index * ROWS, ROWS)
         dr1, dgain = norm_back(r1_ref[here, :], g1_ref[...], acc_ref[here, :])
@@ -615,6 +649,43 @@
     )[0]
 
 
+def finish_kernel(
+    query_ref, key_ref, value_ref, high_ref, low_ref, came_ref,
+    gq_ref, gk_ref, gv_ref, out_ref, one_ref, two_ref, rms_ref,
+):
+    rows, cols = gq_ref.shape
+    lines = high_ref.shape[0]
+    starts = (0, rows + 2 * lines, 2 * rows + 2 * lines)
+    tails = []
+    for keep_ref, start, to_ref in zip((query_ref, key_ref, value_ref), starts, (gq_ref, gk_ref, gv_ref)):
+        total = keep_ref[...].astype(F32) + came_ref[start : start + rows, :].astype(F32)
+        to_ref[...] = total[:, :cols]
+        tails.append(total[:, cols:])
+    out_ref[...] = jnp.concatenate(tails, axis=1)
+    small = whole_of(high_ref[...], low_ref[...]) + whole_of(
+        came_ref[rows : rows + lines, :], came_ref[rows + lines : rows + 2 * lines, :]
+    )
+    lanes = one_ref.shape[1]
+    width = one_ref.shape[0] * lanes
+    for number in range(one_ref.shape[0]):
+        line, start = divmod(number * lanes, WIDE)
+        for index, to_ref in enumerate((one_ref, two_ref)):
+            to_ref[number : number + 1, :] = small[2 * index + line : 2 * index + line + 1, start : start + lanes]
+    sums = jnp.sum(small[4:10], axis=1, keepdims=True)
+    count = small[10:11, 0:1] * width
+    for index in range(3):
+        rms_ref[:, index : index + 1] = jnp.sqrt((sums[2 * index : 2 * index + 1] + sums[2 * index + 1 : 2 * index + 2]) / count)
+
+
+def finish(parts, came, width, head_cols):
+    rows = parts[0].keep.shape[0]
+    return call(
+        finish_kernel, "finish", (), (*[part.keep for part in parts], *parts[0].pair, came),
+        [shape(F32, rows, head_cols)] * 4 + [shape(F32, width // 128, 128)] * 2 + [shape(F32, 1, 3)],
+        1_000_000, room=4,
+    )
+
+
 def stage_order(bits, turn):
     last = bits - 1
     return [(turn + step) % last for step in range(last)] + [last]
@@ -672,7 +743,7 @@
         self.send()
 
     @staticmethod
-    def last(parts):
+    def last(parts, done=False):
         for part in parts:
             part.receive()
             part.size = part.sent.shape[0]
@@ -682,6 +753,8 @@
             parts[0].pair = halves_of(small)
             rows[1:1] = parts[0].pair
         came = swap_dp(jnp.concatenate(rows, axis=0), parts[0].order[-1] + parts[0].shift)
+        if done:
+            return came
         start = 0
         for part in parts:
             end = start + part.size + (2 * small.shape[0] if part.small is not None else 0)
@@ -735,7 +808,7 @@
     gain_one, gain_two = gain_attn.reshape(1, width), gain_ffn.reshape(1, width)
 
     oth = swap_seq(tokens)
-    *started, turned, own_q, own_k, own_v = project_own(info, lengths, tokens, (w_query, w_key, w_value))
+    *started, turned, own_q, own_k, own_v = project_own(info, doc_lengths, tokens, (w_query, w_key, w_value))
     query, key, value, gathered, context, mine, away, lse = attention_forward(
         info, lengths, started, oth, turned
     )
@@ -799,26 +872,30 @@
     for part in attn:
         part.relay()
     down.receive()
-    Halving.last(attn)
     summed_down, summed_gate, summed_up = (part.rest() for part in ffn)
-    sums = [part.rest() for part in attn]
-    summed_out = jnp.concatenate([total[:, head_cols:] for total in sums], axis=1)
-    small = attn[0].small.reshape(8, 2 * WIDE)[:, :width]
-    squares = jnp.sum(small[2:5], axis=1)
-    rms_values = jnp.sqrt(squares / (small[5, 0] * width))
+    summed_down = summed_down.T
+    if shift:
+        Halving.last(attn)
+        sums = [part.rest() for part in attn]
+        attn_grads = [total[:, :head_cols] for total in sums]
+        attn_grads.append(jnp.concatenate([total[:, head_cols:] for total in sums], axis=1).T)
+        small = attn[0].small.reshape(8, 2 * WIDE)[:, :width]
+        grad_one, grad_two = small[0], small[1]
+        rms_values = jnp.sqrt(jnp.sum(small[2:5], axis=1) / (small[5, 0] * width))
+    else:
+        came = after(Halving.last(attn, True), summed_down, summed_gate, summed_up, grad_tokens)
+        *attn_grads, grad_wo, grad_one, grad_two, rms_values = finish(attn, came, width, head_cols)
+        attn_grads.append(grad_wo.T)
     return (
         result,
         grad_tokens,
-        sums[0][:, :head_cols],
-        sums[1][:, :head_cols],
-        sums[2][:, :head_cols],
-        summed_out.T,
+        *attn_grads,
         summed_gate,
         summed_up,
-        summed_down.T,
-        small[0],
-        small[1],
-        rms_values,
+        summed_down,
+        grad_one.reshape(-1),
+        grad_two.reshape(-1),
+        rms_values.reshape(-1),
     )
 
 

time: 171 us -> 148 us (0.87)
  local copies, waits for them, and re-layouts: 14.3 us -> 0.08 us
  Pallas kernels: 81.8 us -> 69.7 us
  waiting for transfers between devices: 36.8 us -> 42.8 us
  starting transfers between devices: 31 us -> 29 us
    pallas_call x15 -> x16, Pallas kernels: 79.2 us -> 65.5 us  [call(): pl.pallas_call(kernel, in_specs=[pl.BlockSpec(memory_space=pltpu.SMEM)] *...]
    unnamed x66 -> x26, local copies, waits for them, and re-layouts: 11.2 us -> 0.07 us
    ppermute x21, waiting for transfers between devices: 35.1 us -> 41.1 us  [swap_dp(): return lax.ppermute(value, 'dp', [(i, i ^ 1 << bit) for i in range(size)])]
    slice x8 -> x0, local copies, waits for them, and re-layouts: 3.06 us -> none  [the longest x1 0.64 us: shards(): sums[2][:, :head_cols]]
    ppermute x21, starting transfers between devices: 29 us -> 27 us  [swap_dp(): return lax.ppermute(value, 'dp', [(i, i ^ 1 << bit) for i in range(size)])]
  transfers between devices with their start and end apart: 30 -> 30, of which waited for: 10 -> 11; matrix products, arithmetic and copies ran while one was open for 4% -> 3% of each run, Pallas kernels for 30% -> 32%
where the time goes in v3:
time: 148 us
  Pallas kernels  69.7 us (47%)
  waiting for transfers between devices  42.8 us (29%)
  starting transfers between devices  29 us (20%)
  other arithmetic  4.74 us (3%)
    pallas_call x16, Pallas kernels, call(): pl.pallas_call(kernel, in_specs=[pl.BlockSpec(memory_space=pltpu.SMEM)] *...  65.5 us
    ppermute x21, waiting for transfers between devices, swap_dp(): return lax.ppermute(value, 'dp', [(i, i ^ 1 << bit) for i in range(size)])  41.1 us
    ppermute x21, starting transfers between devices, swap_dp(): return lax.ppermute(value, 'dp', [(i, i ^ 1 << bit) for i in range(size)])  27 us
    pallas_call x1, Pallas kernels, project_own(): pl.pallas_call(project_own_kernel, in_specs=[pl.BlockSpec(memory_space=pl...  4.16 us
  transfers between devices with their start and end apart: 30, of which 11 were waited for; matrix products, arithmetic and copies ran while one was open for 3% of the time, Pallas kernels for 32%

profile of v3, /device:TPU:0, one launch (start us, length us, event | category | flops | bytes accessed | tf_op | source)
XLA Modules:
  0.0 147.5 jit_solution(8296847478614111698)
XLA Ops:
  1.3 4.2 %project_own.1 = (bf16[384,1024]{1,0:T(8,128)(2,1)S(1)}, bf16[384,1024]{1,0:T(8,128)(2,1)S(1)}, bf16[384,1024]{1,0:T(8,128)(2,1)S(1)}, bf16[1024,768]{1,0:T(8,12...) custom-call(s32[2]{0:T(128)S(1)} %pad_add_fusion.info_ref, ...), custom_call_target="tpu_custom_call" | custom-call | flops 4000000000 | bytes 8000000 | tf_op jit(solution)/shard_map/project_own/pallas_call | solution.py:146
  5.6 8.4 %attention_forward.1 = (bf16[384,1024]{1,0:T(8,128)(2,1)S(1)}, bf16[384,1024]{1,0:T(8,128)(2,1)S(1)}, bf16[384,1024]{1,0:T(8,128)(2,1)S(1)}, bf16[1024,768]{1,0:...) custom-call(s32[2]{0:T(128)S(1)} %pad_add_fusion.info_ref, ...), custom_call_target="tpu_custom_call", output_to_operand_aliasing={{0}: (2, {}), {1}: (3, {}), {2}: (4, {}), {3}: (5, {})} | custom-call | flops 300000000 | bytes 110755 | tf_op jit(solution)/shard_map/attention_forward/pallas_call | solution.py:32
  14.1 1.7 %collective-permute-done.1.came_ref = bf16[384,512]{1,0:T(8,128)(2,1)S(1)} collective-permute-done((bf16[384,512]{1,0:T(8,128)(2,1)S(1)}, bf16[384,512]{1,0:T(8,128)(2,1)S(1)}, u32[]{:S(2)}, u32[]{:S(2)}) %collective-permute-start.1) | collective-permute-done | bytes 393248 | tf_op jit(solution)/shard_map/ppermute | solution.py:695
  15.9 11.4 %ffn_forward.1 = (bf16[512,2560]{1,0:T(8,128)(2,1)S(1)}, bf16[512,2560]{1,0:T(8,128)(2,1)S(1)}, bf16[512,2560]{1,0:T(8,128)(2,1)S(1)}, bf16[512,768]{1,0:T(8,128...) custom-call(s32[2]{0:T(128)S(1)} %pad_add_fusion.info_ref, ...), custom_call_target="tpu_custom_call" | custom-call | flops 120795952 | bytes 283770 | tf_op jit(solution)/shard_map/ffn_forward/pallas_call | solution.py:32
  27.3 1.7 %weight_away.1 = bf16[768,1280]{1,0:T(8,128)(2,1)S(1)} custom-call(s32[2]{0:T(128)S(1)} %pad_add_fusion.info_ref, bf16[768,512]{1,0:T(8,128)(2,1)S(1)} %get-tuple-element.104.left_ref, bf16[512,2560]{1,0:T(8,128)(2,1)S(1)} %get-tuple-element.111.right_ref), custom_call_target="tpu_custom_call" | custom-call | flops 20132660 | bytes 39321 | tf_op jit(solution)/shard_map/weight_away/pallas_call | solution.py:32
  29.2 4.0 %swiglu_away.1 = (bf16[512,2560]{1,0:T(8,128)(2,1)S(1)}, bf16[512,2560]{1,0:T(8,128)(2,1)S(1)}, bf16[768,1280]{1,0:T(8,128)(2,1)S(1)}, bf16[768,1280]{1,0:T(8,128)(2,1)S(1)}) custom-call(s32[2]{0:T(128)S(1)} %pad_add_fusion.info_ref, bf16[512,768]{1,0:T(8,128)(2,1)S(1)} %get-tuple-element.113.dm_ref, bf16[2560,768]{1,0:T(8,128)(2,1)S(1)} %copy-done, ...), custom_call_target="tpu_custom_call" | custom-call | flops 60397976 | bytes 183500 | tf_op jit(solution)/shard_map/swiglu_away/pallas_call | solution.py:32
  33.8 2.7 %weight_mine.3 = (bf16[384,1280]{1,0:T(8,128)(2,1)S(1)}, bf16[384,1280]{1,0:T(8,128)(2,1)}) custom-call(s32[2]{0:T(128)S(1)} %pad_add_fusion.info_ref, bf16[768,512]{1,0:T(8,128)(2,1)S(1)} %get-tuple-element.104.left_ref, bf16[512,2560]{1,0:T(8,128)(2,1)S(1)} %get-tuple-element.111.right_ref, bf16[768,1280]{1,0:T(8,128)(2,1)S(1)} %collective-permute-done.2.rest_0_), custom_call_target="tpu_custom_call" | custom-call | flops 20132660 | bytes 39321 | tf_op jit(solution)/shard_map/weight_mine/pallas_call | solution.py:32
  36.5 2.9 %collective-permute-start.5 = (bf16[384,1280]{1,0:T(8,128)(2,1)}, bf16[384,1280]{1,0:T(8,128)(2,1)}, u32[]{:S(2)}, u32[]{:S(2)}) collective-permute-start(bf16[384,1280]{1,0:T(8,128)(2,1)} %get-tuple-element.112), channel_id=1, source_target_pairs={{0,8},{2,10},{4,12},{6,14},{8,0},{10,2},{12,4},{14,6},{16,24},{18,... | collective-permute-start | bytes 2949128 | tf_op jit(solution)/shard_map/ppermute | solution.py:700
  39.5 2.0 %swiglu_mine.1 = (bf16[512,2560]{1,0:T(8,128)(2,1)S(1)}, bf16[512,2560]{1,0:T(8,128)(2,1)S(1)}) custom-call(s32[2]{0:T(128)S(1)} %pad_add_fusion.info_ref, bf16[512,768]{1,0:T(8,128)(2,1)S(1)} %get-tuple-element.113.dm_ref, bf16[2560,768]{1,0:T(8,128)(2,1)S(1)} %copy-done, ...), custom_call_target="tpu_custom_call", output_to_operand_aliasing={{0}: (5, {}), {1}: (6, {})} | custom-call | flops 20132660 | bytes 104857 | tf_op jit(solution)/shard_map/swiglu_mine/pallas_call | solution.py:32
  41.5 1.7 %weight_mine.4 = (bf16[384,1280]{1,0:T(8,128)(2,1)S(1)}, bf16[384,1280]{1,0:T(8,128)(2,1)S(1)}) custom-call(s32[2]{0:T(128)S(1)} %pad_add_fusion.info_ref, bf16[768,512]{1,0:T(8,128)(2,1)S(1)} %get-tuple-element.126.hbt_ref.left_ref, bf16[512,2560]{1,0:T(8,128)(2,1)S(1)} %get-tuple-element.118.right_ref.dgt_ref, ...), custom_call_target="tpu_custom_call" | custom-call | flops 20132660 | bytes 39321 | tf_op jit(solution)/shard_map/weight_mine/pallas_call | solution.py:32
  44.8 7.5 %norm_one_back.1 = (f32[512,768]{1,0:T(8,128)S(1)}, bf16[768,512]{1,0:T(8,128)(2,1)S(1)}, bf16[384,512]{1,0:T(8,128)(2,1)S(1)}, bf16[384,512]{1,0:T(8,128)(2,1)S(1)}, f32[16,512]{1,0:T(8,128)S(1)}) custom-call(s32[2]{0:T(128)S(1)} %pad_add_fusion.info_ref, bf16[512,2560]{1,0:T(8,128)(2,1)S(1)} %get-tuple-element.118.right_ref.dgt_ref, ...), custom_call_target="tpu_custom_call" | custom-call | flops 80530640 | bytes 63569 | tf_op jit(solution)/shard_map/norm_one_back/pallas_call | solution.py:32
  52.8 1.7 %weight_mine.5 = (bf16[384,1280]{1,0:T(8,128)(2,1)S(1)}, bf16[384,1280]{1,0:T(8,128)(2,1)S(1)}) custom-call(s32[2]{0:T(128)S(1)} %pad_add_fusion.info_ref, bf16[768,512]{1,0:T(8,128)(2,1)S(1)} %get-tuple-element.126.hbt_ref.left_ref, bf16[512,2560]{1,0:T(8,128)(2,1)S(1)} %get-tuple-element.119.dup_ref.right_ref, ...), custom_call_target="tpu_custom_call" | custom-call | flops 20132660 | bytes 39321 | tf_op jit(solution)/shard_map/weight_mine/pallas_call | solution.py:32
  54.6 1.6 %collective-permute-start.26 = (bf16[384,1280]{1,0:T(8,128)(2,1)S(1)}, bf16[384,1280]{1,0:T(8,128)(2,1)S(1)}, u32[]{:S(2)}, u32[]{:S(2)}) collective-permute-start(bf16[384,1280]{1,0:T(8,128)(2,1)S(1)} %get-tuple-element.128), channel_id=1, source_target_pairs={{0,4},{2,6},{4,0},{6,2},{8,12},{10,14},{12,8},{14,10},{16,20},{18,... | collective-permute-start | bytes 2949128 | tf_op jit(solution)/shard_map/ppermute | solution.py:700
  57.3 4.6 %collective-permute-done.5 = bf16[384,1280]{1,0:T(8,128)(2,1)} collective-permute-done((bf16[384,1280]{1,0:T(8,128)(2,1)}, bf16[384,1280]{1,0:T(8,128)(2,1)}, u32[]{:S(2)}, u32[]{:S(2)}) %collective-permute-start.5) | collective-permute-done | bytes 983072 | tf_op jit(solution)/shard_map/ppermute | solution.py:700
  63.2 2.8 %collective-permute-start.21 = (bf16[192,1280]{1,0:T(8,128)(2,1)S(1)}, bf16[192,1280]{1,0:T(8,128)(2,1)S(1)}, u32[]{:S(2)}, u32[]{:S(2)}) collective-permute-start(bf16[192,1280]{1,0:T(8,128)(2,1)S(1)} %get-tuple-element.179), channel_id=1, source_target_pairs={{0,16},{2,18},{4,20},{6,22},{8,24},{10,26},{12,28},{14,30},{16,0},... | collective-permute-start | bytes 1474568 | tf_op jit(solution)/shard_map/ppermute | solution.py:700
  66.1 7.0 %attention_backward.2 = (bf16[384,1024]{1,0:T(8,128)(2,1)S(1)}, bf16[384,1024]{1,0:T(8,128)(2,1)S(1)}, bf16[384,1024]{1,0:T(8,128)(2,1)S(1)}) custom-call(s32[2]{0:T(128)S(1)} %pad_add_fusion.info_ref, s32[4]{0:T(128)S(1)} %bitcast.11, bf16[384,1024]{1,0:T(8,128)(2,1)S(1)} %get-tuple-element.99.q_ref, bf16[384,1024]{1,0:T(8,128)(2,1)S(1)} %get-tuple-element.100.k_ref, ...), custom_call_target="tpu_custom_call" | custom-call | flops 240000000 | bytes 47185 | tf_op jit(solution)/shard_map/attention_backward/pallas_call | solution.py:32
  73.3 1.6 %collective-permute-start.24 = (bf16[192,1280]{1,0:T(8,128)(2,1)S(1)}, bf16[192,1280]{1,0:T(8,128)(2,1)S(1)}, u32[]{:S(2)}, u32[]{:S(2)}) collective-permute-start(bf16[192,1280]{1,0:T(8,128)(2,1)S(1)} %get-tuple-element.175), channel_id=1, source_target_pairs={{0,8},{2,10},{4,12},{6,14},{8,0},{10,2},{12,4},{14,6},{16,24},{18,... | collective-permute-start | bytes 1474568 | tf_op jit(solution)/shard_map/ppermute | solution.py:700
  74.9 6.7 %attention_backward.3 = (bf16[384,1024]{1,0:T(8,128)(2,1)S(1)}, bf16[384,1024]{1,0:T(8,128)(2,1)S(1)}, bf16[384,1024]{1,0:T(8,128)(2,1)S(1)}) custom-call(s32[2]{0:T(128)S(1)} %pad_add_fusion.info_ref, s32[4]{0:T(128)S(1)} %bitcast.12, bf16[384,1024]{1,0:T(8,128)(2,1)S(1)} %get-tuple-element.99.q_ref, ...), custom_call_target="tpu_custom_call", output_to_operand_aliasing={{0}: (11, {}), {1}: (12, {}), {2}: (13, {})} | custom-call | flops 240000000 | bytes 47185 | tf_op jit(solution)/shard_map/attention_backward/pallas_call | solution.py:32
  81.7 3.8 %project_grad.1 = (bf16[384,512]{1,0:T(8,128)(2,1)S(1)}, bf16[384,512]{1,0:T(8,128)(2,1)S(1)}, bf16[384,512]{1,0:T(8,128)(2,1)S(1)}, bf16[384,512]{1,0:T(8,128)(...) custom-call(s32[2]{0:T(128)S(1)} %pad_add_fusion.info_ref, ...), custom_call_target="tpu_custom_call" | custom-call | flops 36238784 | bytes 47185 | tf_op jit(solution)/shard_map/project_grad/pallas_call | solution.py:32
  85.4 1.6 %collective-permute-start.14 = (bf16[384,512]{1,0:T(8,128)(2,1)S(1)}, bf16[384,512]{1,0:T(8,128)(2,1)S(1)}, u32[]{:S(2)}, u32[]{:S(2)}) collective-permute-start(bf16[384,512]{1,0:T(8,128)(2,1)S(1)} %get-tuple-element.151), channel_id=1, source_target_pairs={{0,4},{2,6},{4,0},{6,2},{8,12},{10,14},{12,8},{14,10},{16,20},{18,... | collective-permute-start | bytes 1179656 | tf_op jit(solution)/shard_map/ppermute | solution.py:700
  89.3 1.9 %stream_grad.2 = bf16[768,512]{1,0:T(8,128)(2,1)S(1)} custom-call(s32[2]{0:T(128)S(1)} %pad_add_fusion.info_ref, bf16[384,1024]{1,0:T(8,128)(2,1)S(1)} %get-tuple-element.154.dq_ref, bf16[384,1024]{1,0:T(8,128)(2,1)S(1)} %get-tuple-element.155.dk_ref, bf16[384,1024]{1,0:T(8,128)(2,1)S(1)} %get-tuple-element.156.dv_ref, ...), custom_call_target="tpu_custom_call" | custom-call | flops 18119392 | bytes 15728 | tf_op jit(solution)/shard_map/stream_grad/pallas_call | solution.py:32
  91.3 4.0 %collective-permute-done.14 = bf16[384,512]{1,0:T(8,128)(2,1)S(1)} collective-permute-done((bf16[384,512]{1,0:T(8,128)(2,1)S(1)}, bf16[384,512]{1,0:T(8,128)(2,1)S(1)}, u32[]{:S(2)}, u32[]{:S(2)}) %collective-permute-start.14) | collective-permute-done | bytes 393248 | tf_op jit(solution)/shard_map/ppermute | solution.py:700
  96.9 6.6 %collective-permute-done.17 = bf16[384,512]{1,0:T(8,128)(2,1)S(1)} collective-permute-done((bf16[384,512]{1,0:T(8,128)(2,1)S(1)}, bf16[384,512]{1,0:T(8,128)(2,1)S(1)}, u32[]{:S(2)}, u32[]{:S(2)}) %collective-permute-start.17) | collective-permute-done | bytes 393248 | tf_op jit(solution)/shard_map/ppermute | solution.py:700
  105.4 4.2 %collective-permute-done.27 = bf16[192,1280]{1,0:T(8,128)(2,1)S(1)} collective-permute-done((bf16[192,1280]{1,0:T(8,128)(2,1)S(1)}, bf16[192,1280]{1,0:T(8,128)(2,1)S(1)}, u32[]{:S(2)}, u32[]{:S(2)}) %collective-permute-start.27) | collective-permute-done | bytes 491552 | tf_op jit(solution)/shard_map/ppermute | solution.py:700
  109.7 2.1 %collective-permute-start.22 = (bf16[96,1280]{1,0:T(8,128)(2,1)S(1)}, bf16[96,1280]{1,0:T(8,128)(2,1)S(1)}, u32[]{:S(2)}, u32[]{:S(2)}) collective-permute-start(bf16[96,1280]{1,0:T(8,128)(2,1)S(1)} %get-tuple-element.185), channel_id=1, source_target_pairs={{0,4},{2,6},{4,0},{6,2},{8,12},{10,14},{12,8},{14,10},{16,20},{18,... | collective-permute-start | bytes 737288 | tf_op jit(solution)/shard_map/ppermute | solution.py:700
  113.6 4.5 %collective-permute-done.12 = bf16[224,512]{1,0:T(8,128)(2,1)S(1)} collective-permute-done((bf16[224,512]{1,0:T(8,128)(2,1)S(1)}, bf16[224,512]{1,0:T(8,128)(2,1)S(1)}, u32[]{:S(2)}, u32[]{:S(2)}) %collective-permute-start.12) | collective-permute-done | bytes 229408 | tf_op jit(solution)/shard_map/ppermute | solution.py:700
  119.7 3.0 %collective-permute-done.16 = bf16[96,512]{1,0:T(8,128)(2,1)S(1)} collective-permute-done((bf16[96,512]{1,0:T(8,128)(2,1)S(1)}, bf16[96,512]{1,0:T(8,128)(2,1)S(1)}, u32[]{:S(2)}, u32[]{:S(2)}) %collective-permute-start.16) | collective-permute-done | bytes 98336 | tf_op jit(solution)/shard_map/ppermute | solution.py:700
  122.7 4.6 %collective-permute-done.19 = bf16[96,512]{1,0:T(8,128)(2,1)S(1)} collective-permute-done((bf16[96,512]{1,0:T(8,128)(2,1)S(1)}, bf16[96,512]{1,0:T(8,128)(2,1)S(1)}, u32[]{:S(2)}, u32[]{:S(2)}) %collective-permute-start.19) | collective-permute-done | bytes 98336 | tf_op jit(solution)/shard_map/ppermute | solution.py:700
  130.0 2.8 %collective-permute-done.13 = bf16[128,512]{1,0:T(8,128)(2,1)S(1)} collective-permute-done((bf16[128,512]{1,0:T(8,128)(2,1)S(1)}, bf16[128,512]{1,0:T(8,128)(2,1)S(1)}, u32[]{:S(2)}, u32[]{:S(2)}) %collective-permute-start.13) | collective-permute-done | bytes 131104 | tf_op jit(solution)/shard_map/ppermute | solution.py:700
  132.9 2.0 %collective-permute-start.20 = (bf16[176,512]{1,0:T(8,128)(2,1)S(1)}, bf16[176,512]{1,0:T(8,128)(2,1)S(1)}, u32[]{:S(2)}, u32[]{:S(2)}) collective-permute-start(bf16[176,512]{1,0:T(8,128)(2,1)S(1)} %fusion.2), channel_id=1, source_target_pairs={{0,16},{2,18},{4,20},{6,22},{8,24},{10,26},{12,28},{14,30},{16,0},... | collective-permute-start | bytes 540680 | tf_op jit(solution)/shard_map/ppermute | solution.py:700
  135.0 3.1 %stream_grad.3 = bf16[512,768]{1,0:T(8,128)(2,1)} custom-call(s32[2]{0:T(128)S(1)} %pad_add_fusion.info_ref, bf16[384,1024]{1,0:T(8,128)(2,1)S(1)} %get-tuple-element.154.dq_ref, bf16[384,1024]{1,0:T(8,128)(2,1)S(1)} %get-tuple-element.155.dk_ref, bf16[384,1024]{1,0:T(8,128)(2,1)S(1)} %get-tuple-element.156.dv_ref, ...), custom_call_target="tpu_custom_call" | custom-call | flops 18119392 | bytes 15728 | tf_op jit(solution)/shard_map/stream_grad/pallas_call | solution.py:32
  138.9 5.9 %collective-permute-done.29 = bf16[96,1280]{1,0:T(8,128)(2,1)S(1)} collective-permute-done((bf16[96,1280]{1,0:T(8,128)(2,1)S(1)}, bf16[96,1280]{1,0:T(8,128)(2,1)S(1)}, u32[]{:S(2)}, u32[]{:S(2)}) %collective-permute-start.29) | collective-permute-done | bytes 245792 | tf_op jit(solution)/shard_map/ppermute | solution.py:700
  (106 shorter events, 22.0 us)
Async XLA Ops:
  0.6 4.8 %collective-permute-start = (bf16[512,768]{1,0:T(8,128)(2,1)}, bf16[512,768]{1,0:T(8,128)(2,1)S(1)}, u32[]{:S(2)}, u32[]{:S(2)}) collective-permute-start(bf16[512,768]{1,0:T(8,128)(2,1)} %x_ref.1), channel_id=1, source_target_pairs={{0,1},{1,0},{2,3},{3,2},{4,5},{5,4},{6,7},{7,6},{8,9},{9,8},{10,11... | collective-permute-start | bytes 2359304 | tf_op jit(solution)/shard_map/ppermute | solution.py:695
  1.3 14.5 %copy-start.1 = (bf16[768,2560]{1,0:T(8,128)(2,1)S(1)}, bf16[768,2560]{1,0:T(8,128)(2,1)}, u32[]{:S(2)}) copy-start(bf16[768,2560]{1,0:T(8,128)(2,1)} %wg_ref.3) | copy-start | bytes 11796484
  1.3 14.5 %copy-start.2 = (bf16[768,2560]{1,0:T(8,128)(2,1)S(1)}, bf16[768,2560]{1,0:T(8,128)(2,1)}, u32[]{:S(2)}) copy-start(bf16[768,2560]{1,0:T(8,128)(2,1)} %wu_ref.3) | copy-start | bytes 11796484
  14.0 1.8 %collective-permute-start.1 = (bf16[384,512]{1,0:T(8,128)(2,1)S(1)}, bf16[384,512]{1,0:T(8,128)(2,1)S(1)}, u32[]{:S(2)}, u32[]{:S(2)}) collective-permute-start(bf16[384,512]{1,0:T(8,128)(2,1)S(1)} %get-tuple-element.97), channel_id=1, source_target_pairs={{0,1},{1,0},{2,3},{3,2},{4,5},{5,4},{6,7},{7,6},{8,9},{9,8},{10,11... | collective-permute-start | bytes 1179656 | tf_op jit(solution)/shard_map/ppermute | solution.py:695
  29.0 4.8 %collective-permute-start.2 = (bf16[768,1280]{1,0:T(8,128)(2,1)S(1)}, bf16[768,1280]{1,0:T(8,128)(2,1)S(1)}, u32[]{:S(2)}, u32[]{:S(2)}) collective-permute-start(bf16[768,1280]{1,0:T(8,128)(2,1)S(1)} %weight_away.1), channel_id=1, source_target_pairs={{0,1},{1,0},{2,3},{3,2},{4,5},{5,4},{6,7},{7,6},{8,9},{9,8},{10,11... | collective-permute-start | bytes 5898248 | tf_op jit(solution)/shard_map/ppermute | solution.py:695
  33.2 8.2 %collective-permute-start.3 = (bf16[768,1280]{1,0:T(8,128)(2,1)S(1)}, bf16[768,1280]{1,0:T(8,128)(2,1)S(1)}, u32[]{:S(2)}, u32[]{:S(2)}) collective-permute-start(bf16[768,1280]{1,0:T(8,128)(2,1)S(1)} %get-tuple-element.110), channel_id=1, source_target_pairs={{0,1},{1,0},{2,3},{3,2},{4,5},{5,4},{6,7},{7,6},{8,9},{9,8},{10,11... | collective-permute-start | bytes 5898248 | tf_op jit(solution)/shard_map/ppermute | solution.py:695
  33.7 19.1 %collective-permute-start.4 = (bf16[768,1280]{1,0:T(8,128)(2,1)S(1)}, bf16[768,1280]{1,0:T(8,128)(2,1)S(1)}, u32[]{:S(2)}, u32[]{:S(2)}) collective-permute-start(bf16[768,1280]{1,0:T(8,128)(2,1)S(1)} %get-tuple-element.127), channel_id=1, source_target_pairs={{0,1},{1,0},{2,3},{3,2},{4,5},{5,4},{6,7},{7,6},{8,9},{9,8},{10,11... | collective-permute-start | bytes 5898248 | tf_op jit(solution)/shard_map/ppermute | solution.py:695
  36.5 25.3 %collective-permute-start.5 = (bf16[384,1280]{1,0:T(8,128)(2,1)}, bf16[384,1280]{1,0:T(8,128)(2,1)}, u32[]{:S(2)}, u32[]{:S(2)}) collective-permute-start(bf16[384,1280]{1,0:T(8,128)(2,1)} %get-tuple-element.112), channel_id=1, source_target_pairs={{0,8},{2,10},{4,12},{6,14},{8,0},{10,2},{12,4},{14,6},{16,24},{18,... | collective-permute-start | bytes 2949128 | tf_op jit(solution)/shard_map/ppermute | solution.py:700
  43.2 29.8 %collective-permute-start.7 = (bf16[384,1280]{1,0:T(8,128)(2,1)S(1)}, bf16[384,1280]{1,0:T(8,128)(2,1)S(1)}, u32[]{:S(2)}, u32[]{:S(2)}) collective-permute-start(bf16[384,1280]{1,0:T(8,128)(2,1)S(1)} %get-tuple-element.117), channel_id=1, source_target_pairs={{0,2},{2,0},{4,6},{6,4},{8,10},{10,8},{12,14},{14,12},{16,18},{18,... | collective-permute-start | bytes 2949128 | tf_op jit(solution)/shard_map/ppermute | solution.py:700
  52.2 4.9 %collective-permute-start.10 = (f32[16,512]{1,0:T(8,128)S(1)}, f32[16,512]{1,0:T(8,128)S(1)}, u32[]{:S(2)}, u32[]{:S(2)}) collective-permute-start(f32[16,512]{1,0:T(8,128)S(1)} %get-tuple-element.158), channel_id=1, source_target_pairs={{0,1},{1,0},{2,3},{3,2},{4,5},{5,4},{6,7},{7,6},{8,9},{9,8},{10,11... | collective-permute-start | bytes 98312 | tf_op jit(solution)/shard_map/ppermute | solution.py:695
  52.3 13.7 %collective-permute-start.6 = (bf16[384,512]{1,0:T(8,128)(2,1)S(1)}, bf16[384,512]{1,0:T(8,128)(2,1)S(1)}, u32[]{:S(2)}, u32[]{:S(2)}) collective-permute-start(bf16[384,512]{1,0:T(8,128)(2,1)S(1)} %get-tuple-element.125), channel_id=1, source_target_pairs={{0,1},{1,0},{2,3},{3,2},{4,5},{5,4},{6,7},{7,6},{8,9},{9,8},{10,11... | collective-permute-start | bytes 1179656 | tf_op jit(solution)/shard_map/ppermute | solution.py:695
  54.6 32.9 %collective-permute-start.26 = (bf16[384,1280]{1,0:T(8,128)(2,1)S(1)}, bf16[384,1280]{1,0:T(8,128)(2,1)S(1)}, u32[]{:S(2)}, u32[]{:S(2)}) collective-permute-start(bf16[384,1280]{1,0:T(8,128)(2,1)S(1)} %get-tuple-element.128), channel_id=1, source_target_pairs={{0,4},{2,6},{4,0},{6,2},{8,12},{10,14},{12,8},{14,10},{16,20},{18,... | collective-permute-start | bytes 2949128 | tf_op jit(solution)/shard_map/ppermute | solution.py:700
  57.2 24.5 %collective-permute-start.8 = (bf16[768,384]{1,0:T(8,128)(2,1)S(1)}, bf16[768,384]{1,0:T(8,128)(2,1)S(1)}, u32[]{:S(2)}, u32[]{:S(2)}) collective-permute-start(bf16[768,384]{1,0:T(8,128)(2,1)S(1)} %get-tuple-element.130), channel_id=1, source_target_pairs={{0,1},{1,0},{2,3},{3,2},{4,5},{5,4},{6,7},{7,6},{8,9},{9,8},{10,11... | collective-permute-start | bytes 1769480 | tf_op jit(solution)/shard_map/ppermute | solution.py:695
  63.2 40.5 %collective-permute-start.21 = (bf16[192,1280]{1,0:T(8,128)(2,1)S(1)}, bf16[192,1280]{1,0:T(8,128)(2,1)S(1)}, u32[]{:S(2)}, u32[]{:S(2)}) collective-permute-start(bf16[192,1280]{1,0:T(8,128)(2,1)S(1)} %get-tuple-element.179), channel_id=1, source_target_pairs={{0,16},{2,18},{4,20},{6,22},{8,24},{10,26},{12,28},{14,30},{16,0},... | collective-permute-start | bytes 1474568 | tf_op jit(solution)/shard_map/ppermute | solution.py:700
  73.3 36.4 %collective-permute-start.24 = (bf16[192,1280]{1,0:T(8,128)(2,1)S(1)}, bf16[192,1280]{1,0:T(8,128)(2,1)S(1)}, u32[]{:S(2)}, u32[]{:S(2)}) collective-permute-start(bf16[192,1280]{1,0:T(8,128)(2,1)S(1)} %get-tuple-element.175), channel_id=1, source_target_pairs={{0,8},{2,10},{4,12},{6,14},{8,0},{10,2},{12,4},{14,6},{16,24},{18,... | collective-permute-start | bytes 1474568 | tf_op jit(solution)/shard_map/ppermute | solution.py:700
  85.4 9.8 %collective-permute-start.14 = (bf16[384,512]{1,0:T(8,128)(2,1)S(1)}, bf16[384,512]{1,0:T(8,128)(2,1)S(1)}, u32[]{:S(2)}, u32[]{:S(2)}) collective-permute-start(bf16[384,512]{1,0:T(8,128)(2,1)S(1)} %get-tuple-element.151), channel_id=1, source_target_pairs={{0,4},{2,6},{4,0},{6,2},{8,12},{10,14},{12,8},{14,10},{16,20},{18,... | collective-permute-start | bytes 1179656 | tf_op jit(solution)/shard_map/ppermute | solution.py:700
  87.0 16.4 %collective-permute-start.17 = (bf16[384,512]{1,0:T(8,128)(2,1)S(1)}, bf16[384,512]{1,0:T(8,128)(2,1)S(1)}, u32[]{:S(2)}, u32[]{:S(2)}) collective-permute-start(bf16[384,512]{1,0:T(8,128)(2,1)S(1)} %get-tuple-element.153), channel_id=1, source_target_pairs={{0,8},{2,10},{4,12},{6,14},{8,0},{10,2},{12,4},{14,6},{16,24},{18,... | collective-permute-start | bytes 1179656 | tf_op jit(solution)/shard_map/ppermute | solution.py:700
  87.8 15.8 %collective-permute-start.11 = (bf16[416,512]{1,0:T(8,128)(2,1)S(1)}, bf16[416,512]{1,0:T(8,128)(2,1)S(1)}, u32[]{:S(2)}, u32[]{:S(2)}) collective-permute-start(bf16[416,512]{1,0:T(8,128)(2,1)S(1)} %pad_maximum_fusion), channel_id=1, source_target_pairs={{0,2},{2,0},{4,6},{6,4},{8,10},{10,8},{12,14},{14,12},{16,18},{18,... | collective-permute-start | bytes 1277960 | tf_op jit(solution)/shard_map/ppermute | solution.py:700
  95.2 14.3 %collective-permute-start.27 = (bf16[192,1280]{1,0:T(8,128)(2,1)S(1)}, bf16[192,1280]{1,0:T(8,128)(2,1)S(1)}, u32[]{:S(2)}, u32[]{:S(2)}) collective-permute-start(bf16[192,1280]{1,0:T(8,128)(2,1)S(1)} %get-tuple-element.177), channel_id=1, source_target_pairs={{0,2},{2,0},{4,6},{6,4},{8,10},{10,8},{12,14},{14,12},{16,18},{18,... | collective-permute-start | bytes 1474568 | tf_op jit(solution)/shard_map/ppermute | solution.py:700
  103.4 31.6 %collective-permute-start.9 = (bf16[768,512]{1,0:T(8,128)(2,1)S(1)}, bf16[768,512]{1,0:T(8,128)(2,1)S(1)}, u32[]{:S(2)}, u32[]{:S(2)}) collective-permute-start(bf16[768,512]{1,0:T(8,128)(2,1)S(1)} %stream_grad.2), channel_id=1, source_target_pairs={{0,1},{1,0},{2,3},{3,2},{4,5},{5,4},{6,7},{7,6},{8,9},{9,8},{10,11... | collective-permute-start | bytes 2359304 | tf_op jit(solution)/shard_map/ppermute | solution.py:695
  103.5 8.4 %collective-permute-start.15 = (bf16[192,512]{1,0:T(8,128)(2,1)S(1)}, bf16[192,512]{1,0:T(8,128)(2,1)S(1)}, u32[]{:S(2)}, u32[]{:S(2)}) collective-permute-start(bf16[192,512]{1,0:T(8,128)(2,1)S(1)} %get-tuple-element.191), channel_id=1, source_target_pairs={{0,8},{2,10},{4,12},{6,14},{8,0},{10,2},{12,4},{14,6},{16,24},{18,... | collective-permute-start | bytes 589832 | tf_op jit(solution)/shard_map/ppermute | solution.py:700
  103.8 9.6 %collective-permute-start.18 = (bf16[192,512]{1,0:T(8,128)(2,1)S(1)}, bf16[192,512]{1,0:T(8,128)(2,1)S(1)}, u32[]{:S(2)}, u32[]{:S(2)}) collective-permute-start(bf16[192,512]{1,0:T(8,128)(2,1)S(1)} %get-tuple-element.189), channel_id=1, source_target_pairs={{0,2},{2,0},{4,6},{6,4},{8,10},{10,8},{12,14},{14,12},{16,18},{18,... | collective-permute-start | bytes 589832 | tf_op jit(solution)/shard_map/ppermute | solution.py:700
  109.5 8.5 %collective-permute-start.12 = (bf16[224,512]{1,0:T(8,128)(2,1)S(1)}, bf16[224,512]{1,0:T(8,128)(2,1)S(1)}, u32[]{:S(2)}, u32[]{:S(2)}) collective-permute-start(bf16[224,512]{1,0:T(8,128)(2,1)S(1)} %pad_maximum_fusion.2), channel_id=1, source_target_pairs={{0,4},{2,6},{4,0},{6,2},{8,12},{10,14},{12,8},{14,10},{16,20},{18,... | collective-permute-start | bytes 688136 | tf_op jit(solution)/shard_map/ppermute | solution.py:700
  109.7 19.0 %collective-permute-start.22 = (bf16[96,1280]{1,0:T(8,128)(2,1)S(1)}, bf16[96,1280]{1,0:T(8,128)(2,1)S(1)}, u32[]{:S(2)}, u32[]{:S(2)}) collective-permute-start(bf16[96,1280]{1,0:T(8,128)(2,1)S(1)} %get-tuple-element.185), channel_id=1, source_target_pairs={{0,4},{2,6},{4,0},{6,2},{8,12},{10,14},{12,8},{14,10},{16,20},{18,... | collective-permute-start | bytes 737288 | tf_op jit(solution)/shard_map/ppermute | solution.py:700
  111.9 17.9 %collective-permute-start.28 = (bf16[96,1280]{1,0:T(8,128)(2,1)S(1)}, bf16[96,1280]{1,0:T(8,128)(2,1)S(1)}, u32[]{:S(2)}, u32[]{:S(2)}) collective-permute-start(bf16[96,1280]{1,0:T(8,128)(2,1)S(1)} %get-tuple-element.183), channel_id=1, source_target_pairs={{0,8},{2,10},{4,12},{6,14},{8,0},{10,2},{12,4},{14,6},{16,24},{18,... | collective-permute-start | bytes 737288 | tf_op jit(solution)/shard_map/ppermute | solution.py:700
  113.4 16.4 %collective-permute-start.25 = (bf16[96,1280]{1,0:T(8,128)(2,1)S(1)}, bf16[96,1280]{1,0:T(8,128)(2,1)S(1)}, u32[]{:S(2)}, u32[]{:S(2)}) collective-permute-start(bf16[96,1280]{1,0:T(8,128)(2,1)S(1)} %get-tuple-element.181), channel_id=1, source_target_pairs={{0,4},{2,6},{4,0},{6,2},{8,12},{10,14},{12,8},{14,10},{16,20},{18,... | collective-permute-start | bytes 737288 | tf_op jit(solution)/shard_map/ppermute | solution.py:700
  118.0 4.6 %collective-permute-start.16 = (bf16[96,512]{1,0:T(8,128)(2,1)S(1)}, bf16[96,512]{1,0:T(8,128)(2,1)S(1)}, u32[]{:S(2)}, u32[]{:S(2)}) collective-permute-start(bf16[96,512]{1,0:T(8,128)(2,1)S(1)} %get-tuple-element.199), channel_id=1, source_target_pairs={{0,2},{2,0},{4,6},{6,4},{8,10},{10,8},{12,14},{14,12},{16,18},{18,... | collective-permute-start | bytes 294920 | tf_op jit(solution)/shard_map/ppermute | solution.py:700
  122.6 4.6 %collective-permute-start.19 = (bf16[96,512]{1,0:T(8,128)(2,1)S(1)}, bf16[96,512]{1,0:T(8,128)(2,1)S(1)}, u32[]{:S(2)}, u32[]{:S(2)}) collective-permute-start(bf16[96,512]{1,0:T(8,128)(2,1)S(1)} %get-tuple-element.197), channel_id=1, source_target_pairs={{0,4},{2,6},{4,0},{6,2},{8,12},{10,14},{12,8},{14,10},{16,20},{18,... | collective-permute-start | bytes 294920 | tf_op jit(solution)/shard_map/ppermute | solution.py:700
  127.2 5.6 %collective-permute-start.13 = (bf16[128,512]{1,0:T(8,128)(2,1)S(1)}, bf16[128,512]{1,0:T(8,128)(2,1)S(1)}, u32[]{:S(2)}, u32[]{:S(2)}) collective-permute-start(bf16[128,512]{1,0:T(8,128)(2,1)S(1)} %pad_maximum_fusion.3), channel_id=1, source_target_pairs={{0,8},{2,10},{4,12},{6,14},{8,0},{10,2},{12,4},{14,6},{16,24},{18,... | collective-permute-start | bytes 393224 | tf_op jit(solution)/shard_map/ppermute | solution.py:700
  128.7 9.4 %collective-permute-start.23 = (bf16[48,1280]{1,0:T(8,128)(2,1)S(1)}, bf16[48,1280]{1,0:T(8,128)(2,1)S(1)}, u32[]{:S(2)}, u32[]{:S(2)}) collective-permute-start(bf16[48,1280]{1,0:T(8,128)(2,1)S(1)} %add_convert_fusion.22), channel_id=1, source_target_pairs={{0,2},{2,0},{4,6},{6,4},{8,10},{10,8},{12,14},{14,12},{16,18},{18,... | collective-permute-start | bytes 368648 | tf_op jit(solution)/shard_map/ppermute | solution.py:700
  129.9 14.9 %collective-permute-start.29 = (bf16[96,1280]{1,0:T(8,128)(2,1)S(1)}, bf16[96,1280]{1,0:T(8,128)(2,1)S(1)}, u32[]{:S(2)}, u32[]{:S(2)}) collective-permute-start(bf16[96,1280]{1,0:T(8,128)(2,1)S(1)} %pad_maximum_fusion.1), channel_id=1, source_target_pairs={{0,16},{2,18},{4,20},{6,22},{8,24},{10,26},{12,28},{14,30},{16,0},... | collective-permute-start | bytes 737288 | tf_op jit(solution)/shard_map/ppermute | solution.py:700
  132.9 13.8 %collective-permute-start.20 = (bf16[176,512]{1,0:T(8,128)(2,1)S(1)}, bf16[176,512]{1,0:T(8,128)(2,1)S(1)}, u32[]{:S(2)}, u32[]{:S(2)}) collective-permute-start(bf16[176,512]{1,0:T(8,128)(2,1)S(1)} %fusion.2), channel_id=1, source_target_pairs={{0,16},{2,18},{4,20},{6,22},{8,24},{10,26},{12,28},{14,30},{16,0},... | collective-permute-start | bytes 540680 | tf_op jit(solution)/shard_map/ppermute | solution.py:700
  (11 other events, 80.3 us)

commit v4 on v3

--- a/solution.py
+++ b/solution.py
@@ -686,11 +686,6 @@
     )
 
 
-def stage_order(bits, turn):
-    last = bits - 1
-    return [(turn + step) % last for step in range(last)] + [last]
-
-
 def swap_seq(value):
     return lax.ppermute(value, "seq", [(0, 1), (1, 0)])
 
@@ -752,7 +747,8 @@
         if small is not None:
             parts[0].pair = halves_of(small)
             rows[1:1] = parts[0].pair
-        came = swap_dp(jnp.concatenate(rows, axis=0), parts[0].order[-1] + parts[0].shift)
+        joint = jnp.concatenate(rows, axis=0)
+        came = swap_dp(joint, parts[0].order[-1] + parts[0].shift)
         if done:
             return came
         start = 0
@@ -762,6 +758,7 @@
             start = end
             part.step += 1
             part.receive()
+        return joint
 
     def rest(self):
         value = self.keep
@@ -798,10 +795,9 @@
     head_cols = w_query.shape[1] // lax.axis_size("seq")
     dp_size = lax.axis_size("dp")
     blocks = min(dp_size, 16)
-    bits = blocks.bit_length() - 1
     shift = (dp_size // blocks).bit_length() - 1
-    turns = [stage_order(bits, turn) for turn in range(3)]
-    orders = ((0, 2, 1, 3), (1, 0, 2, 3), (2, 3, 1, 0))
+    orders = ((0, 2, 1, 3), (1, 0, 2, 3), (2, 3, 0, 1))
+    turns = ((1, 2, 0, 3), (1, 0, 2, 3), (2, 1, 0, 3))
     lengths = doc_lengths[0]
     seq_index = lax.axis_index("seq")
     info = jnp.stack([seq_index, lax.axis_index("dp") >> shift]).astype(jnp.int32)
@@ -857,20 +853,25 @@
         for index in range(3)
     ]
     up.relay(*sides)
-    down.relay(*sides)
-    for part in attn:
-        part.send()
+    query_part, key_part, value_part = attn
+    key_part.send()
+    value_part.send()
     weights = (own_q, own_k, own_v)
-    stream_away = stream_grad(info, after(grads, *sides), weights)
-    grad_tokens = stream_grad(info, grads, weights, swap_seq(stream_away), dr1)
-    gate.relay()
-    up.relay()
-    down.relay()
-    for part in attn:
-        part.relay()
-    Halving.last([gate, up])
-    for part in attn:
-        part.relay()
+    stream_away = stream_grad(info, after(grads, *sides, up.sent), weights)
+    stream_came = swap_seq(stream_away)
+    gate.relay(stream_away)
+    down.relay(stream_away)
+    query_part.sent = after(query_part.sent, gate.sent, down.sent, key_part.came)
+    query_part.send()
+    grad_tokens = stream_grad(info, after(grads, key_part.came), weights, stream_came, dr1)
+    up.relay(grad_tokens)
+    key_part.relay(up.sent)
+    value_part.relay(up.sent)
+    joint = Halving.last([gate, up])
+    down.relay(joint)
+    query_part.relay(joint)
+    for part in (key_part, value_part, query_part):
+        part.relay(joint)
     down.receive()
     summed_down, summed_gate, summed_up = (part.rest() for part in ffn)
     summed_down = summed_down.T

time: 148 us -> 144 us (0.973)
  waiting for transfers between devices: 42.8 us -> 36.7 us
  starting transfers between devices: 29 us -> 31.8 us
    ppermute x21, waiting for transfers between devices: 41.1 us -> 35 us  [swap_dp(): return lax.ppermute(value, 'dp', [(i, i ^ 1 << bit) for i in range(size)])]
    ppermute x21, starting transfers between devices: 27 us -> 29.7 us  [swap_dp(): return lax.ppermute(value, 'dp', [(i, i ^ 1 << bit) for i in range(size)])]
  transfers between devices with their start and end apart: 30 -> 30, of which waited for: 11 -> 11; matrix products, arithmetic and copies ran while one was open for 3% -> 3% of each run, Pallas kernels for 32% -> 33%
where the time goes in v4:
time: 144 us
  Pallas kernels  69.7 us (48%)
  waiting for transfers between devices  36.7 us (25%)
  starting transfers between devices  31.8 us (22%)
  other arithmetic  4.74 us (3%)
    pallas_call x16, Pallas kernels, call(): pl.pallas_call(kernel, in_specs=[pl.BlockSpec(memory_space=pltpu.SMEM)] *...  65.5 us
    ppermute x21, waiting for transfers between devices, swap_dp(): return lax.ppermute(value, 'dp', [(i, i ^ 1 << bit) for i in range(size)])  35 us
    ppermute x21, starting transfers between devices, swap_dp(): return lax.ppermute(value, 'dp', [(i, i ^ 1 << bit) for i in range(size)])  29.7 us
    pallas_call x1, Pallas kernels, project_own(): pl.pallas_call(project_own_kernel, in_specs=[pl.BlockSpec(memory_space=pl...  4.16 us
  transfers between devices with their start and end apart: 30, of which 11 were waited for; matrix products, arithmetic and copies ran while one was open for 3% of the time, Pallas kernels for 33%

profile of v4, /device:TPU:0, one launch (start us, length us, event | category | flops | bytes accessed | tf_op | source)
XLA Modules:
  0.0 144.2 jit_solution(18300611687388188913)
XLA Ops:
  1.3 4.2 %project_own.1 = (bf16[384,1024]{1,0:T(8,128)(2,1)S(1)}, bf16[384,1024]{1,0:T(8,128)(2,1)S(1)}, bf16[384,1024]{1,0:T(8,128)(2,1)S(1)}, bf16[1024,768]{1,0:T(8,12...) custom-call(s32[2]{0:T(128)S(1)} %pad_add_fusion.info_ref, ...), custom_call_target="tpu_custom_call" | custom-call | flops 4000000000 | bytes 8000000 | tf_op jit(solution)/shard_map/project_own/pallas_call | solution.py:146
  5.6 8.4 %attention_forward.1 = (bf16[384,1024]{1,0:T(8,128)(2,1)S(1)}, bf16[384,1024]{1,0:T(8,128)(2,1)S(1)}, bf16[384,1024]{1,0:T(8,128)(2,1)S(1)}, bf16[1024,768]{1,0:...) custom-call(s32[2]{0:T(128)S(1)} %pad_add_fusion.info_ref, ...), custom_call_target="tpu_custom_call", output_to_operand_aliasing={{0}: (2, {}), {1}: (3, {}), {2}: (4, {}), {3}: (5, {})} | custom-call | flops 300000000 | bytes 110755 | tf_op jit(solution)/shard_map/attention_forward/pallas_call | solution.py:32
  14.1 1.7 %collective-permute-done.1.came_ref = bf16[384,512]{1,0:T(8,128)(2,1)S(1)} collective-permute-done((bf16[384,512]{1,0:T(8,128)(2,1)S(1)}, bf16[384,512]{1,0:T(8,128)(2,1)S(1)}, u32[]{:S(2)}, u32[]{:S(2)}) %collective-permute-start.1) | collective-permute-done | bytes 393248 | tf_op jit(solution)/shard_map/ppermute | solution.py:690
  15.9 11.4 %ffn_forward.1 = (bf16[512,2560]{1,0:T(8,128)(2,1)S(1)}, bf16[512,2560]{1,0:T(8,128)(2,1)S(1)}, bf16[512,2560]{1,0:T(8,128)(2,1)S(1)}, bf16[512,768]{1,0:T(8,128...) custom-call(s32[2]{0:T(128)S(1)} %pad_add_fusion.info_ref, ...), custom_call_target="tpu_custom_call" | custom-call | flops 120795952 | bytes 283770 | tf_op jit(solution)/shard_map/ffn_forward/pallas_call | solution.py:32
  27.3 1.7 %weight_away.1 = bf16[768,1280]{1,0:T(8,128)(2,1)S(1)} custom-call(s32[2]{0:T(128)S(1)} %pad_add_fusion.info_ref, bf16[768,512]{1,0:T(8,128)(2,1)S(1)} %get-tuple-element.117.left_ref, bf16[512,2560]{1,0:T(8,128)(2,1)S(1)} %get-tuple-element.124.right_ref), custom_call_target="tpu_custom_call" | custom-call | flops 20132660 | bytes 39321 | tf_op jit(solution)/shard_map/weight_away/pallas_call | solution.py:32
  29.2 4.0 %swiglu_away.1 = (bf16[512,2560]{1,0:T(8,128)(2,1)S(1)}, bf16[512,2560]{1,0:T(8,128)(2,1)S(1)}, bf16[768,1280]{1,0:T(8,128)(2,1)S(1)}, bf16[768,1280]{1,0:T(8,128)(2,1)S(1)}) custom-call(s32[2]{0:T(128)S(1)} %pad_add_fusion.info_ref, bf16[512,768]{1,0:T(8,128)(2,1)S(1)} %get-tuple-element.126.dm_ref, bf16[2560,768]{1,0:T(8,128)(2,1)S(1)} %copy-done, ...), custom_call_target="tpu_custom_call" | custom-call | flops 60397976 | bytes 183500 | tf_op jit(solution)/shard_map/swiglu_away/pallas_call | solution.py:32
  33.8 2.7 %weight_mine.3 = (bf16[384,1280]{1,0:T(8,128)(2,1)S(1)}, bf16[384,1280]{1,0:T(8,128)(2,1)}) custom-call(s32[2]{0:T(128)S(1)} %pad_add_fusion.info_ref, bf16[768,512]{1,0:T(8,128)(2,1)S(1)} %get-tuple-element.117.left_ref, bf16[512,2560]{1,0:T(8,128)(2,1)S(1)} %get-tuple-element.124.right_ref, bf16[768,1280]{1,0:T(8,128)(2,1)S(1)} %collective-permute-done.2.rest_0_), custom_call_target="tpu_custom_call" | custom-call | flops 20132660 | bytes 39321 | tf_op jit(solution)/shard_map/weight_mine/pallas_call | solution.py:32
  36.5 3.0 %collective-permute-start.5 = (bf16[384,1280]{1,0:T(8,128)(2,1)}, bf16[384,1280]{1,0:T(8,128)(2,1)}, u32[]{:S(2)}, u32[]{:S(2)}) collective-permute-start(bf16[384,1280]{1,0:T(8,128)(2,1)} %get-tuple-element.125), channel_id=1, source_target_pairs={{0,8},{2,10},{4,12},{6,14},{8,0},{10,2},{12,4},{14,6},{16,24},{18,... | collective-permute-start | bytes 2949128 | tf_op jit(solution)/shard_map/ppermute | solution.py:695
  39.5 2.0 %swiglu_mine.1 = (bf16[512,2560]{1,0:T(8,128)(2,1)S(1)}, bf16[512,2560]{1,0:T(8,128)(2,1)S(1)}) custom-call(s32[2]{0:T(128)S(1)} %pad_add_fusion.info_ref, bf16[512,768]{1,0:T(8,128)(2,1)S(1)} %get-tuple-element.126.dm_ref, bf16[2560,768]{1,0:T(8,128)(2,1)S(1)} %copy-done, ...), custom_call_target="tpu_custom_call", output_to_operand_aliasing={{0}: (5, {}), {1}: (6, {})} | custom-call | flops 20132660 | bytes 104857 | tf_op jit(solution)/shard_map/swiglu_mine/pallas_call | solution.py:32
  41.5 1.7 %weight_mine.4 = (bf16[384,1280]{1,0:T(8,128)(2,1)S(1)}, bf16[384,1280]{1,0:T(8,128)(2,1)S(1)}) custom-call(s32[2]{0:T(128)S(1)} %pad_add_fusion.info_ref, bf16[768,512]{1,0:T(8,128)(2,1)S(1)} %get-tuple-element.139.hbt_ref.left_ref, bf16[512,2560]{1,0:T(8,128)(2,1)S(1)} %get-tuple-element.131.right_ref.dgt_ref, ...), custom_call_target="tpu_custom_call" | custom-call | flops 20132660 | bytes 39321 | tf_op jit(solution)/shard_map/weight_mine/pallas_call | solution.py:32
  44.8 7.4 %norm_one_back.1 = (f32[512,768]{1,0:T(8,128)S(1)}, bf16[768,512]{1,0:T(8,128)(2,1)S(1)}, bf16[384,512]{1,0:T(8,128)(2,1)S(1)}, bf16[384,512]{1,0:T(8,128)(2,1)S(1)}, f32[16,512]{1,0:T(8,128)S(1)}) custom-call(s32[2]{0:T(128)S(1)} %pad_add_fusion.info_ref, bf16[512,2560]{1,0:T(8,128)(2,1)S(1)} %get-tuple-element.131.right_ref.dgt_ref, ...), custom_call_target="tpu_custom_call" | custom-call | flops 80530640 | bytes 63569 | tf_op jit(solution)/shard_map/norm_one_back/pallas_call | solution.py:32
  52.8 1.7 %weight_mine.5 = (bf16[384,1280]{1,0:T(8,128)(2,1)S(1)}, bf16[384,1280]{1,0:T(8,128)(2,1)S(1)}) custom-call(s32[2]{0:T(128)S(1)} %pad_add_fusion.info_ref, bf16[768,512]{1,0:T(8,128)(2,1)S(1)} %get-tuple-element.139.hbt_ref.left_ref, bf16[512,2560]{1,0:T(8,128)(2,1)S(1)} %get-tuple-element.132.dup_ref.right_ref, ...), custom_call_target="tpu_custom_call" | custom-call | flops 20132660 | bytes 39321 | tf_op jit(solution)/shard_map/weight_mine/pallas_call | solution.py:32
  54.6 1.6 %collective-permute-start.10 = (bf16[384,1280]{1,0:T(8,128)(2,1)S(1)}, bf16[384,1280]{1,0:T(8,128)(2,1)S(1)}, u32[]{:S(2)}, u32[]{:S(2)}) collective-permute-start(bf16[384,1280]{1,0:T(8,128)(2,1)S(1)} %get-tuple-element.141), channel_id=1, source_target_pairs={{0,4},{2,6},{4,0},{6,2},{8,12},{10,14},{12,8},{14,10},{16,20},{18,... | collective-permute-start | bytes 2949128 | tf_op jit(solution)/shard_map/ppermute | solution.py:695
  57.3 4.6 %collective-permute-done.5 = bf16[384,1280]{1,0:T(8,128)(2,1)} collective-permute-done((bf16[384,1280]{1,0:T(8,128)(2,1)}, bf16[384,1280]{1,0:T(8,128)(2,1)}, u32[]{:S(2)}, u32[]{:S(2)}) %collective-permute-start.5) | collective-permute-done | bytes 983072 | tf_op jit(solution)/shard_map/ppermute | solution.py:695
  63.2 2.8 %collective-permute-start.16 = (bf16[192,1280]{1,0:T(8,128)(2,1)S(1)}, bf16[192,1280]{1,0:T(8,128)(2,1)S(1)}, u32[]{:S(2)}, u32[]{:S(2)}) collective-permute-start(bf16[192,1280]{1,0:T(8,128)(2,1)S(1)} %get-tuple-element.203), channel_id=1, source_target_pairs={{0,16},{2,18},{4,20},{6,22},{8,24},{10,26},{12,28},{14,30},{16,0},... | collective-permute-start | bytes 1474568 | tf_op jit(solution)/shard_map/ppermute | solution.py:695
  66.1 7.0 %attention_backward.2 = (bf16[384,1024]{1,0:T(8,128)(2,1)S(1)}, bf16[384,1024]{1,0:T(8,128)(2,1)S(1)}, bf16[384,1024]{1,0:T(8,128)(2,1)S(1)}) custom-call(s32[2]{0:T(128)S(1)} %pad_add_fusion.info_ref, s32[4]{0:T(128)S(1)} %bitcast.11, bf16[384,1024]{1,0:T(8,128)(2,1)S(1)} %get-tuple-element.112.q_ref, bf16[384,1024]{1,0:T(8,128)(2,1)S(1)} %get-tuple-element.113.k_ref, ...), custom_call_target="tpu_custom_call" | custom-call | flops 240000000 | bytes 47185 | tf_op jit(solution)/shard_map/attention_backward/pallas_call | solution.py:32
  73.3 1.6 %collective-permute-start.12 = (bf16[192,1280]{1,0:T(8,128)(2,1)S(1)}, bf16[192,1280]{1,0:T(8,128)(2,1)S(1)}, u32[]{:S(2)}, u32[]{:S(2)}) collective-permute-start(bf16[192,1280]{1,0:T(8,128)(2,1)S(1)} %get-tuple-element.205), channel_id=1, source_target_pairs={{0,8},{2,10},{4,12},{6,14},{8,0},{10,2},{12,4},{14,6},{16,24},{18,... | collective-permute-start | bytes 1474568 | tf_op jit(solution)/shard_map/ppermute | solution.py:695
  74.9 6.7 %attention_backward.3 = (bf16[384,1024]{1,0:T(8,128)(2,1)S(1)}, bf16[384,1024]{1,0:T(8,128)(2,1)S(1)}, bf16[384,1024]{1,0:T(8,128)(2,1)S(1)}) custom-call(s32[2]{0:T(128)S(1)} %pad_add_fusion.info_ref, s32[4]{0:T(128)S(1)} %bitcast.12, bf16[384,1024]{1,0:T(8,128)(2,1)S(1)} %get-tuple-element.112.q_ref, ...), custom_call_target="tpu_custom_call", output_to_operand_aliasing={{0}: (11, {}), {1}: (12, {}), {2}: (13, {})} | custom-call | flops 240000000 | bytes 47185 | tf_op jit(solution)/shard_map/attention_backward/pallas_call | solution.py:32
  81.7 3.8 %project_grad.1 = (bf16[384,512]{1,0:T(8,128)(2,1)S(1)}, bf16[384,512]{1,0:T(8,128)(2,1)S(1)}, bf16[384,512]{1,0:T(8,128)(2,1)S(1)}, bf16[384,512]{1,0:T(8,128)(...) custom-call(s32[2]{0:T(128)S(1)} %pad_add_fusion.info_ref, ...), custom_call_target="tpu_custom_call" | custom-call | flops 36238784 | bytes 47185 | tf_op jit(solution)/shard_map/project_grad/pallas_call | solution.py:32
  85.4 1.6 %collective-permute-start.9 = (bf16[384,512]{1,0:T(8,128)(2,1)S(1)}, bf16[384,512]{1,0:T(8,128)(2,1)S(1)}, u32[]{:S(2)}, u32[]{:S(2)}) collective-permute-start(bf16[384,512]{1,0:T(8,128)(2,1)S(1)} %get-tuple-element.158), channel_id=1, source_target_pairs={{0,4},{2,6},{4,0},{6,2},{8,12},{10,14},{12,8},{14,10},{16,20},{18,... | collective-permute-start | bytes 1179656 | tf_op jit(solution)/shard_map/ppermute | solution.py:695
  87.7 1.5 %collective-permute-start.14 = (bf16[192,1280]{1,0:T(8,128)(2,1)S(1)}, bf16[192,1280]{1,0:T(8,128)(2,1)S(1)}, u32[]{:S(2)}, u32[]{:S(2)}) collective-permute-start(bf16[192,1280]{1,0:T(8,128)(2,1)S(1)} %get-tuple-element.201), channel_id=1, source_target_pairs={{0,2},{2,0},{4,6},{6,4},{8,10},{10,8},{12,14},{14,12},{16,18},{18,... | collective-permute-start | bytes 1474568 | tf_op jit(solution)/shard_map/ppermute | solution.py:695
  89.3 1.9 %stream_grad.2 = bf16[768,512]{1,0:T(8,128)(2,1)S(1)} custom-call(s32[2]{0:T(128)S(1)} %pad_add_fusion.info_ref, bf16[384,1024]{1,0:T(8,128)(2,1)S(1)} %get-tuple-element.172.dq_ref, bf16[384,1024]{1,0:T(8,128)(2,1)S(1)} %get-tuple-element.173.dk_ref, bf16[384,1024]{1,0:T(8,128)(2,1)S(1)} %get-tuple-element.174.dv_ref, ...), custom_call_target="tpu_custom_call" | custom-call | flops 18119392 | bytes 15728 | tf_op jit(solution)/shard_map/stream_grad/pallas_call | solution.py:32
  91.2 4.0 %collective-permute-done.9 = bf16[384,512]{1,0:T(8,128)(2,1)S(1)} collective-permute-done((bf16[384,512]{1,0:T(8,128)(2,1)S(1)}, bf16[384,512]{1,0:T(8,128)(2,1)S(1)}, u32[]{:S(2)}, u32[]{:S(2)}) %collective-permute-start.9) | collective-permute-done | bytes 393248 | tf_op jit(solution)/shard_map/ppermute | solution.py:695
  98.4 1.6 %collective-permute-start.27 = (bf16[96,1280]{1,0:T(8,128)(2,1)S(1)}, bf16[96,1280]{1,0:T(8,128)(2,1)S(1)}, u32[]{:S(2)}, u32[]{:S(2)}) collective-permute-start(bf16[96,1280]{1,0:T(8,128)(2,1)S(1)} %get-tuple-element.207), channel_id=1, source_target_pairs={{0,2},{2,0},{4,6},{6,4},{8,10},{10,8},{12,14},{14,12},{16,18},{18,... | collective-permute-start | bytes 737288 | tf_op jit(solution)/shard_map/ppermute | solution.py:695
  100.0 3.8 %collective-permute-done.13 = bf16[96,1280]{1,0:T(8,128)(2,1)S(1)} collective-permute-done((bf16[96,1280]{1,0:T(8,128)(2,1)S(1)}, bf16[96,1280]{1,0:T(8,128)(2,1)S(1)}, u32[]{:S(2)}, u32[]{:S(2)}) %collective-permute-start.13) | collective-permute-done | bytes 245792 | tf_op jit(solution)/shard_map/ppermute | solution.py:695
  105.4 3.1 %stream_grad.3 = bf16[512,768]{1,0:T(8,128)(2,1)} custom-call(s32[2]{0:T(128)S(1)} %pad_add_fusion.info_ref, bf16[384,1024]{1,0:T(8,128)(2,1)S(1)} %get-tuple-element.172.dq_ref, bf16[384,1024]{1,0:T(8,128)(2,1)S(1)} %get-tuple-element.173.dk_ref, bf16[384,1024]{1,0:T(8,128)(2,1)S(1)} %get-tuple-element.174.dv_ref, ...), custom_call_target="tpu_custom_call" | custom-call | flops 18119392 | bytes 15728 | tf_op jit(solution)/shard_map/stream_grad/pallas_call | solution.py:32
  111.5 4.0 %collective-permute-done.18 = bf16[416,512]{1,0:T(8,128)(2,1)S(1)} collective-permute-done((bf16[416,512]{1,0:T(8,128)(2,1)S(1)}, bf16[416,512]{1,0:T(8,128)(2,1)S(1)}, u32[]{:S(2)}, u32[]{:S(2)}) %collective-permute-start.18) | collective-permute-done | bytes 426016 | tf_op jit(solution)/shard_map/ppermute | solution.py:695
  117.3 2.6 %collective-permute-start.22 = (bf16[96,512]{1,0:T(8,128)(2,1)S(1)}, bf16[96,512]{1,0:T(8,128)(2,1)S(1)}, u32[]{:S(2)}, u32[]{:S(2)}) collective-permute-start(bf16[96,512]{1,0:T(8,128)(2,1)S(1)} %get-tuple-element.225), channel_id=1, source_target_pairs={{0,8},{2,10},{4,12},{6,14},{8,0},{10,2},{12,4},{14,6},{16,24},{18,... | collective-permute-start | bytes 294920 | tf_op jit(solution)/shard_map/ppermute | solution.py:695
  122.8 2.8 %collective-permute-done.22 = bf16[96,512]{1,0:T(8,128)(2,1)S(1)} collective-permute-done((bf16[96,512]{1,0:T(8,128)(2,1)S(1)}, bf16[96,512]{1,0:T(8,128)(2,1)S(1)}, u32[]{:S(2)}, u32[]{:S(2)}) %collective-permute-start.22) | collective-permute-done | bytes 98336 | tf_op jit(solution)/shard_map/ppermute | solution.py:695
  127.2 2.7 %collective-permute-done.19 = bf16[224,512]{1,0:T(8,128)(2,1)S(1)} collective-permute-done((bf16[224,512]{1,0:T(8,128)(2,1)S(1)}, bf16[224,512]{1,0:T(8,128)(2,1)S(1)}, u32[]{:S(2)}, u32[]{:S(2)}) %collective-permute-start.19) | collective-permute-done | bytes 229408 | tf_op jit(solution)/shard_map/ppermute | solution.py:695
  132.1 2.9 %collective-permute-done.20 = bf16[128,512]{1,0:T(8,128)(2,1)S(1)} collective-permute-done((bf16[128,512]{1,0:T(8,128)(2,1)S(1)}, bf16[128,512]{1,0:T(8,128)(2,1)S(1)}, u32[]{:S(2)}, u32[]{:S(2)}) %collective-permute-start.20) | collective-permute-done | bytes 131104 | tf_op jit(solution)/shard_map/ppermute | solution.py:695
  135.5 7.9 %collective-permute-done.26.came_ref = bf16[176,512]{1,0:T(8,128)(2,1)S(1)} collective-permute-done((bf16[176,512]{1,0:T(8,128)(2,1)S(1)}, bf16[176,512]{1,0:T(8,128)(2,1)S(1)}, u32[]{:S(2)}, u32[]{:S(2)}) %collective-permute-start.26) | collective-permute-done | bytes 180256 | tf_op jit(solution)/shard_map/ppermute | solution.py:695
  (106 shorter events, 24.4 us)
Async XLA Ops:
  0.6 4.8 %collective-permute-start = (bf16[512,768]{1,0:T(8,128)(2,1)}, bf16[512,768]{1,0:T(8,128)(2,1)S(1)}, u32[]{:S(2)}, u32[]{:S(2)}) collective-permute-start(bf16[512,768]{1,0:T(8,128)(2,1)} %x_ref.1), channel_id=1, source_target_pairs={{0,1},{1,0},{2,3},{3,2},{4,5},{5,4},{6,7},{7,6},{8,9},{9,8},{10,11... | collective-permute-start | bytes 2359304 | tf_op jit(solution)/shard_map/ppermute | solution.py:690
  1.3 14.5 %copy-start.1 = (bf16[768,2560]{1,0:T(8,128)(2,1)S(1)}, bf16[768,2560]{1,0:T(8,128)(2,1)}, u32[]{:S(2)}) copy-start(bf16[768,2560]{1,0:T(8,128)(2,1)} %wg_ref.3) | copy-start | bytes 11796484
  1.3 14.5 %copy-start.2 = (bf16[768,2560]{1,0:T(8,128)(2,1)S(1)}, bf16[768,2560]{1,0:T(8,128)(2,1)}, u32[]{:S(2)}) copy-start(bf16[768,2560]{1,0:T(8,128)(2,1)} %wu_ref.3) | copy-start | bytes 11796484
  14.0 1.8 %collective-permute-start.1 = (bf16[384,512]{1,0:T(8,128)(2,1)S(1)}, bf16[384,512]{1,0:T(8,128)(2,1)S(1)}, u32[]{:S(2)}, u32[]{:S(2)}) collective-permute-start(bf16[384,512]{1,0:T(8,128)(2,1)S(1)} %get-tuple-element.110), channel_id=1, source_target_pairs={{0,1},{1,0},{2,3},{3,2},{4,5},{5,4},{6,7},{7,6},{8,9},{9,8},{10,11... | collective-permute-start | bytes 1179656 | tf_op jit(solution)/shard_map/ppermute | solution.py:690
  29.0 4.8 %collective-permute-start.2 = (bf16[768,1280]{1,0:T(8,128)(2,1)S(1)}, bf16[768,1280]{1,0:T(8,128)(2,1)S(1)}, u32[]{:S(2)}, u32[]{:S(2)}) collective-permute-start(bf16[768,1280]{1,0:T(8,128)(2,1)S(1)} %weight_away.1), channel_id=1, source_target_pairs={{0,1},{1,0},{2,3},{3,2},{4,5},{5,4},{6,7},{7,6},{8,9},{9,8},{10,11... | collective-permute-start | bytes 5898248 | tf_op jit(solution)/shard_map/ppermute | solution.py:690
  33.2 8.2 %collective-permute-start.3 = (bf16[768,1280]{1,0:T(8,128)(2,1)S(1)}, bf16[768,1280]{1,0:T(8,128)(2,1)S(1)}, u32[]{:S(2)}, u32[]{:S(2)}) collective-permute-start(bf16[768,1280]{1,0:T(8,128)(2,1)S(1)} %get-tuple-element.123), channel_id=1, source_target_pairs={{0,1},{1,0},{2,3},{3,2},{4,5},{5,4},{6,7},{7,6},{8,9},{9,8},{10,11... | collective-permute-start | bytes 5898248 | tf_op jit(solution)/shard_map/ppermute | solution.py:690
  33.7 19.1 %collective-permute-start.4 = (bf16[768,1280]{1,0:T(8,128)(2,1)S(1)}, bf16[768,1280]{1,0:T(8,128)(2,1)S(1)}, u32[]{:S(2)}, u32[]{:S(2)}) collective-permute-start(bf16[768,1280]{1,0:T(8,128)(2,1)S(1)} %get-tuple-element.140), channel_id=1, source_target_pairs={{0,1},{1,0},{2,3},{3,2},{4,5},{5,4},{6,7},{7,6},{8,9},{9,8},{10,11... | collective-permute-start | bytes 5898248 | tf_op jit(solution)/shard_map/ppermute | solution.py:690
  36.5 25.3 %collective-permute-start.5 = (bf16[384,1280]{1,0:T(8,128)(2,1)}, bf16[384,1280]{1,0:T(8,128)(2,1)}, u32[]{:S(2)}, u32[]{:S(2)}) collective-permute-start(bf16[384,1280]{1,0:T(8,128)(2,1)} %get-tuple-element.125), channel_id=1, source_target_pairs={{0,8},{2,10},{4,12},{6,14},{8,0},{10,2},{12,4},{14,6},{16,24},{18,... | collective-permute-start | bytes 2949128 | tf_op jit(solution)/shard_map/ppermute | solution.py:695
  43.2 29.8 %collective-permute-start.7 = (bf16[384,1280]{1,0:T(8,128)(2,1)S(1)}, bf16[384,1280]{1,0:T(8,128)(2,1)S(1)}, u32[]{:S(2)}, u32[]{:S(2)}) collective-permute-start(bf16[384,1280]{1,0:T(8,128)(2,1)S(1)} %get-tuple-element.130), channel_id=1, source_target_pairs={{0,2},{2,0},{4,6},{6,4},{8,10},{10,8},{12,14},{14,12},{16,18},{18,... | collective-permute-start | bytes 2949128 | tf_op jit(solution)/shard_map/ppermute | solution.py:695
  52.2 4.9 %collective-permute-start.17 = (f32[16,512]{1,0:T(8,128)S(1)}, f32[16,512]{1,0:T(8,128)S(1)}, u32[]{:S(2)}, u32[]{:S(2)}) collective-permute-start(f32[16,512]{1,0:T(8,128)S(1)} %get-tuple-element.181), channel_id=1, source_target_pairs={{0,1},{1,0},{2,3},{3,2},{4,5},{5,4},{6,7},{7,6},{8,9},{9,8},{10,11... | collective-permute-start | bytes 98312 | tf_op jit(solution)/shard_map/ppermute | solution.py:690
  52.3 13.8 %collective-permute-start.6 = (bf16[384,512]{1,0:T(8,128)(2,1)S(1)}, bf16[384,512]{1,0:T(8,128)(2,1)S(1)}, u32[]{:S(2)}, u32[]{:S(2)}) collective-permute-start(bf16[384,512]{1,0:T(8,128)(2,1)S(1)} %get-tuple-element.138), channel_id=1, source_target_pairs={{0,1},{1,0},{2,3},{3,2},{4,5},{5,4},{6,7},{7,6},{8,9},{9,8},{10,11... | collective-permute-start | bytes 1179656 | tf_op jit(solution)/shard_map/ppermute | solution.py:690
  54.6 32.9 %collective-permute-start.10 = (bf16[384,1280]{1,0:T(8,128)(2,1)S(1)}, bf16[384,1280]{1,0:T(8,128)(2,1)S(1)}, u32[]{:S(2)}, u32[]{:S(2)}) collective-permute-start(bf16[384,1280]{1,0:T(8,128)(2,1)S(1)} %get-tuple-element.141), channel_id=1, source_target_pairs={{0,4},{2,6},{4,0},{6,2},{8,12},{10,14},{12,8},{14,10},{16,20},{18,... | collective-permute-start | bytes 2949128 | tf_op jit(solution)/shard_map/ppermute | solution.py:695
  57.2 24.5 %collective-permute-start.8 = (bf16[768,384]{1,0:T(8,128)(2,1)S(1)}, bf16[768,384]{1,0:T(8,128)(2,1)S(1)}, u32[]{:S(2)}, u32[]{:S(2)}) collective-permute-start(bf16[768,384]{1,0:T(8,128)(2,1)S(1)} %get-tuple-element.143), channel_id=1, source_target_pairs={{0,1},{1,0},{2,3},{3,2},{4,5},{5,4},{6,7},{7,6},{8,9},{9,8},{10,11... | collective-permute-start | bytes 1769480 | tf_op jit(solution)/shard_map/ppermute | solution.py:690
  63.2 35.0 %collective-permute-start.16 = (bf16[192,1280]{1,0:T(8,128)(2,1)S(1)}, bf16[192,1280]{1,0:T(8,128)(2,1)S(1)}, u32[]{:S(2)}, u32[]{:S(2)}) collective-permute-start(bf16[192,1280]{1,0:T(8,128)(2,1)S(1)} %get-tuple-element.203), channel_id=1, source_target_pairs={{0,16},{2,18},{4,20},{6,22},{8,24},{10,26},{12,28},{14,30},{16,0},... | collective-permute-start | bytes 1474568 | tf_op jit(solution)/shard_map/ppermute | solution.py:695
  73.3 23.4 %collective-permute-start.12 = (bf16[192,1280]{1,0:T(8,128)(2,1)S(1)}, bf16[192,1280]{1,0:T(8,128)(2,1)S(1)}, u32[]{:S(2)}, u32[]{:S(2)}) collective-permute-start(bf16[192,1280]{1,0:T(8,128)(2,1)S(1)} %get-tuple-element.205), channel_id=1, source_target_pairs={{0,8},{2,10},{4,12},{6,14},{8,0},{10,2},{12,4},{14,6},{16,24},{18,... | collective-permute-start | bytes 1474568 | tf_op jit(solution)/shard_map/ppermute | solution.py:695
  85.4 9.8 %collective-permute-start.9 = (bf16[384,512]{1,0:T(8,128)(2,1)S(1)}, bf16[384,512]{1,0:T(8,128)(2,1)S(1)}, u32[]{:S(2)}, u32[]{:S(2)}) collective-permute-start(bf16[384,512]{1,0:T(8,128)(2,1)S(1)} %get-tuple-element.158), channel_id=1, source_target_pairs={{0,4},{2,6},{4,0},{6,2},{8,12},{10,14},{12,8},{14,10},{16,20},{18,... | collective-permute-start | bytes 1179656 | tf_op jit(solution)/shard_map/ppermute | solution.py:695
  87.0 23.8 %collective-permute-start.23 = (bf16[384,512]{1,0:T(8,128)(2,1)S(1)}, bf16[384,512]{1,0:T(8,128)(2,1)S(1)}, u32[]{:S(2)}, u32[]{:S(2)}) collective-permute-start(bf16[384,512]{1,0:T(8,128)(2,1)S(1)} %get-tuple-element.169), channel_id=1, source_target_pairs={{0,8},{2,10},{4,12},{6,14},{8,0},{10,2},{12,4},{14,6},{16,24},{18,... | collective-permute-start | bytes 1179656 | tf_op jit(solution)/shard_map/ppermute | solution.py:695
  87.7 20.8 %collective-permute-start.14 = (bf16[192,1280]{1,0:T(8,128)(2,1)S(1)}, bf16[192,1280]{1,0:T(8,128)(2,1)S(1)}, u32[]{:S(2)}, u32[]{:S(2)}) collective-permute-start(bf16[192,1280]{1,0:T(8,128)(2,1)S(1)} %get-tuple-element.201), channel_id=1, source_target_pairs={{0,2},{2,0},{4,6},{6,4},{8,10},{10,8},{12,14},{14,12},{16,18},{18,... | collective-permute-start | bytes 1474568 | tf_op jit(solution)/shard_map/ppermute | solution.py:695
  95.2 10.1 %collective-permute-start.11 = (bf16[768,512]{1,0:T(8,128)(2,1)S(1)}, bf16[768,512]{1,0:T(8,128)(2,1)S(1)}, u32[]{:S(2)}, u32[]{:S(2)}) collective-permute-start(bf16[768,512]{1,0:T(8,128)(2,1)S(1)} %stream_grad.2), channel_id=1, source_target_pairs={{0,1},{1,0},{2,3},{3,2},{4,5},{5,4},{6,7},{7,6},{8,9},{9,8},{10,11... | collective-permute-start | bytes 2359304 | tf_op jit(solution)/shard_map/ppermute | solution.py:690
  96.8 7.0 %collective-permute-start.13 = (bf16[96,1280]{1,0:T(8,128)(2,1)S(1)}, bf16[96,1280]{1,0:T(8,128)(2,1)S(1)}, u32[]{:S(2)}, u32[]{:S(2)}) collective-permute-start(bf16[96,1280]{1,0:T(8,128)(2,1)S(1)} %get-tuple-element.209), channel_id=1, source_target_pairs={{0,4},{2,6},{4,0},{6,2},{8,12},{10,14},{12,8},{14,10},{16,20},{18,... | collective-permute-start | bytes 737288 | tf_op jit(solution)/shard_map/ppermute | solution.py:695
  98.4 23.1 %collective-permute-start.27 = (bf16[96,1280]{1,0:T(8,128)(2,1)S(1)}, bf16[96,1280]{1,0:T(8,128)(2,1)S(1)}, u32[]{:S(2)}, u32[]{:S(2)}) collective-permute-start(bf16[96,1280]{1,0:T(8,128)(2,1)S(1)} %get-tuple-element.207), channel_id=1, source_target_pairs={{0,2},{2,0},{4,6},{6,4},{8,10},{10,8},{12,14},{14,12},{16,18},{18,... | collective-permute-start | bytes 737288 | tf_op jit(solution)/shard_map/ppermute | solution.py:695
  103.8 11.7 %collective-permute-start.18 = (bf16[416,512]{1,0:T(8,128)(2,1)S(1)}, bf16[416,512]{1,0:T(8,128)(2,1)S(1)}, u32[]{:S(2)}, u32[]{:S(2)}) collective-permute-start(bf16[416,512]{1,0:T(8,128)(2,1)S(1)} %pad_maximum_fusion), channel_id=1, source_target_pairs={{0,4},{2,6},{4,0},{6,2},{8,12},{10,14},{12,8},{14,10},{16,20},{18,... | collective-permute-start | bytes 1277960 | tf_op jit(solution)/shard_map/ppermute | solution.py:695
  108.6 6.9 %collective-permute-start.15 = (bf16[96,1280]{1,0:T(8,128)(2,1)S(1)}, bf16[96,1280]{1,0:T(8,128)(2,1)S(1)}, u32[]{:S(2)}, u32[]{:S(2)}) collective-permute-start(bf16[96,1280]{1,0:T(8,128)(2,1)S(1)} %get-tuple-element.211), channel_id=1, source_target_pairs={{0,8},{2,10},{4,12},{6,14},{8,0},{10,2},{12,4},{14,6},{16,24},{18,... | collective-permute-start | bytes 737288 | tf_op jit(solution)/shard_map/ppermute | solution.py:695
  109.3 7.9 %collective-permute-start.21 = (bf16[192,512]{1,0:T(8,128)(2,1)S(1)}, bf16[192,512]{1,0:T(8,128)(2,1)S(1)}, u32[]{:S(2)}, u32[]{:S(2)}) collective-permute-start(bf16[192,512]{1,0:T(8,128)(2,1)S(1)} %get-tuple-element.217), channel_id=1, source_target_pairs={{0,2},{2,0},{4,6},{6,4},{8,10},{10,8},{12,14},{14,12},{16,18},{18,... | collective-permute-start | bytes 589832 | tf_op jit(solution)/shard_map/ppermute | solution.py:695
  110.9 9.0 %collective-permute-start.24 = (bf16[192,512]{1,0:T(8,128)(2,1)S(1)}, bf16[192,512]{1,0:T(8,128)(2,1)S(1)}, u32[]{:S(2)}, u32[]{:S(2)}) collective-permute-start(bf16[192,512]{1,0:T(8,128)(2,1)S(1)} %get-tuple-element.215), channel_id=1, source_target_pairs={{0,4},{2,6},{4,0},{6,2},{8,12},{10,14},{12,8},{14,10},{16,20},{18,... | collective-permute-start | bytes 589832 | tf_op jit(solution)/shard_map/ppermute | solution.py:695
  115.6 15.7 %collective-permute-start.29 = (bf16[96,1280]{1,0:T(8,128)(2,1)S(1)}, bf16[96,1280]{1,0:T(8,128)(2,1)S(1)}, u32[]{:S(2)}, u32[]{:S(2)}) collective-permute-start(bf16[96,1280]{1,0:T(8,128)(2,1)S(1)} %pad_maximum_fusion.1), channel_id=1, source_target_pairs={{0,16},{2,18},{4,20},{6,22},{8,24},{10,26},{12,28},{14,30},{16,0},... | collective-permute-start | bytes 737288 | tf_op jit(solution)/shard_map/ppermute | solution.py:695
  117.3 8.3 %collective-permute-start.22 = (bf16[96,512]{1,0:T(8,128)(2,1)S(1)}, bf16[96,512]{1,0:T(8,128)(2,1)S(1)}, u32[]{:S(2)}, u32[]{:S(2)}) collective-permute-start(bf16[96,512]{1,0:T(8,128)(2,1)S(1)} %get-tuple-element.225), channel_id=1, source_target_pairs={{0,8},{2,10},{4,12},{6,14},{8,0},{10,2},{12,4},{14,6},{16,24},{18,... | collective-permute-start | bytes 294920 | tf_op jit(solution)/shard_map/ppermute | solution.py:695
  119.9 5.7 %collective-permute-start.25 = (bf16[96,512]{1,0:T(8,128)(2,1)S(1)}, bf16[96,512]{1,0:T(8,128)(2,1)S(1)}, u32[]{:S(2)}, u32[]{:S(2)}) collective-permute-start(bf16[96,512]{1,0:T(8,128)(2,1)S(1)} %get-tuple-element.223), channel_id=1, source_target_pairs={{0,2},{2,0},{4,6},{6,4},{8,10},{10,8},{12,14},{14,12},{16,18},{18,... | collective-permute-start | bytes 294920 | tf_op jit(solution)/shard_map/ppermute | solution.py:695
  121.5 4.9 %collective-permute-start.28 = (bf16[48,1280]{1,0:T(8,128)(2,1)S(1)}, bf16[48,1280]{1,0:T(8,128)(2,1)S(1)}, u32[]{:S(2)}, u32[]{:S(2)}) collective-permute-start(bf16[48,1280]{1,0:T(8,128)(2,1)S(1)} %add_convert_fusion.20), channel_id=1, source_target_pairs={{0,4},{2,6},{4,0},{6,2},{8,12},{10,14},{12,8},{14,10},{16,20},{18,... | collective-permute-start | bytes 368648 | tf_op jit(solution)/shard_map/ppermute | solution.py:695
  121.6 8.3 %collective-permute-start.19 = (bf16[224,512]{1,0:T(8,128)(2,1)S(1)}, bf16[224,512]{1,0:T(8,128)(2,1)S(1)}, u32[]{:S(2)}, u32[]{:S(2)}) collective-permute-start(bf16[224,512]{1,0:T(8,128)(2,1)S(1)} %pad_maximum_fusion.2), channel_id=1, source_target_pairs={{0,8},{2,10},{4,12},{6,14},{8,0},{10,2},{12,4},{14,6},{16,24},{18,... | collective-permute-start | bytes 688136 | tf_op jit(solution)/shard_map/ppermute | solution.py:695
  130.0 5.0 %collective-permute-start.20 = (bf16[128,512]{1,0:T(8,128)(2,1)S(1)}, bf16[128,512]{1,0:T(8,128)(2,1)S(1)}, u32[]{:S(2)}, u32[]{:S(2)}) collective-permute-start(bf16[128,512]{1,0:T(8,128)(2,1)S(1)} %pad_maximum_fusion.3), channel_id=1, source_target_pairs={{0,2},{2,0},{4,6},{6,4},{8,10},{10,8},{12,14},{14,12},{16,18},{18,... | collective-permute-start | bytes 393224 | tf_op jit(solution)/shard_map/ppermute | solution.py:695
  135.2 8.2 %collective-permute-start.26 = (bf16[176,512]{1,0:T(8,128)(2,1)S(1)}, bf16[176,512]{1,0:T(8,128)(2,1)S(1)}, u32[]{:S(2)}, u32[]{:S(2)}) collective-permute-start(bf16[176,512]{1,0:T(8,128)(2,1)S(1)} %fusion.2), channel_id=1, source_target_pairs={{0,16},{2,18},{4,20},{6,22},{8,24},{10,26},{12,28},{14,30},{16,0},... | collective-permute-start | bytes 540680 | tf_op jit(solution)/shard_map/ppermute | solution.py:695
  (11 other events, 80.3 us)

commit v5 on v4

--- a/solution.py
+++ b/solution.py
@@ -21,7 +21,7 @@
 ROWS = 64
 SPANS = 4
 PAIR = 2
-PLAN = ((0,), (1,))
+PLAN = ((), (0, 1))
 MIB = 1 << 20
 EASE = 50
 ROOM = 8

time: 144 us -> 140 us (0.972)
  starting transfers between devices: 31.8 us -> 28.9 us
    ppermute x21, starting transfers between devices: 29.7 us -> 26.8 us  [swap_dp(): return lax.ppermute(value, 'dp', [(i, i ^ 1 << bit) for i in range(size)])]
  transfers between devices with their start and end apart: 30 -> 30, of which waited for: 11 -> 10; matrix products, arithmetic and copies ran while one was open for 3% -> 3% of each run, Pallas kernels for 33% -> 34%
where the time goes in v5:
time: 140 us
  Pallas kernels  69.7 us (50%)
  waiting for transfers between devices  35.4 us (25%)
  starting transfers between devices  28.9 us (21%)
  other arithmetic  4.74 us (3%)
    pallas_call x16, Pallas kernels, call(): pl.pallas_call(kernel, in_specs=[pl.BlockSpec(memory_space=pltpu.SMEM)] *...  65.5 us
    ppermute x21, waiting for transfers between devices, swap_dp(): return lax.ppermute(value, 'dp', [(i, i ^ 1 << bit) for i in range(size)])  33.7 us
    ppermute x21, starting transfers between devices, swap_dp(): return lax.ppermute(value, 'dp', [(i, i ^ 1 << bit) for i in range(size)])  26.8 us
    pallas_call x1, Pallas kernels, project_own(): pl.pallas_call(project_own_kernel, in_specs=[pl.BlockSpec(memory_space=pl...  4.16 us
    convert_element_type x18, other arithmetic, add(): (self.keep[low:high].astype(F32) + self.came[low:high].astype(F32)).astyp...  2.86 us
  transfers between devices with their start and end apart: 30, of which 10 were waited for; matrix products, arithmetic and copies ran while one was open for 3% of the time, Pallas kernels for 34%

profile of v5, /device:TPU:0, one launch (start us, length us, event | category | flops | bytes accessed | tf_op | source)
XLA Modules:
  0.0 140.0 jit_solution(1399283774999319485)
XLA Ops:
  1.3 4.2 %project_own.1 = (bf16[384,1024]{1,0:T(8,128)(2,1)S(1)}, bf16[384,1024]{1,0:T(8,128)(2,1)S(1)}, bf16[384,1024]{1,0:T(8,128)(2,1)S(1)}, bf16[1024,768]{1,0:T(8,12...) custom-call(s32[2]{0:T(128)S(1)} %pad_add_fusion.info_ref, ...), custom_call_target="tpu_custom_call" | custom-call | flops 4000000000 | bytes 8000000 | tf_op jit(solution)/shard_map/project_own/pallas_call | solution.py:146
  5.6 8.4 %attention_forward.1 = (bf16[384,1024]{1,0:T(8,128)(2,1)S(1)}, bf16[384,1024]{1,0:T(8,128)(2,1)S(1)}, bf16[384,1024]{1,0:T(8,128)(2,1)S(1)}, bf16[1024,768]{1,0:...) custom-call(s32[2]{0:T(128)S(1)} %pad_add_fusion.info_ref, ...), custom_call_target="tpu_custom_call", output_to_operand_aliasing={{0}: (2, {}), {1}: (3, {}), {2}: (4, {}), {3}: (5, {})} | custom-call | flops 300000000 | bytes 110755 | tf_op jit(solution)/shard_map/attention_forward/pallas_call | solution.py:32
  14.1 1.7 %collective-permute-done.1.came_ref = bf16[384,512]{1,0:T(8,128)(2,1)S(1)} collective-permute-done((bf16[384,512]{1,0:T(8,128)(2,1)S(1)}, bf16[384,512]{1,0:T(8,128)(2,1)S(1)}, u32[]{:S(2)}, u32[]{:S(2)}) %collective-permute-start.1) | collective-permute-done | bytes 393248 | tf_op jit(solution)/shard_map/ppermute | solution.py:690
  15.9 11.4 %ffn_forward.1 = (bf16[512,2560]{1,0:T(8,128)(2,1)S(1)}, bf16[512,2560]{1,0:T(8,128)(2,1)S(1)}, bf16[512,2560]{1,0:T(8,128)(2,1)S(1)}, bf16[512,768]{1,0:T(8,128...) custom-call(s32[2]{0:T(128)S(1)} %pad_add_fusion.info_ref, ...), custom_call_target="tpu_custom_call" | custom-call | flops 120795952 | bytes 283770 | tf_op jit(solution)/shard_map/ffn_forward/pallas_call | solution.py:32
  27.3 1.7 %weight_away.1 = bf16[768,1280]{1,0:T(8,128)(2,1)S(1)} custom-call(s32[2]{0:T(128)S(1)} %pad_add_fusion.info_ref, bf16[768,512]{1,0:T(8,128)(2,1)S(1)} %get-tuple-element.118.left_ref, bf16[512,2560]{1,0:T(8,128)(2,1)S(1)} %get-tuple-element.125.right_ref), custom_call_target="tpu_custom_call" | custom-call | flops 20132660 | bytes 39321 | tf_op jit(solution)/shard_map/weight_away/pallas_call | solution.py:32
  29.2 4.0 %swiglu_away.1 = (bf16[512,2560]{1,0:T(8,128)(2,1)S(1)}, bf16[512,2560]{1,0:T(8,128)(2,1)S(1)}, bf16[768,1280]{1,0:T(8,128)(2,1)S(1)}, bf16[768,1280]{1,0:T(8,128)(2,1)S(1)}) custom-call(s32[2]{0:T(128)S(1)} %pad_add_fusion.info_ref, bf16[512,768]{1,0:T(8,128)(2,1)S(1)} %get-tuple-element.127.dm_ref, bf16[2560,768]{1,0:T(8,128)(2,1)S(1)} %copy-done, ...), custom_call_target="tpu_custom_call" | custom-call | flops 60397976 | bytes 183500 | tf_op jit(solution)/shard_map/swiglu_away/pallas_call | solution.py:32
  33.8 2.7 %weight_mine.3 = (bf16[384,1280]{1,0:T(8,128)(2,1)S(1)}, bf16[384,1280]{1,0:T(8,128)(2,1)}) custom-call(s32[2]{0:T(128)S(1)} %pad_add_fusion.info_ref, bf16[768,512]{1,0:T(8,128)(2,1)S(1)} %get-tuple-element.118.left_ref, bf16[512,2560]{1,0:T(8,128)(2,1)S(1)} %get-tuple-element.125.right_ref, bf16[768,1280]{1,0:T(8,128)(2,1)S(1)} %collective-permute-done.2.rest_0_), custom_call_target="tpu_custom_call" | custom-call | flops 20132660 | bytes 39321 | tf_op jit(solution)/shard_map/weight_mine/pallas_call | solution.py:32
  36.5 3.0 %collective-permute-start.6 = (bf16[384,1280]{1,0:T(8,128)(2,1)}, bf16[384,1280]{1,0:T(8,128)(2,1)}, u32[]{:S(2)}, u32[]{:S(2)}) collective-permute-start(bf16[384,1280]{1,0:T(8,128)(2,1)} %get-tuple-element.126), channel_id=1, source_target_pairs={{0,8},{2,10},{4,12},{6,14},{8,0},{10,2},{12,4},{14,6},{16,24},{18,... | collective-permute-start | bytes 2949128 | tf_op jit(solution)/shard_map/ppermute | solution.py:695
  39.5 2.0 %swiglu_mine.1 = (bf16[512,2560]{1,0:T(8,128)(2,1)S(1)}, bf16[512,2560]{1,0:T(8,128)(2,1)S(1)}) custom-call(s32[2]{0:T(128)S(1)} %pad_add_fusion.info_ref, bf16[512,768]{1,0:T(8,128)(2,1)S(1)} %get-tuple-element.127.dm_ref, bf16[2560,768]{1,0:T(8,128)(2,1)S(1)} %copy-done, ...), custom_call_target="tpu_custom_call", output_to_operand_aliasing={{0}: (5, {}), {1}: (6, {})} | custom-call | flops 20132660 | bytes 104857 | tf_op jit(solution)/shard_map/swiglu_mine/pallas_call | solution.py:32
  41.5 1.7 %weight_mine.4 = (bf16[384,1280]{1,0:T(8,128)(2,1)S(1)}, bf16[384,1280]{1,0:T(8,128)(2,1)S(1)}) custom-call(s32[2]{0:T(128)S(1)} %pad_add_fusion.info_ref, bf16[768,512]{1,0:T(8,128)(2,1)S(1)} %get-tuple-element.140.hbt_ref.left_ref, bf16[512,2560]{1,0:T(8,128)(2,1)S(1)} %get-tuple-element.132.right_ref.dgt_ref, ...), custom_call_target="tpu_custom_call" | custom-call | flops 20132660 | bytes 39321 | tf_op jit(solution)/shard_map/weight_mine/pallas_call | solution.py:32
  43.2 1.5 %collective-permute-start.7 = (bf16[384,1280]{1,0:T(8,128)(2,1)S(1)}, bf16[384,1280]{1,0:T(8,128)(2,1)S(1)}, u32[]{:S(2)}, u32[]{:S(2)}) collective-permute-start(bf16[384,1280]{1,0:T(8,128)(2,1)S(1)} %get-tuple-element.131), channel_id=1, source_target_pairs={{0,2},{2,0},{4,6},{6,4},{8,10},{10,8},{12,14},{14,12},{16,18},{18,... | collective-permute-start | bytes 2949128 | tf_op jit(solution)/shard_map/ppermute | solution.py:695
  44.8 7.4 %norm_one_back.1 = (f32[512,768]{1,0:T(8,128)S(1)}, bf16[768,512]{1,0:T(8,128)(2,1)S(1)}, bf16[384,512]{1,0:T(8,128)(2,1)S(1)}, bf16[384,512]{1,0:T(8,128)(2,1)S(1)}, f32[16,512]{1,0:T(8,128)S(1)}) custom-call(s32[2]{0:T(128)S(1)} %pad_add_fusion.info_ref, bf16[512,2560]{1,0:T(8,128)(2,1)S(1)} %get-tuple-element.132.right_ref.dgt_ref, ...), custom_call_target="tpu_custom_call" | custom-call | flops 80530640 | bytes 63569 | tf_op jit(solution)/shard_map/norm_one_back/pallas_call | solution.py:32
  52.8 1.7 %weight_mine.5 = (bf16[384,1280]{1,0:T(8,128)(2,1)S(1)}, bf16[384,1280]{1,0:T(8,128)(2,1)S(1)}) custom-call(s32[2]{0:T(128)S(1)} %pad_add_fusion.info_ref, bf16[768,512]{1,0:T(8,128)(2,1)S(1)} %get-tuple-element.140.hbt_ref.left_ref, bf16[512,2560]{1,0:T(8,128)(2,1)S(1)} %get-tuple-element.133.dup_ref.right_ref, ...), custom_call_target="tpu_custom_call" | custom-call | flops 20132660 | bytes 39321 | tf_op jit(solution)/shard_map/weight_mine/pallas_call | solution.py:32
  55.7 1.6 %collective-permute-start.10 = (bf16[384,1280]{1,0:T(8,128)(2,1)S(1)}, bf16[384,1280]{1,0:T(8,128)(2,1)S(1)}, u32[]{:S(2)}, u32[]{:S(2)}) collective-permute-start(bf16[384,1280]{1,0:T(8,128)(2,1)S(1)} %get-tuple-element.142), channel_id=1, source_target_pairs={{0,4},{2,6},{4,0},{6,2},{8,12},{10,14},{12,8},{14,10},{16,20},{18,... | collective-permute-start | bytes 2949128 | tf_op jit(solution)/shard_map/ppermute | solution.py:695
  57.3 7.0 %attention_backward.2 = (bf16[384,1024]{1,0:T(8,128)(2,1)S(1)}, bf16[384,1024]{1,0:T(8,128)(2,1)S(1)}, bf16[384,1024]{1,0:T(8,128)(2,1)S(1)}) custom-call(s32[2]{0:T(128)S(1)} %pad_add_fusion.info_ref, s32[4]{0:T(128)S(1)} %bitcast.11, bf16[384,1024]{1,0:T(8,128)(2,1)S(1)} %get-tuple-element.113.q_ref, bf16[384,1024]{1,0:T(8,128)(2,1)S(1)} %get-tuple-element.114.k_ref, ...), custom_call_target="tpu_custom_call" | custom-call | flops 240000000 | bytes 47185 | tf_op jit(solution)/shard_map/attention_backward/pallas_call | solution.py:32
  65.6 2.6 %collective-permute-start.16 = (bf16[192,1280]{1,0:T(8,128)(2,1)S(1)}, bf16[192,1280]{1,0:T(8,128)(2,1)S(1)}, u32[]{:S(2)}, u32[]{:S(2)}) collective-permute-start(bf16[192,1280]{1,0:T(8,128)(2,1)S(1)} %get-tuple-element.205), channel_id=1, source_target_pairs={{0,16},{2,18},{4,20},{6,22},{8,24},{10,26},{12,28},{14,30},{16,0},... | collective-permute-start | bytes 1474568 | tf_op jit(solution)/shard_map/ppermute | solution.py:695
  69.1 6.7 %attention_backward.3 = (bf16[384,1024]{1,0:T(8,128)(2,1)S(1)}, bf16[384,1024]{1,0:T(8,128)(2,1)S(1)}, bf16[384,1024]{1,0:T(8,128)(2,1)S(1)}) custom-call(s32[2]{0:T(128)S(1)} %pad_add_fusion.info_ref, s32[4]{0:T(128)S(1)} %bitcast.12, bf16[384,1024]{1,0:T(8,128)(2,1)S(1)} %get-tuple-element.113.q_ref, ...), custom_call_target="tpu_custom_call", output_to_operand_aliasing={{0}: (11, {}), {1}: (12, {}), {2}: (13, {})} | custom-call | flops 240000000 | bytes 47185 | tf_op jit(solution)/shard_map/attention_backward/pallas_call | solution.py:32
  75.8 3.8 %project_grad.1 = (bf16[384,512]{1,0:T(8,128)(2,1)S(1)}, bf16[384,512]{1,0:T(8,128)(2,1)S(1)}, bf16[384,512]{1,0:T(8,128)(2,1)S(1)}, bf16[384,512]{1,0:T(8,128)(...) custom-call(s32[2]{0:T(128)S(1)} %pad_add_fusion.info_ref, ...), custom_call_target="tpu_custom_call" | custom-call | flops 36238784 | bytes 47185 | tf_op jit(solution)/shard_map/project_grad/pallas_call | solution.py:32
  80.2 1.6 %collective-permute-start.23 = (bf16[384,512]{1,0:T(8,128)(2,1)S(1)}, bf16[384,512]{1,0:T(8,128)(2,1)S(1)}, u32[]{:S(2)}, u32[]{:S(2)}) collective-permute-start(bf16[384,512]{1,0:T(8,128)(2,1)S(1)} %get-tuple-element.171), channel_id=1, source_target_pairs={{0,8},{2,10},{4,12},{6,14},{8,0},{10,2},{12,4},{14,6},{16,24},{18,... | collective-permute-start | bytes 1179656 | tf_op jit(solution)/shard_map/ppermute | solution.py:695
  83.1 1.9 %stream_grad.2 = bf16[768,512]{1,0:T(8,128)(2,1)S(1)} custom-call(s32[2]{0:T(128)S(1)} %pad_add_fusion.info_ref, bf16[384,1024]{1,0:T(8,128)(2,1)S(1)} %get-tuple-element.174.dq_ref, bf16[384,1024]{1,0:T(8,128)(2,1)S(1)} %get-tuple-element.175.dk_ref, bf16[384,1024]{1,0:T(8,128)(2,1)S(1)} %get-tuple-element.176.dv_ref, ...), custom_call_target="tpu_custom_call" | custom-call | flops 18119392 | bytes 15728 | tf_op jit(solution)/shard_map/stream_grad/pallas_call | solution.py:32
  85.0 5.2 %collective-permute-done.9 = bf16[384,512]{1,0:T(8,128)(2,1)S(1)} collective-permute-done((bf16[384,512]{1,0:T(8,128)(2,1)S(1)}, bf16[384,512]{1,0:T(8,128)(2,1)S(1)}, u32[]{:S(2)}, u32[]{:S(2)}) %collective-permute-start.9) | collective-permute-done | bytes 393248 | tf_op jit(solution)/shard_map/ppermute | solution.py:695
  90.2 2.9 %collective-permute-done.12 = bf16[192,1280]{1,0:T(8,128)(2,1)S(1)} collective-permute-done((bf16[192,1280]{1,0:T(8,128)(2,1)S(1)}, bf16[192,1280]{1,0:T(8,128)(2,1)S(1)}, u32[]{:S(2)}, u32[]{:S(2)}) %collective-permute-start.12) | collective-permute-done | bytes 491552 | tf_op jit(solution)/shard_map/ppermute | solution.py:695
  95.1 4.8 %collective-permute-done.13 = bf16[96,1280]{1,0:T(8,128)(2,1)S(1)} collective-permute-done((bf16[96,1280]{1,0:T(8,128)(2,1)S(1)}, bf16[96,1280]{1,0:T(8,128)(2,1)S(1)}, u32[]{:S(2)}, u32[]{:S(2)}) %collective-permute-start.13) | collective-permute-done | bytes 245792 | tf_op jit(solution)/shard_map/ppermute | solution.py:695
  100.4 3.1 %stream_grad.3 = bf16[512,768]{1,0:T(8,128)(2,1)} custom-call(s32[2]{0:T(128)S(1)} %pad_add_fusion.info_ref, bf16[384,1024]{1,0:T(8,128)(2,1)S(1)} %get-tuple-element.174.dq_ref, bf16[384,1024]{1,0:T(8,128)(2,1)S(1)} %get-tuple-element.175.dk_ref, bf16[384,1024]{1,0:T(8,128)(2,1)S(1)} %get-tuple-element.176.dv_ref, ...), custom_call_target="tpu_custom_call" | custom-call | flops 18119392 | bytes 15728 | tf_op jit(solution)/shard_map/stream_grad/pallas_call | solution.py:32
  106.7 4.1 %collective-permute-done.18 = bf16[416,512]{1,0:T(8,128)(2,1)S(1)} collective-permute-done((bf16[416,512]{1,0:T(8,128)(2,1)S(1)}, bf16[416,512]{1,0:T(8,128)(2,1)S(1)}, u32[]{:S(2)}, u32[]{:S(2)}) %collective-permute-start.18) | collective-permute-done | bytes 426016 | tf_op jit(solution)/shard_map/ppermute | solution.py:695
  113.9 1.4 %collective-permute-start.25 = (bf16[96,512]{1,0:T(8,128)(2,1)S(1)}, bf16[96,512]{1,0:T(8,128)(2,1)S(1)}, u32[]{:S(2)}, u32[]{:S(2)}) collective-permute-start(bf16[96,512]{1,0:T(8,128)(2,1)S(1)} %get-tuple-element.225), channel_id=1, source_target_pairs={{0,2},{2,0},{4,6},{6,4},{8,10},{10,8},{12,14},{14,12},{16,18},{18,... | collective-permute-start | bytes 294920 | tf_op jit(solution)/shard_map/ppermute | solution.py:695
  115.4 1.6 %collective-permute-start.28 = (bf16[48,1280]{1,0:T(8,128)(2,1)S(1)}, bf16[48,1280]{1,0:T(8,128)(2,1)S(1)}, u32[]{:S(2)}, u32[]{:S(2)}) collective-permute-start(bf16[48,1280]{1,0:T(8,128)(2,1)S(1)} %add_convert_fusion.20), channel_id=1, source_target_pairs={{0,4},{2,6},{4,0},{6,2},{8,12},{10,14},{12,8},{14,10},{16,20},{18,... | collective-permute-start | bytes 368648 | tf_op jit(solution)/shard_map/ppermute | solution.py:695
  117.5 2.7 %collective-permute-done.22 = bf16[96,512]{1,0:T(8,128)(2,1)S(1)} collective-permute-done((bf16[96,512]{1,0:T(8,128)(2,1)S(1)}, bf16[96,512]{1,0:T(8,128)(2,1)S(1)}, u32[]{:S(2)}, u32[]{:S(2)}) %collective-permute-start.22) | collective-permute-done | bytes 98336 | tf_op jit(solution)/shard_map/ppermute | solution.py:695
  121.1 3.8 %collective-permute-done.19 = bf16[224,512]{1,0:T(8,128)(2,1)S(1)} collective-permute-done((bf16[224,512]{1,0:T(8,128)(2,1)S(1)}, bf16[224,512]{1,0:T(8,128)(2,1)S(1)}, u32[]{:S(2)}, u32[]{:S(2)}) %collective-permute-start.19) | collective-permute-done | bytes 229408 | tf_op jit(solution)/shard_map/ppermute | solution.py:695
  126.7 3.3 %collective-permute-done.20 = bf16[128,512]{1,0:T(8,128)(2,1)S(1)} collective-permute-done((bf16[128,512]{1,0:T(8,128)(2,1)S(1)}, bf16[128,512]{1,0:T(8,128)(2,1)S(1)}, u32[]{:S(2)}, u32[]{:S(2)}) %collective-permute-start.20) | collective-permute-done | bytes 131104 | tf_op jit(solution)/shard_map/ppermute | solution.py:695
  130.1 2.2 %collective-permute-start.26 = (bf16[176,512]{1,0:T(8,128)(2,1)S(1)}, bf16[176,512]{1,0:T(8,128)(2,1)S(1)}, u32[]{:S(2)}, u32[]{:S(2)}) collective-permute-start(bf16[176,512]{1,0:T(8,128)(2,1)S(1)} %fusion.2), channel_id=1, source_target_pairs={{0,16},{2,18},{4,20},{6,22},{8,24},{10,26},{12,28},{14,30},{16,0},... | collective-permute-start | bytes 540680 | tf_op jit(solution)/shard_map/ppermute | solution.py:695
  132.3 6.8 %collective-permute-done.26.came_ref = bf16[176,512]{1,0:T(8,128)(2,1)S(1)} collective-permute-done((bf16[176,512]{1,0:T(8,128)(2,1)S(1)}, bf16[176,512]{1,0:T(8,128)(2,1)S(1)}, u32[]{:S(2)}, u32[]{:S(2)}) %collective-permute-start.26) | collective-permute-done | bytes 180256 | tf_op jit(solution)/shard_map/ppermute | solution.py:695
  (106 shorter events, 20.3 us)
Async XLA Ops:
  0.6 4.8 %collective-permute-start = (bf16[512,768]{1,0:T(8,128)(2,1)}, bf16[512,768]{1,0:T(8,128)(2,1)S(1)}, u32[]{:S(2)}, u32[]{:S(2)}) collective-permute-start(bf16[512,768]{1,0:T(8,128)(2,1)} %x_ref.1), channel_id=1, source_target_pairs={{0,1},{1,0},{2,3},{3,2},{4,5},{5,4},{6,7},{7,6},{8,9},{9,8},{10,11... | collective-permute-start | bytes 2359304 | tf_op jit(solution)/shard_map/ppermute | solution.py:690
  1.3 14.5 %copy-start.1 = (bf16[768,2560]{1,0:T(8,128)(2,1)S(1)}, bf16[768,2560]{1,0:T(8,128)(2,1)}, u32[]{:S(2)}) copy-start(bf16[768,2560]{1,0:T(8,128)(2,1)} %wg_ref.3) | copy-start | bytes 11796484
  1.3 14.5 %copy-start.2 = (bf16[768,2560]{1,0:T(8,128)(2,1)S(1)}, bf16[768,2560]{1,0:T(8,128)(2,1)}, u32[]{:S(2)}) copy-start(bf16[768,2560]{1,0:T(8,128)(2,1)} %wu_ref.3) | copy-start | bytes 11796484
  14.0 1.8 %collective-permute-start.1 = (bf16[384,512]{1,0:T(8,128)(2,1)S(1)}, bf16[384,512]{1,0:T(8,128)(2,1)S(1)}, u32[]{:S(2)}, u32[]{:S(2)}) collective-permute-start(bf16[384,512]{1,0:T(8,128)(2,1)S(1)} %get-tuple-element.111), channel_id=1, source_target_pairs={{0,1},{1,0},{2,3},{3,2},{4,5},{5,4},{6,7},{7,6},{8,9},{9,8},{10,11... | collective-permute-start | bytes 1179656 | tf_op jit(solution)/shard_map/ppermute | solution.py:690
  29.0 4.8 %collective-permute-start.2 = (bf16[768,1280]{1,0:T(8,128)(2,1)S(1)}, bf16[768,1280]{1,0:T(8,128)(2,1)S(1)}, u32[]{:S(2)}, u32[]{:S(2)}) collective-permute-start(bf16[768,1280]{1,0:T(8,128)(2,1)S(1)} %weight_away.1), channel_id=1, source_target_pairs={{0,1},{1,0},{2,3},{3,2},{4,5},{5,4},{6,7},{7,6},{8,9},{9,8},{10,11... | collective-permute-start | bytes 5898248 | tf_op jit(solution)/shard_map/ppermute | solution.py:690
  33.2 8.2 %collective-permute-start.3 = (bf16[768,1280]{1,0:T(8,128)(2,1)S(1)}, bf16[768,1280]{1,0:T(8,128)(2,1)S(1)}, u32[]{:S(2)}, u32[]{:S(2)}) collective-permute-start(bf16[768,1280]{1,0:T(8,128)(2,1)S(1)} %get-tuple-element.124), channel_id=1, source_target_pairs={{0,1},{1,0},{2,3},{3,2},{4,5},{5,4},{6,7},{7,6},{8,9},{9,8},{10,11... | collective-permute-start | bytes 5898248 | tf_op jit(solution)/shard_map/ppermute | solution.py:690
  33.7 19.1 %collective-permute-start.4 = (bf16[768,1280]{1,0:T(8,128)(2,1)S(1)}, bf16[768,1280]{1,0:T(8,128)(2,1)S(1)}, u32[]{:S(2)}, u32[]{:S(2)}) collective-permute-start(bf16[768,1280]{1,0:T(8,128)(2,1)S(1)} %get-tuple-element.141), channel_id=1, source_target_pairs={{0,1},{1,0},{2,3},{3,2},{4,5},{5,4},{6,7},{7,6},{8,9},{9,8},{10,11... | collective-permute-start | bytes 5898248 | tf_op jit(solution)/shard_map/ppermute | solution.py:690
  36.5 27.7 %collective-permute-start.6 = (bf16[384,1280]{1,0:T(8,128)(2,1)}, bf16[384,1280]{1,0:T(8,128)(2,1)}, u32[]{:S(2)}, u32[]{:S(2)}) collective-permute-start(bf16[384,1280]{1,0:T(8,128)(2,1)} %get-tuple-element.126), channel_id=1, source_target_pairs={{0,8},{2,10},{4,12},{6,14},{8,0},{10,2},{12,4},{14,6},{16,24},{18,... | collective-permute-start | bytes 2949128 | tf_op jit(solution)/shard_map/ppermute | solution.py:695
  43.2 25.1 %collective-permute-start.7 = (bf16[384,1280]{1,0:T(8,128)(2,1)S(1)}, bf16[384,1280]{1,0:T(8,128)(2,1)S(1)}, u32[]{:S(2)}, u32[]{:S(2)}) collective-permute-start(bf16[384,1280]{1,0:T(8,128)(2,1)S(1)} %get-tuple-element.131), channel_id=1, source_target_pairs={{0,2},{2,0},{4,6},{6,4},{8,10},{10,8},{12,14},{14,12},{16,18},{18,... | collective-permute-start | bytes 2949128 | tf_op jit(solution)/shard_map/ppermute | solution.py:695
  52.2 5.0 %collective-permute-start.5 = (bf16[384,512]{1,0:T(8,128)(2,1)S(1)}, bf16[384,512]{1,0:T(8,128)(2,1)S(1)}, u32[]{:S(2)}, u32[]{:S(2)}) collective-permute-start(bf16[384,512]{1,0:T(8,128)(2,1)S(1)} %get-tuple-element.139), channel_id=1, source_target_pairs={{0,1},{1,0},{2,3},{3,2},{4,5},{5,4},{6,7},{7,6},{8,9},{9,8},{10,11... | collective-permute-start | bytes 1179656 | tf_op jit(solution)/shard_map/ppermute | solution.py:690
  52.3 3.4 %collective-permute-start.17 = (f32[16,512]{1,0:T(8,128)S(1)}, f32[16,512]{1,0:T(8,128)S(1)}, u32[]{:S(2)}, u32[]{:S(2)}) collective-permute-start(f32[16,512]{1,0:T(8,128)S(1)} %get-tuple-element.183), channel_id=1, source_target_pairs={{0,1},{1,0},{2,3},{3,2},{4,5},{5,4},{6,7},{7,6},{8,9},{9,8},{10,11... | collective-permute-start | bytes 98312 | tf_op jit(solution)/shard_map/ppermute | solution.py:690
  55.5 20.3 %collective-permute-start.8 = (bf16[768,384]{1,0:T(8,128)(2,1)S(1)}, bf16[768,384]{1,0:T(8,128)(2,1)S(1)}, u32[]{:S(2)}, u32[]{:S(2)}) collective-permute-start(bf16[768,384]{1,0:T(8,128)(2,1)S(1)} %get-tuple-element.144), channel_id=1, source_target_pairs={{0,1},{1,0},{2,3},{3,2},{4,5},{5,4},{6,7},{7,6},{8,9},{9,8},{10,11... | collective-permute-start | bytes 1769480 | tf_op jit(solution)/shard_map/ppermute | solution.py:690
  55.7 26.1 %collective-permute-start.10 = (bf16[384,1280]{1,0:T(8,128)(2,1)S(1)}, bf16[384,1280]{1,0:T(8,128)(2,1)S(1)}, u32[]{:S(2)}, u32[]{:S(2)}) collective-permute-start(bf16[384,1280]{1,0:T(8,128)(2,1)S(1)} %get-tuple-element.142), channel_id=1, source_target_pairs={{0,4},{2,6},{4,0},{6,2},{8,12},{10,14},{12,8},{14,10},{16,20},{18,... | collective-permute-start | bytes 2949128 | tf_op jit(solution)/shard_map/ppermute | solution.py:695
  65.6 28.2 %collective-permute-start.16 = (bf16[192,1280]{1,0:T(8,128)(2,1)S(1)}, bf16[192,1280]{1,0:T(8,128)(2,1)S(1)}, u32[]{:S(2)}, u32[]{:S(2)}) collective-permute-start(bf16[192,1280]{1,0:T(8,128)(2,1)S(1)} %get-tuple-element.205), channel_id=1, source_target_pairs={{0,16},{2,18},{4,20},{6,22},{8,24},{10,26},{12,28},{14,30},{16,0},... | collective-permute-start | bytes 1474568 | tf_op jit(solution)/shard_map/ppermute | solution.py:695
  68.5 24.6 %collective-permute-start.12 = (bf16[192,1280]{1,0:T(8,128)(2,1)S(1)}, bf16[192,1280]{1,0:T(8,128)(2,1)S(1)}, u32[]{:S(2)}, u32[]{:S(2)}) collective-permute-start(bf16[192,1280]{1,0:T(8,128)(2,1)S(1)} %get-tuple-element.207), channel_id=1, source_target_pairs={{0,8},{2,10},{4,12},{6,14},{8,0},{10,2},{12,4},{14,6},{16,24},{18,... | collective-permute-start | bytes 1474568 | tf_op jit(solution)/shard_map/ppermute | solution.py:695
  79.6 10.7 %collective-permute-start.9 = (bf16[384,512]{1,0:T(8,128)(2,1)S(1)}, bf16[384,512]{1,0:T(8,128)(2,1)S(1)}, u32[]{:S(2)}, u32[]{:S(2)}) collective-permute-start(bf16[384,512]{1,0:T(8,128)(2,1)S(1)} %get-tuple-element.160), channel_id=1, source_target_pairs={{0,4},{2,6},{4,0},{6,2},{8,12},{10,14},{12,8},{14,10},{16,20},{18,... | collective-permute-start | bytes 1179656 | tf_op jit(solution)/shard_map/ppermute | solution.py:695
  80.2 25.5 %collective-permute-start.23 = (bf16[384,512]{1,0:T(8,128)(2,1)S(1)}, bf16[384,512]{1,0:T(8,128)(2,1)S(1)}, u32[]{:S(2)}, u32[]{:S(2)}) collective-permute-start(bf16[384,512]{1,0:T(8,128)(2,1)S(1)} %get-tuple-element.171), channel_id=1, source_target_pairs={{0,8},{2,10},{4,12},{6,14},{8,0},{10,2},{12,4},{14,6},{16,24},{18,... | collective-permute-start | bytes 1179656 | tf_op jit(solution)/shard_map/ppermute | solution.py:695
  82.0 21.6 %collective-permute-start.14 = (bf16[192,1280]{1,0:T(8,128)(2,1)S(1)}, bf16[192,1280]{1,0:T(8,128)(2,1)S(1)}, u32[]{:S(2)}, u32[]{:S(2)}) collective-permute-start(bf16[192,1280]{1,0:T(8,128)(2,1)S(1)} %get-tuple-element.203), channel_id=1, source_target_pairs={{0,2},{2,0},{4,6},{6,4},{8,10},{10,8},{12,14},{14,12},{16,18},{18,... | collective-permute-start | bytes 1474568 | tf_op jit(solution)/shard_map/ppermute | solution.py:695
  90.2 10.2 %collective-permute-start.11 = (bf16[768,512]{1,0:T(8,128)(2,1)S(1)}, bf16[768,512]{1,0:T(8,128)(2,1)S(1)}, u32[]{:S(2)}, u32[]{:S(2)}) collective-permute-start(bf16[768,512]{1,0:T(8,128)(2,1)S(1)} %stream_grad.2), channel_id=1, source_target_pairs={{0,1},{1,0},{2,3},{3,2},{4,5},{5,4},{6,7},{7,6},{8,9},{9,8},{10,11... | collective-permute-start | bytes 2359304 | tf_op jit(solution)/shard_map/ppermute | solution.py:690
  93.2 6.6 %collective-permute-start.13 = (bf16[96,1280]{1,0:T(8,128)(2,1)S(1)}, bf16[96,1280]{1,0:T(8,128)(2,1)S(1)}, u32[]{:S(2)}, u32[]{:S(2)}) collective-permute-start(bf16[96,1280]{1,0:T(8,128)(2,1)S(1)} %get-tuple-element.211), channel_id=1, source_target_pairs={{0,4},{2,6},{4,0},{6,2},{8,12},{10,14},{12,8},{14,10},{16,20},{18,... | collective-permute-start | bytes 737288 | tf_op jit(solution)/shard_map/ppermute | solution.py:695
  94.0 21.4 %collective-permute-start.27 = (bf16[96,1280]{1,0:T(8,128)(2,1)S(1)}, bf16[96,1280]{1,0:T(8,128)(2,1)S(1)}, u32[]{:S(2)}, u32[]{:S(2)}) collective-permute-start(bf16[96,1280]{1,0:T(8,128)(2,1)S(1)} %get-tuple-element.209), channel_id=1, source_target_pairs={{0,2},{2,0},{4,6},{6,4},{8,10},{10,8},{12,14},{14,12},{16,18},{18,... | collective-permute-start | bytes 737288 | tf_op jit(solution)/shard_map/ppermute | solution.py:695
  99.9 10.9 %collective-permute-start.18 = (bf16[416,512]{1,0:T(8,128)(2,1)S(1)}, bf16[416,512]{1,0:T(8,128)(2,1)S(1)}, u32[]{:S(2)}, u32[]{:S(2)}) collective-permute-start(bf16[416,512]{1,0:T(8,128)(2,1)S(1)} %pad_maximum_fusion), channel_id=1, source_target_pairs={{0,4},{2,6},{4,0},{6,2},{8,12},{10,14},{12,8},{14,10},{16,20},{18,... | collective-permute-start | bytes 1277960 | tf_op jit(solution)/shard_map/ppermute | solution.py:695
  103.7 7.1 %collective-permute-start.15 = (bf16[96,1280]{1,0:T(8,128)(2,1)S(1)}, bf16[96,1280]{1,0:T(8,128)(2,1)S(1)}, u32[]{:S(2)}, u32[]{:S(2)}) collective-permute-start(bf16[96,1280]{1,0:T(8,128)(2,1)S(1)} %get-tuple-element.213), channel_id=1, source_target_pairs={{0,8},{2,10},{4,12},{6,14},{8,0},{10,2},{12,4},{14,6},{16,24},{18,... | collective-permute-start | bytes 737288 | tf_op jit(solution)/shard_map/ppermute | solution.py:695
  104.4 8.0 %collective-permute-start.21 = (bf16[192,512]{1,0:T(8,128)(2,1)S(1)}, bf16[192,512]{1,0:T(8,128)(2,1)S(1)}, u32[]{:S(2)}, u32[]{:S(2)}) collective-permute-start(bf16[192,512]{1,0:T(8,128)(2,1)S(1)} %get-tuple-element.219), channel_id=1, source_target_pairs={{0,2},{2,0},{4,6},{6,4},{8,10},{10,8},{12,14},{14,12},{16,18},{18,... | collective-permute-start | bytes 589832 | tf_op jit(solution)/shard_map/ppermute | solution.py:695
  105.8 8.1 %collective-permute-start.24 = (bf16[192,512]{1,0:T(8,128)(2,1)S(1)}, bf16[192,512]{1,0:T(8,128)(2,1)S(1)}, u32[]{:S(2)}, u32[]{:S(2)}) collective-permute-start(bf16[192,512]{1,0:T(8,128)(2,1)S(1)} %get-tuple-element.217), channel_id=1, source_target_pairs={{0,4},{2,6},{4,0},{6,2},{8,12},{10,14},{12,8},{14,10},{16,20},{18,... | collective-permute-start | bytes 589832 | tf_op jit(solution)/shard_map/ppermute | solution.py:695
  110.8 15.0 %collective-permute-start.29 = (bf16[96,1280]{1,0:T(8,128)(2,1)S(1)}, bf16[96,1280]{1,0:T(8,128)(2,1)S(1)}, u32[]{:S(2)}, u32[]{:S(2)}) collective-permute-start(bf16[96,1280]{1,0:T(8,128)(2,1)S(1)} %pad_maximum_fusion.1), channel_id=1, source_target_pairs={{0,16},{2,18},{4,20},{6,22},{8,24},{10,26},{12,28},{14,30},{16,0},... | collective-permute-start | bytes 737288 | tf_op jit(solution)/shard_map/ppermute | solution.py:695
  112.4 7.7 %collective-permute-start.22 = (bf16[96,512]{1,0:T(8,128)(2,1)S(1)}, bf16[96,512]{1,0:T(8,128)(2,1)S(1)}, u32[]{:S(2)}, u32[]{:S(2)}) collective-permute-start(bf16[96,512]{1,0:T(8,128)(2,1)S(1)} %get-tuple-element.227), channel_id=1, source_target_pairs={{0,8},{2,10},{4,12},{6,14},{8,0},{10,2},{12,4},{14,6},{16,24},{18,... | collective-permute-start | bytes 294920 | tf_op jit(solution)/shard_map/ppermute | solution.py:695
  113.9 6.3 %collective-permute-start.25 = (bf16[96,512]{1,0:T(8,128)(2,1)S(1)}, bf16[96,512]{1,0:T(8,128)(2,1)S(1)}, u32[]{:S(2)}, u32[]{:S(2)}) collective-permute-start(bf16[96,512]{1,0:T(8,128)(2,1)S(1)} %get-tuple-element.225), channel_id=1, source_target_pairs={{0,2},{2,0},{4,6},{6,4},{8,10},{10,8},{12,14},{14,12},{16,18},{18,... | collective-permute-start | bytes 294920 | tf_op jit(solution)/shard_map/ppermute | solution.py:695
  115.4 4.9 %collective-permute-start.28 = (bf16[48,1280]{1,0:T(8,128)(2,1)S(1)}, bf16[48,1280]{1,0:T(8,128)(2,1)S(1)}, u32[]{:S(2)}, u32[]{:S(2)}) collective-permute-start(bf16[48,1280]{1,0:T(8,128)(2,1)S(1)} %add_convert_fusion.20), channel_id=1, source_target_pairs={{0,4},{2,6},{4,0},{6,2},{8,12},{10,14},{12,8},{14,10},{16,20},{18,... | collective-permute-start | bytes 368648 | tf_op jit(solution)/shard_map/ppermute | solution.py:695
  116.9 7.9 %collective-permute-start.19 = (bf16[224,512]{1,0:T(8,128)(2,1)S(1)}, bf16[224,512]{1,0:T(8,128)(2,1)S(1)}, u32[]{:S(2)}, u32[]{:S(2)}) collective-permute-start(bf16[224,512]{1,0:T(8,128)(2,1)S(1)} %pad_maximum_fusion.2), channel_id=1, source_target_pairs={{0,8},{2,10},{4,12},{6,14},{8,0},{10,2},{12,4},{14,6},{16,24},{18,... | collective-permute-start | bytes 688136 | tf_op jit(solution)/shard_map/ppermute | solution.py:695
  125.0 5.0 %collective-permute-start.20 = (bf16[128,512]{1,0:T(8,128)(2,1)S(1)}, bf16[128,512]{1,0:T(8,128)(2,1)S(1)}, u32[]{:S(2)}, u32[]{:S(2)}) collective-permute-start(bf16[128,512]{1,0:T(8,128)(2,1)S(1)} %pad_maximum_fusion.3), channel_id=1, source_target_pairs={{0,2},{2,0},{4,6},{6,4},{8,10},{10,8},{12,14},{14,12},{16,18},{18,... | collective-permute-start | bytes 393224 | tf_op jit(solution)/shard_map/ppermute | solution.py:695
  130.1 9.0 %collective-permute-start.26 = (bf16[176,512]{1,0:T(8,128)(2,1)S(1)}, bf16[176,512]{1,0:T(8,128)(2,1)S(1)}, u32[]{:S(2)}, u32[]{:S(2)}) collective-permute-start(bf16[176,512]{1,0:T(8,128)(2,1)S(1)} %fusion.2), channel_id=1, source_target_pairs={{0,16},{2,18},{4,20},{6,22},{8,24},{10,26},{12,28},{14,30},{16,0},... | collective-permute-start | bytes 540680 | tf_op jit(solution)/shard_map/ppermute | solution.py:695
  (11 other events, 80.3 us)

commit v6 on v5

--- a/solution.py
+++ b/solution.py
@@ -797,7 +797,7 @@
     blocks = min(dp_size, 16)
     shift = (dp_size // blocks).bit_length() - 1
     orders = ((0, 2, 1, 3), (1, 0, 2, 3), (2, 3, 0, 1))
-    turns = ((1, 2, 0, 3), (1, 0, 2, 3), (2, 1, 0, 3))
+    turns = ((1, 2, 0, 3), (1, 0, 2, 3), (2, 0, 1, 3))
     lengths = doc_lengths[0]
     seq_index = lax.axis_index("seq")
     info = jnp.stack([seq_index, lax.axis_index("dp") >> shift]).astype(jnp.int32)

time: 140 us -> 140 us (level)
  waiting for transfers between devices: 35.4 us -> 37.5 us
  starting transfers between devices: 28.9 us -> 27.1 us
    ppermute x21, waiting for transfers between devices: 33.7 us -> 35.8 us  [swap_dp(): return lax.ppermute(value, 'dp', [(i, i ^ 1 << bit) for i in range(size)])]
    ppermute x21, starting transfers between devices: 26.8 us -> 25 us  [swap_dp(): return lax.ppermute(value, 'dp', [(i, i ^ 1 << bit) for i in range(size)])]
  transfers between devices with their start and end apart: 30 -> 30, of which waited for: 10 -> 11; matrix products, arithmetic and copies ran while one was open for 3% -> 3% of each run, Pallas kernels for 34% -> 34%
where the time goes in v6:
time: 140 us
  Pallas kernels  69.7 us (50%)
  waiting for transfers between devices  37.5 us (27%)
  starting transfers between devices  27.1 us (19%)
  other arithmetic  4.74 us (3%)
    pallas_call x16, Pallas kernels, call(): pl.pallas_call(kernel, in_specs=[pl.BlockSpec(memory_space=pltpu.SMEM)] *...  65.5 us
    ppermute x21, waiting for transfers between devices, swap_dp(): return lax.ppermute(value, 'dp', [(i, i ^ 1 << bit) for i in range(size)])  35.8 us
    ppermute x21, starting transfers between devices, swap_dp(): return lax.ppermute(value, 'dp', [(i, i ^ 1 << bit) for i in range(size)])  25 us
    pallas_call x1, Pallas kernels, project_own(): pl.pallas_call(project_own_kernel, in_specs=[pl.BlockSpec(memory_space=pl...  4.16 us
    convert_element_type x18, other arithmetic, add(): (self.keep[low:high].astype(F32) + self.came[low:high].astype(F32)).astyp...  2.86 us
  transfers between devices with their start and end apart: 30, of which 11 were waited for; matrix products, arithmetic and copies ran while one was open for 3% of the time, Pallas kernels for 34%

profile of v6, /device:TPU:0, one launch (start us, length us, event | category | flops | bytes accessed | tf_op | source)
XLA Modules:
  0.0 140.2 jit_solution(10699072578305985143)
XLA Ops:
  1.3 4.2 %project_own.1 = (bf16[384,1024]{1,0:T(8,128)(2,1)S(1)}, bf16[384,1024]{1,0:T(8,128)(2,1)S(1)}, bf16[384,1024]{1,0:T(8,128)(2,1)S(1)}, bf16[1024,768]{1,0:T(8,12...) custom-call(s32[2]{0:T(128)S(1)} %pad_add_fusion.info_ref, ...), custom_call_target="tpu_custom_call" | custom-call | flops 4000000000 | bytes 8000000 | tf_op jit(solution)/shard_map/project_own/pallas_call | solution.py:146
  5.6 8.4 %attention_forward.1 = (bf16[384,1024]{1,0:T(8,128)(2,1)S(1)}, bf16[384,1024]{1,0:T(8,128)(2,1)S(1)}, bf16[384,1024]{1,0:T(8,128)(2,1)S(1)}, bf16[1024,768]{1,0:...) custom-call(s32[2]{0:T(128)S(1)} %pad_add_fusion.info_ref, ...), custom_call_target="tpu_custom_call", output_to_operand_aliasing={{0}: (2, {}), {1}: (3, {}), {2}: (4, {}), {3}: (5, {})} | custom-call | flops 300000000 | bytes 110755 | tf_op jit(solution)/shard_map/attention_forward/pallas_call | solution.py:32
  14.1 1.7 %collective-permute-done.1.came_ref = bf16[384,512]{1,0:T(8,128)(2,1)S(1)} collective-permute-done((bf16[384,512]{1,0:T(8,128)(2,1)S(1)}, bf16[384,512]{1,0:T(8,128)(2,1)S(1)}, u32[]{:S(2)}, u32[]{:S(2)}) %collective-permute-start.1) | collective-permute-done | bytes 393248 | tf_op jit(solution)/shard_map/ppermute | solution.py:690
  15.9 11.4 %ffn_forward.1 = (bf16[512,2560]{1,0:T(8,128)(2,1)S(1)}, bf16[512,2560]{1,0:T(8,128)(2,1)S(1)}, bf16[512,2560]{1,0:T(8,128)(2,1)S(1)}, bf16[512,768]{1,0:T(8,128...) custom-call(s32[2]{0:T(128)S(1)} %pad_add_fusion.info_ref, ...), custom_call_target="tpu_custom_call" | custom-call | flops 120795952 | bytes 283770 | tf_op jit(solution)/shard_map/ffn_forward/pallas_call | solution.py:32
  27.3 1.7 %weight_away.1 = bf16[768,1280]{1,0:T(8,128)(2,1)S(1)} custom-call(s32[2]{0:T(128)S(1)} %pad_add_fusion.info_ref, bf16[768,512]{1,0:T(8,128)(2,1)S(1)} %get-tuple-element.118.left_ref, bf16[512,2560]{1,0:T(8,128)(2,1)S(1)} %get-tuple-element.125.right_ref), custom_call_target="tpu_custom_call" | custom-call | flops 20132660 | bytes 39321 | tf_op jit(solution)/shard_map/weight_away/pallas_call | solution.py:32
  29.2 4.0 %swiglu_away.1 = (bf16[512,2560]{1,0:T(8,128)(2,1)S(1)}, bf16[512,2560]{1,0:T(8,128)(2,1)S(1)}, bf16[768,1280]{1,0:T(8,128)(2,1)S(1)}, bf16[768,1280]{1,0:T(8,128)(2,1)S(1)}) custom-call(s32[2]{0:T(128)S(1)} %pad_add_fusion.info_ref, bf16[512,768]{1,0:T(8,128)(2,1)S(1)} %get-tuple-element.127.dm_ref, bf16[2560,768]{1,0:T(8,128)(2,1)S(1)} %copy-done, ...), custom_call_target="tpu_custom_call" | custom-call | flops 60397976 | bytes 183500 | tf_op jit(solution)/shard_map/swiglu_away/pallas_call | solution.py:32
  33.8 2.7 %weight_mine.3 = (bf16[384,1280]{1,0:T(8,128)(2,1)S(1)}, bf16[384,1280]{1,0:T(8,128)(2,1)}) custom-call(s32[2]{0:T(128)S(1)} %pad_add_fusion.info_ref, bf16[768,512]{1,0:T(8,128)(2,1)S(1)} %get-tuple-element.118.left_ref, bf16[512,2560]{1,0:T(8,128)(2,1)S(1)} %get-tuple-element.125.right_ref, bf16[768,1280]{1,0:T(8,128)(2,1)S(1)} %collective-permute-done.2.rest_0_), custom_call_target="tpu_custom_call" | custom-call | flops 20132660 | bytes 39321 | tf_op jit(solution)/shard_map/weight_mine/pallas_call | solution.py:32
  36.5 3.0 %collective-permute-start.6 = (bf16[384,1280]{1,0:T(8,128)(2,1)}, bf16[384,1280]{1,0:T(8,128)(2,1)}, u32[]{:S(2)}, u32[]{:S(2)}) collective-permute-start(bf16[384,1280]{1,0:T(8,128)(2,1)} %get-tuple-element.126), channel_id=1, source_target_pairs={{0,8},{2,10},{4,12},{6,14},{8,0},{10,2},{12,4},{14,6},{16,24},{18,... | collective-permute-start | bytes 2949128 | tf_op jit(solution)/shard_map/ppermute | solution.py:695
  39.5 2.0 %swiglu_mine.1 = (bf16[512,2560]{1,0:T(8,128)(2,1)S(1)}, bf16[512,2560]{1,0:T(8,128)(2,1)S(1)}) custom-call(s32[2]{0:T(128)S(1)} %pad_add_fusion.info_ref, bf16[512,768]{1,0:T(8,128)(2,1)S(1)} %get-tuple-element.127.dm_ref, bf16[2560,768]{1,0:T(8,128)(2,1)S(1)} %copy-done, ...), custom_call_target="tpu_custom_call", output_to_operand_aliasing={{0}: (5, {}), {1}: (6, {})} | custom-call | flops 20132660 | bytes 104857 | tf_op jit(solution)/shard_map/swiglu_mine/pallas_call | solution.py:32
  41.5 1.7 %weight_mine.4 = (bf16[384,1280]{1,0:T(8,128)(2,1)S(1)}, bf16[384,1280]{1,0:T(8,128)(2,1)S(1)}) custom-call(s32[2]{0:T(128)S(1)} %pad_add_fusion.info_ref, bf16[768,512]{1,0:T(8,128)(2,1)S(1)} %get-tuple-element.140.hbt_ref.left_ref, bf16[512,2560]{1,0:T(8,128)(2,1)S(1)} %get-tuple-element.132.right_ref.dgt_ref, ...), custom_call_target="tpu_custom_call" | custom-call | flops 20132660 | bytes 39321 | tf_op jit(solution)/shard_map/weight_mine/pallas_call | solution.py:32
  43.2 1.5 %collective-permute-start.7 = (bf16[384,1280]{1,0:T(8,128)(2,1)S(1)}, bf16[384,1280]{1,0:T(8,128)(2,1)S(1)}, u32[]{:S(2)}, u32[]{:S(2)}) collective-permute-start(bf16[384,1280]{1,0:T(8,128)(2,1)S(1)} %get-tuple-element.131), channel_id=1, source_target_pairs={{0,2},{2,0},{4,6},{6,4},{8,10},{10,8},{12,14},{14,12},{16,18},{18,... | collective-permute-start | bytes 2949128 | tf_op jit(solution)/shard_map/ppermute | solution.py:695
  44.8 7.4 %norm_one_back.1 = (f32[512,768]{1,0:T(8,128)S(1)}, bf16[768,512]{1,0:T(8,128)(2,1)S(1)}, bf16[384,512]{1,0:T(8,128)(2,1)S(1)}, bf16[384,512]{1,0:T(8,128)(2,1)S(1)}, f32[16,512]{1,0:T(8,128)S(1)}) custom-call(s32[2]{0:T(128)S(1)} %pad_add_fusion.info_ref, bf16[512,2560]{1,0:T(8,128)(2,1)S(1)} %get-tuple-element.132.right_ref.dgt_ref, ...), custom_call_target="tpu_custom_call" | custom-call | flops 80530640 | bytes 63569 | tf_op jit(solution)/shard_map/norm_one_back/pallas_call | solution.py:32
  52.8 1.7 %weight_mine.5 = (bf16[384,1280]{1,0:T(8,128)(2,1)S(1)}, bf16[384,1280]{1,0:T(8,128)(2,1)S(1)}) custom-call(s32[2]{0:T(128)S(1)} %pad_add_fusion.info_ref, bf16[768,512]{1,0:T(8,128)(2,1)S(1)} %get-tuple-element.140.hbt_ref.left_ref, bf16[512,2560]{1,0:T(8,128)(2,1)S(1)} %get-tuple-element.133.dup_ref.right_ref, ...), custom_call_target="tpu_custom_call" | custom-call | flops 20132660 | bytes 39321 | tf_op jit(solution)/shard_map/weight_mine/pallas_call | solution.py:32
  55.7 1.6 %collective-permute-start.10 = (bf16[384,1280]{1,0:T(8,128)(2,1)S(1)}, bf16[384,1280]{1,0:T(8,128)(2,1)S(1)}, u32[]{:S(2)}, u32[]{:S(2)}) collective-permute-start(bf16[384,1280]{1,0:T(8,128)(2,1)S(1)} %get-tuple-element.142), channel_id=1, source_target_pairs={{0,4},{2,6},{4,0},{6,2},{8,12},{10,14},{12,8},{14,10},{16,20},{18,... | collective-permute-start | bytes 2949128 | tf_op jit(solution)/shard_map/ppermute | solution.py:695
  57.3 7.0 %attention_backward.2 = (bf16[384,1024]{1,0:T(8,128)(2,1)S(1)}, bf16[384,1024]{1,0:T(8,128)(2,1)S(1)}, bf16[384,1024]{1,0:T(8,128)(2,1)S(1)}) custom-call(s32[2]{0:T(128)S(1)} %pad_add_fusion.info_ref, s32[4]{0:T(128)S(1)} %bitcast.11, bf16[384,1024]{1,0:T(8,128)(2,1)S(1)} %get-tuple-element.113.q_ref, bf16[384,1024]{1,0:T(8,128)(2,1)S(1)} %get-tuple-element.114.k_ref, ...), custom_call_target="tpu_custom_call" | custom-call | flops 240000000 | bytes 47185 | tf_op jit(solution)/shard_map/attention_backward/pallas_call | solution.py:32
  64.2 1.4 %add_convert_fusion = (bf16[192,1280]{1,0:T(8,128)(2,1)S(1)}, bf16[192,1280]{1,0:T(8,128)(2,1)S(1)}) fusion(bf16[384,1280]{1,0:T(8,128)(2,1)} %collective-permute-done.6, bf16[384,1280]{1,0:T(8,128)(2,1)S(1)} %get-tuple-element.151), kind=kLoop, calls=%fused_computation | loop fusion | flops 1966080 | bytes 2949120 | tf_op jit(solution)/shard_map/convert_element_type | solution.py:732
  65.6 2.6 %collective-permute-start.16 = (bf16[192,1280]{1,0:T(8,128)(2,1)S(1)}, bf16[192,1280]{1,0:T(8,128)(2,1)S(1)}, u32[]{:S(2)}, u32[]{:S(2)}) collective-permute-start(bf16[192,1280]{1,0:T(8,128)(2,1)S(1)} %get-tuple-element.205), channel_id=1, source_target_pairs={{0,16},{2,18},{4,20},{6,22},{8,24},{10,26},{12,28},{14,30},{16,0},... | collective-permute-start | bytes 1474568 | tf_op jit(solution)/shard_map/ppermute | solution.py:695
  69.1 6.7 %attention_backward.3 = (bf16[384,1024]{1,0:T(8,128)(2,1)S(1)}, bf16[384,1024]{1,0:T(8,128)(2,1)S(1)}, bf16[384,1024]{1,0:T(8,128)(2,1)S(1)}) custom-call(s32[2]{0:T(128)S(1)} %pad_add_fusion.info_ref, s32[4]{0:T(128)S(1)} %bitcast.12, bf16[384,1024]{1,0:T(8,128)(2,1)S(1)} %get-tuple-element.113.q_ref, ...), custom_call_target="tpu_custom_call", output_to_operand_aliasing={{0}: (11, {}), {1}: (12, {}), {2}: (13, {})} | custom-call | flops 240000000 | bytes 47185 | tf_op jit(solution)/shard_map/attention_backward/pallas_call | solution.py:32
  75.8 3.8 %project_grad.1 = (bf16[384,512]{1,0:T(8,128)(2,1)S(1)}, bf16[384,512]{1,0:T(8,128)(2,1)S(1)}, bf16[384,512]{1,0:T(8,128)(2,1)S(1)}, bf16[384,512]{1,0:T(8,128)(...) custom-call(s32[2]{0:T(128)S(1)} %pad_add_fusion.info_ref, ...), custom_call_target="tpu_custom_call" | custom-call | flops 36238784 | bytes 47185 | tf_op jit(solution)/shard_map/project_grad/pallas_call | solution.py:32
  80.2 1.6 %collective-permute-start.23 = (bf16[384,512]{1,0:T(8,128)(2,1)S(1)}, bf16[384,512]{1,0:T(8,128)(2,1)S(1)}, u32[]{:S(2)}, u32[]{:S(2)}) collective-permute-start(bf16[384,512]{1,0:T(8,128)(2,1)S(1)} %get-tuple-element.171), channel_id=1, source_target_pairs={{0,8},{2,10},{4,12},{6,14},{8,0},{10,2},{12,4},{14,6},{16,24},{18,... | collective-permute-start | bytes 1179656 | tf_op jit(solution)/shard_map/ppermute | solution.py:695
  83.1 1.9 %stream_grad.2 = bf16[768,512]{1,0:T(8,128)(2,1)S(1)} custom-call(s32[2]{0:T(128)S(1)} %pad_add_fusion.info_ref, bf16[384,1024]{1,0:T(8,128)(2,1)S(1)} %get-tuple-element.174.dq_ref, bf16[384,1024]{1,0:T(8,128)(2,1)S(1)} %get-tuple-element.175.dk_ref, bf16[384,1024]{1,0:T(8,128)(2,1)S(1)} %get-tuple-element.176.dv_ref, ...), custom_call_target="tpu_custom_call" | custom-call | flops 18119392 | bytes 15728 | tf_op jit(solution)/shard_map/stream_grad/pallas_call | solution.py:32
  85.0 5.2 %collective-permute-done.9 = bf16[384,512]{1,0:T(8,128)(2,1)S(1)} collective-permute-done((bf16[384,512]{1,0:T(8,128)(2,1)S(1)}, bf16[384,512]{1,0:T(8,128)(2,1)S(1)}, u32[]{:S(2)}, u32[]{:S(2)}) %collective-permute-start.9) | collective-permute-done | bytes 393248 | tf_op jit(solution)/shard_map/ppermute | solution.py:695
  90.2 2.9 %collective-permute-done.12 = bf16[192,1280]{1,0:T(8,128)(2,1)S(1)} collective-permute-done((bf16[192,1280]{1,0:T(8,128)(2,1)S(1)}, bf16[192,1280]{1,0:T(8,128)(2,1)S(1)}, u32[]{:S(2)}, u32[]{:S(2)}) %collective-permute-start.12) | collective-permute-done | bytes 491552 | tf_op jit(solution)/shard_map/ppermute | solution.py:695
  95.1 4.8 %collective-permute-done.13 = bf16[96,1280]{1,0:T(8,128)(2,1)S(1)} collective-permute-done((bf16[96,1280]{1,0:T(8,128)(2,1)S(1)}, bf16[96,1280]{1,0:T(8,128)(2,1)S(1)}, u32[]{:S(2)}, u32[]{:S(2)}) %collective-permute-start.13) | collective-permute-done | bytes 245792 | tf_op jit(solution)/shard_map/ppermute | solution.py:695
  100.4 3.1 %stream_grad.3 = bf16[512,768]{1,0:T(8,128)(2,1)} custom-call(s32[2]{0:T(128)S(1)} %pad_add_fusion.info_ref, bf16[384,1024]{1,0:T(8,128)(2,1)S(1)} %get-tuple-element.174.dq_ref, bf16[384,1024]{1,0:T(8,128)(2,1)S(1)} %get-tuple-element.175.dk_ref, bf16[384,1024]{1,0:T(8,128)(2,1)S(1)} %get-tuple-element.176.dv_ref, ...), custom_call_target="tpu_custom_call" | custom-call | flops 18119392 | bytes 15728 | tf_op jit(solution)/shard_map/stream_grad/pallas_call | solution.py:32
  106.6 2.0 %collective-permute-done.18 = bf16[416,512]{1,0:T(8,128)(2,1)S(1)} collective-permute-done((bf16[416,512]{1,0:T(8,128)(2,1)S(1)}, bf16[416,512]{1,0:T(8,128)(2,1)S(1)}, u32[]{:S(2)}, u32[]{:S(2)}) %collective-permute-start.18) | collective-permute-done | bytes 426016 | tf_op jit(solution)/shard_map/ppermute | solution.py:695
  110.0 1.6 %collective-permute-start.29 = (bf16[96,1280]{1,0:T(8,128)(2,1)S(1)}, bf16[96,1280]{1,0:T(8,128)(2,1)S(1)}, u32[]{:S(2)}, u32[]{:S(2)}) collective-permute-start(bf16[96,1280]{1,0:T(8,128)(2,1)S(1)} %pad_maximum_fusion.1), channel_id=1, source_target_pairs={{0,16},{2,18},{4,20},{6,22},{8,24},{10,26},{12,28},{14,30},{16,0},... | collective-permute-start | bytes 737288 | tf_op jit(solution)/shard_map/ppermute | solution.py:695
  113.5 1.6 %collective-permute-start.25 = (bf16[96,512]{1,0:T(8,128)(2,1)S(1)}, bf16[96,512]{1,0:T(8,128)(2,1)S(1)}, u32[]{:S(2)}, u32[]{:S(2)}) collective-permute-start(bf16[96,512]{1,0:T(8,128)(2,1)S(1)} %get-tuple-element.225), channel_id=1, source_target_pairs={{0,4},{2,6},{4,0},{6,2},{8,12},{10,14},{12,8},{14,10},{16,20},{18,... | collective-permute-start | bytes 294920 | tf_op jit(solution)/shard_map/ppermute | solution.py:695
  116.2 3.8 %collective-permute-done.22 = bf16[96,512]{1,0:T(8,128)(2,1)S(1)} collective-permute-done((bf16[96,512]{1,0:T(8,128)(2,1)S(1)}, bf16[96,512]{1,0:T(8,128)(2,1)S(1)}, u32[]{:S(2)}, u32[]{:S(2)}) %collective-permute-start.22) | collective-permute-done | bytes 98336 | tf_op jit(solution)/shard_map/ppermute | solution.py:695
  120.9 4.3 %collective-permute-done.19 = bf16[224,512]{1,0:T(8,128)(2,1)S(1)} collective-permute-done((bf16[224,512]{1,0:T(8,128)(2,1)S(1)}, bf16[224,512]{1,0:T(8,128)(2,1)S(1)}, u32[]{:S(2)}, u32[]{:S(2)}) %collective-permute-start.19) | collective-permute-done | bytes 229408 | tf_op jit(solution)/shard_map/ppermute | solution.py:695
  127.1 3.3 %collective-permute-done.20 = bf16[128,512]{1,0:T(8,128)(2,1)S(1)} collective-permute-done((bf16[128,512]{1,0:T(8,128)(2,1)S(1)}, bf16[128,512]{1,0:T(8,128)(2,1)S(1)}, u32[]{:S(2)}, u32[]{:S(2)}) %collective-permute-start.20) | collective-permute-done | bytes 131104 | tf_op jit(solution)/shard_map/ppermute | solution.py:695
  131.6 7.8 %collective-permute-done.26.came_ref = bf16[176,512]{1,0:T(8,128)(2,1)S(1)} collective-permute-done((bf16[176,512]{1,0:T(8,128)(2,1)S(1)}, bf16[176,512]{1,0:T(8,128)(2,1)S(1)}, u32[]{:S(2)}, u32[]{:S(2)}) %collective-permute-start.26) | collective-permute-done | bytes 180256 | tf_op jit(solution)/shard_map/ppermute | solution.py:695
  (106 shorter events, 20.5 us)
Async XLA Ops:
  0.6 4.8 %collective-permute-start = (bf16[512,768]{1,0:T(8,128)(2,1)}, bf16[512,768]{1,0:T(8,128)(2,1)S(1)}, u32[]{:S(2)}, u32[]{:S(2)}) collective-permute-start(bf16[512,768]{1,0:T(8,128)(2,1)} %x_ref.1), channel_id=1, source_target_pairs={{0,1},{1,0},{2,3},{3,2},{4,5},{5,4},{6,7},{7,6},{8,9},{9,8},{10,11... | collective-permute-start | bytes 2359304 | tf_op jit(solution)/shard_map/ppermute | solution.py:690
  1.3 14.5 %copy-start.1 = (bf16[768,2560]{1,0:T(8,128)(2,1)S(1)}, bf16[768,2560]{1,0:T(8,128)(2,1)}, u32[]{:S(2)}) copy-start(bf16[768,2560]{1,0:T(8,128)(2,1)} %wg_ref.3) | copy-start | bytes 11796484
  1.3 14.5 %copy-start.2 = (bf16[768,2560]{1,0:T(8,128)(2,1)S(1)}, bf16[768,2560]{1,0:T(8,128)(2,1)}, u32[]{:S(2)}) copy-start(bf16[768,2560]{1,0:T(8,128)(2,1)} %wu_ref.3) | copy-start | bytes 11796484
  14.0 1.8 %collective-permute-start.1 = (bf16[384,512]{1,0:T(8,128)(2,1)S(1)}, bf16[384,512]{1,0:T(8,128)(2,1)S(1)}, u32[]{:S(2)}, u32[]{:S(2)}) collective-permute-start(bf16[384,512]{1,0:T(8,128)(2,1)S(1)} %get-tuple-element.111), channel_id=1, source_target_pairs={{0,1},{1,0},{2,3},{3,2},{4,5},{5,4},{6,7},{7,6},{8,9},{9,8},{10,11... | collective-permute-start | bytes 1179656 | tf_op jit(solution)/shard_map/ppermute | solution.py:690
  29.0 4.8 %collective-permute-start.2 = (bf16[768,1280]{1,0:T(8,128)(2,1)S(1)}, bf16[768,1280]{1,0:T(8,128)(2,1)S(1)}, u32[]{:S(2)}, u32[]{:S(2)}) collective-permute-start(bf16[768,1280]{1,0:T(8,128)(2,1)S(1)} %weight_away.1), channel_id=1, source_target_pairs={{0,1},{1,0},{2,3},{3,2},{4,5},{5,4},{6,7},{7,6},{8,9},{9,8},{10,11... | collective-permute-start | bytes 5898248 | tf_op jit(solution)/shard_map/ppermute | solution.py:690
  33.2 8.2 %collective-permute-start.3 = (bf16[768,1280]{1,0:T(8,128)(2,1)S(1)}, bf16[768,1280]{1,0:T(8,128)(2,1)S(1)}, u32[]{:S(2)}, u32[]{:S(2)}) collective-permute-start(bf16[768,1280]{1,0:T(8,128)(2,1)S(1)} %get-tuple-element.124), channel_id=1, source_target_pairs={{0,1},{1,0},{2,3},{3,2},{4,5},{5,4},{6,7},{7,6},{8,9},{9,8},{10,11... | collective-permute-start | bytes 5898248 | tf_op jit(solution)/shard_map/ppermute | solution.py:690
  33.7 19.1 %collective-permute-start.4 = (bf16[768,1280]{1,0:T(8,128)(2,1)S(1)}, bf16[768,1280]{1,0:T(8,128)(2,1)S(1)}, u32[]{:S(2)}, u32[]{:S(2)}) collective-permute-start(bf16[768,1280]{1,0:T(8,128)(2,1)S(1)} %get-tuple-element.141), channel_id=1, source_target_pairs={{0,1},{1,0},{2,3},{3,2},{4,5},{5,4},{6,7},{7,6},{8,9},{9,8},{10,11... | collective-permute-start | bytes 5898248 | tf_op jit(solution)/shard_map/ppermute | solution.py:690
  36.5 27.7 %collective-permute-start.6 = (bf16[384,1280]{1,0:T(8,128)(2,1)}, bf16[384,1280]{1,0:T(8,128)(2,1)}, u32[]{:S(2)}, u32[]{:S(2)}) collective-permute-start(bf16[384,1280]{1,0:T(8,128)(2,1)} %get-tuple-element.126), channel_id=1, source_target_pairs={{0,8},{2,10},{4,12},{6,14},{8,0},{10,2},{12,4},{14,6},{16,24},{18,... | collective-permute-start | bytes 2949128 | tf_op jit(solution)/shard_map/ppermute | solution.py:695
  43.2 25.1 %collective-permute-start.7 = (bf16[384,1280]{1,0:T(8,128)(2,1)S(1)}, bf16[384,1280]{1,0:T(8,128)(2,1)S(1)}, u32[]{:S(2)}, u32[]{:S(2)}) collective-permute-start(bf16[384,1280]{1,0:T(8,128)(2,1)S(1)} %get-tuple-element.131), channel_id=1, source_target_pairs={{0,2},{2,0},{4,6},{6,4},{8,10},{10,8},{12,14},{14,12},{16,18},{18,... | collective-permute-start | bytes 2949128 | tf_op jit(solution)/shard_map/ppermute | solution.py:695
  52.2 5.0 %collective-permute-start.5 = (bf16[384,512]{1,0:T(8,128)(2,1)S(1)}, bf16[384,512]{1,0:T(8,128)(2,1)S(1)}, u32[]{:S(2)}, u32[]{:S(2)}) collective-permute-start(bf16[384,512]{1,0:T(8,128)(2,1)S(1)} %get-tuple-element.139), channel_id=1, source_target_pairs={{0,1},{1,0},{2,3},{3,2},{4,5},{5,4},{6,7},{7,6},{8,9},{9,8},{10,11... | collective-permute-start | bytes 1179656 | tf_op jit(solution)/shard_map/ppermute | solution.py:690
  52.3 3.4 %collective-permute-start.17 = (f32[16,512]{1,0:T(8,128)S(1)}, f32[16,512]{1,0:T(8,128)S(1)}, u32[]{:S(2)}, u32[]{:S(2)}) collective-permute-start(f32[16,512]{1,0:T(8,128)S(1)} %get-tuple-element.183), channel_id=1, source_target_pairs={{0,1},{1,0},{2,3},{3,2},{4,5},{5,4},{6,7},{7,6},{8,9},{9,8},{10,11... | collective-permute-start | bytes 98312 | tf_op jit(solution)/shard_map/ppermute | solution.py:690
  55.5 20.3 %collective-permute-start.8 = (bf16[768,384]{1,0:T(8,128)(2,1)S(1)}, bf16[768,384]{1,0:T(8,128)(2,1)S(1)}, u32[]{:S(2)}, u32[]{:S(2)}) collective-permute-start(bf16[768,384]{1,0:T(8,128)(2,1)S(1)} %get-tuple-element.144), channel_id=1, source_target_pairs={{0,1},{1,0},{2,3},{3,2},{4,5},{5,4},{6,7},{7,6},{8,9},{9,8},{10,11... | collective-permute-start | bytes 1769480 | tf_op jit(solution)/shard_map/ppermute | solution.py:690
  55.7 26.0 %collective-permute-start.10 = (bf16[384,1280]{1,0:T(8,128)(2,1)S(1)}, bf16[384,1280]{1,0:T(8,128)(2,1)S(1)}, u32[]{:S(2)}, u32[]{:S(2)}) collective-permute-start(bf16[384,1280]{1,0:T(8,128)(2,1)S(1)} %get-tuple-element.142), channel_id=1, source_target_pairs={{0,4},{2,6},{4,0},{6,2},{8,12},{10,14},{12,8},{14,10},{16,20},{18,... | collective-permute-start | bytes 2949128 | tf_op jit(solution)/shard_map/ppermute | solution.py:695
  65.6 28.2 %collective-permute-start.16 = (bf16[192,1280]{1,0:T(8,128)(2,1)S(1)}, bf16[192,1280]{1,0:T(8,128)(2,1)S(1)}, u32[]{:S(2)}, u32[]{:S(2)}) collective-permute-start(bf16[192,1280]{1,0:T(8,128)(2,1)S(1)} %get-tuple-element.205), channel_id=1, source_target_pairs={{0,16},{2,18},{4,20},{6,22},{8,24},{10,26},{12,28},{14,30},{16,0},... | collective-permute-start | bytes 1474568 | tf_op jit(solution)/shard_map/ppermute | solution.py:695
  68.5 24.6 %collective-permute-start.12 = (bf16[192,1280]{1,0:T(8,128)(2,1)S(1)}, bf16[192,1280]{1,0:T(8,128)(2,1)S(1)}, u32[]{:S(2)}, u32[]{:S(2)}) collective-permute-start(bf16[192,1280]{1,0:T(8,128)(2,1)S(1)} %get-tuple-element.207), channel_id=1, source_target_pairs={{0,8},{2,10},{4,12},{6,14},{8,0},{10,2},{12,4},{14,6},{16,24},{18,... | collective-permute-start | bytes 1474568 | tf_op jit(solution)/shard_map/ppermute | solution.py:695
  79.6 10.7 %collective-permute-start.9 = (bf16[384,512]{1,0:T(8,128)(2,1)S(1)}, bf16[384,512]{1,0:T(8,128)(2,1)S(1)}, u32[]{:S(2)}, u32[]{:S(2)}) collective-permute-start(bf16[384,512]{1,0:T(8,128)(2,1)S(1)} %get-tuple-element.160), channel_id=1, source_target_pairs={{0,4},{2,6},{4,0},{6,2},{8,12},{10,14},{12,8},{14,10},{16,20},{18,... | collective-permute-start | bytes 1179656 | tf_op jit(solution)/shard_map/ppermute | solution.py:695
  80.2 25.5 %collective-permute-start.23 = (bf16[384,512]{1,0:T(8,128)(2,1)S(1)}, bf16[384,512]{1,0:T(8,128)(2,1)S(1)}, u32[]{:S(2)}, u32[]{:S(2)}) collective-permute-start(bf16[384,512]{1,0:T(8,128)(2,1)S(1)} %get-tuple-element.171), channel_id=1, source_target_pairs={{0,8},{2,10},{4,12},{6,14},{8,0},{10,2},{12,4},{14,6},{16,24},{18,... | collective-permute-start | bytes 1179656 | tf_op jit(solution)/shard_map/ppermute | solution.py:695
  82.0 21.6 %collective-permute-start.14 = (bf16[192,1280]{1,0:T(8,128)(2,1)S(1)}, bf16[192,1280]{1,0:T(8,128)(2,1)S(1)}, u32[]{:S(2)}, u32[]{:S(2)}) collective-permute-start(bf16[192,1280]{1,0:T(8,128)(2,1)S(1)} %get-tuple-element.203), channel_id=1, source_target_pairs={{0,2},{2,0},{4,6},{6,4},{8,10},{10,8},{12,14},{14,12},{16,18},{18,... | collective-permute-start | bytes 1474568 | tf_op jit(solution)/shard_map/ppermute | solution.py:695
  90.2 10.2 %collective-permute-start.11 = (bf16[768,512]{1,0:T(8,128)(2,1)S(1)}, bf16[768,512]{1,0:T(8,128)(2,1)S(1)}, u32[]{:S(2)}, u32[]{:S(2)}) collective-permute-start(bf16[768,512]{1,0:T(8,128)(2,1)S(1)} %stream_grad.2), channel_id=1, source_target_pairs={{0,1},{1,0},{2,3},{3,2},{4,5},{5,4},{6,7},{7,6},{8,9},{9,8},{10,11... | collective-permute-start | bytes 2359304 | tf_op jit(solution)/shard_map/ppermute | solution.py:690
  93.3 6.6 %collective-permute-start.13 = (bf16[96,1280]{1,0:T(8,128)(2,1)S(1)}, bf16[96,1280]{1,0:T(8,128)(2,1)S(1)}, u32[]{:S(2)}, u32[]{:S(2)}) collective-permute-start(bf16[96,1280]{1,0:T(8,128)(2,1)S(1)} %get-tuple-element.211), channel_id=1, source_target_pairs={{0,4},{2,6},{4,0},{6,2},{8,12},{10,14},{12,8},{14,10},{16,20},{18,... | collective-permute-start | bytes 737288 | tf_op jit(solution)/shard_map/ppermute | solution.py:695
  94.0 21.1 %collective-permute-start.27 = (bf16[96,1280]{1,0:T(8,128)(2,1)S(1)}, bf16[96,1280]{1,0:T(8,128)(2,1)S(1)}, u32[]{:S(2)}, u32[]{:S(2)}) collective-permute-start(bf16[96,1280]{1,0:T(8,128)(2,1)S(1)} %get-tuple-element.209), channel_id=1, source_target_pairs={{0,2},{2,0},{4,6},{6,4},{8,10},{10,8},{12,14},{14,12},{16,18},{18,... | collective-permute-start | bytes 737288 | tf_op jit(solution)/shard_map/ppermute | solution.py:695
  99.9 8.8 %collective-permute-start.18 = (bf16[416,512]{1,0:T(8,128)(2,1)S(1)}, bf16[416,512]{1,0:T(8,128)(2,1)S(1)}, u32[]{:S(2)}, u32[]{:S(2)}) collective-permute-start(bf16[416,512]{1,0:T(8,128)(2,1)S(1)} %pad_maximum_fusion), channel_id=1, source_target_pairs={{0,4},{2,6},{4,0},{6,2},{8,12},{10,14},{12,8},{14,10},{16,20},{18,... | collective-permute-start | bytes 1277960 | tf_op jit(solution)/shard_map/ppermute | solution.py:695
  103.7 6.3 %collective-permute-start.15 = (bf16[96,1280]{1,0:T(8,128)(2,1)S(1)}, bf16[96,1280]{1,0:T(8,128)(2,1)S(1)}, u32[]{:S(2)}, u32[]{:S(2)}) collective-permute-start(bf16[96,1280]{1,0:T(8,128)(2,1)S(1)} %get-tuple-element.213), channel_id=1, source_target_pairs={{0,8},{2,10},{4,12},{6,14},{8,0},{10,2},{12,4},{14,6},{16,24},{18,... | collective-permute-start | bytes 737288 | tf_op jit(solution)/shard_map/ppermute | solution.py:695
  104.4 7.4 %collective-permute-start.21 = (bf16[192,512]{1,0:T(8,128)(2,1)S(1)}, bf16[192,512]{1,0:T(8,128)(2,1)S(1)}, u32[]{:S(2)}, u32[]{:S(2)}) collective-permute-start(bf16[192,512]{1,0:T(8,128)(2,1)S(1)} %get-tuple-element.219), channel_id=1, source_target_pairs={{0,2},{2,0},{4,6},{6,4},{8,10},{10,8},{12,14},{14,12},{16,18},{18,... | collective-permute-start | bytes 589832 | tf_op jit(solution)/shard_map/ppermute | solution.py:695
  105.8 7.6 %collective-permute-start.24 = (bf16[192,512]{1,0:T(8,128)(2,1)S(1)}, bf16[192,512]{1,0:T(8,128)(2,1)S(1)}, u32[]{:S(2)}, u32[]{:S(2)}) collective-permute-start(bf16[192,512]{1,0:T(8,128)(2,1)S(1)} %get-tuple-element.217), channel_id=1, source_target_pairs={{0,2},{2,0},{4,6},{6,4},{8,10},{10,8},{12,14},{14,12},{16,18},{18,... | collective-permute-start | bytes 589832 | tf_op jit(solution)/shard_map/ppermute | solution.py:695
  110.0 16.2 %collective-permute-start.29 = (bf16[96,1280]{1,0:T(8,128)(2,1)S(1)}, bf16[96,1280]{1,0:T(8,128)(2,1)S(1)}, u32[]{:S(2)}, u32[]{:S(2)}) collective-permute-start(bf16[96,1280]{1,0:T(8,128)(2,1)S(1)} %pad_maximum_fusion.1), channel_id=1, source_target_pairs={{0,16},{2,18},{4,20},{6,22},{8,24},{10,26},{12,28},{14,30},{16,0},... | collective-permute-start | bytes 737288 | tf_op jit(solution)/shard_map/ppermute | solution.py:695
  111.8 8.3 %collective-permute-start.22 = (bf16[96,512]{1,0:T(8,128)(2,1)S(1)}, bf16[96,512]{1,0:T(8,128)(2,1)S(1)}, u32[]{:S(2)}, u32[]{:S(2)}) collective-permute-start(bf16[96,512]{1,0:T(8,128)(2,1)S(1)} %get-tuple-element.227), channel_id=1, source_target_pairs={{0,8},{2,10},{4,12},{6,14},{8,0},{10,2},{12,4},{14,6},{16,24},{18,... | collective-permute-start | bytes 294920 | tf_op jit(solution)/shard_map/ppermute | solution.py:695
  113.5 6.6 %collective-permute-start.25 = (bf16[96,512]{1,0:T(8,128)(2,1)S(1)}, bf16[96,512]{1,0:T(8,128)(2,1)S(1)}, u32[]{:S(2)}, u32[]{:S(2)}) collective-permute-start(bf16[96,512]{1,0:T(8,128)(2,1)S(1)} %get-tuple-element.225), channel_id=1, source_target_pairs={{0,4},{2,6},{4,0},{6,2},{8,12},{10,14},{12,8},{14,10},{16,20},{18,... | collective-permute-start | bytes 294920 | tf_op jit(solution)/shard_map/ppermute | solution.py:695
  115.1 5.0 %collective-permute-start.28 = (bf16[48,1280]{1,0:T(8,128)(2,1)S(1)}, bf16[48,1280]{1,0:T(8,128)(2,1)S(1)}, u32[]{:S(2)}, u32[]{:S(2)}) collective-permute-start(bf16[48,1280]{1,0:T(8,128)(2,1)S(1)} %add_convert_fusion.20), channel_id=1, source_target_pairs={{0,4},{2,6},{4,0},{6,2},{8,12},{10,14},{12,8},{14,10},{16,20},{18,... | collective-permute-start | bytes 368648 | tf_op jit(solution)/shard_map/ppermute | solution.py:695
  115.7 9.5 %collective-permute-start.19 = (bf16[224,512]{1,0:T(8,128)(2,1)S(1)}, bf16[224,512]{1,0:T(8,128)(2,1)S(1)}, u32[]{:S(2)}, u32[]{:S(2)}) collective-permute-start(bf16[224,512]{1,0:T(8,128)(2,1)S(1)} %pad_maximum_fusion.2), channel_id=1, source_target_pairs={{0,8},{2,10},{4,12},{6,14},{8,0},{10,2},{12,4},{14,6},{16,24},{18,... | collective-permute-start | bytes 688136 | tf_op jit(solution)/shard_map/ppermute | solution.py:695
  125.3 5.0 %collective-permute-start.20 = (bf16[128,512]{1,0:T(8,128)(2,1)S(1)}, bf16[128,512]{1,0:T(8,128)(2,1)S(1)}, u32[]{:S(2)}, u32[]{:S(2)}) collective-permute-start(bf16[128,512]{1,0:T(8,128)(2,1)S(1)} %pad_maximum_fusion.3), channel_id=1, source_target_pairs={{0,2},{2,0},{4,6},{6,4},{8,10},{10,8},{12,14},{14,12},{16,18},{18,... | collective-permute-start | bytes 393224 | tf_op jit(solution)/shard_map/ppermute | solution.py:695
  130.5 8.9 %collective-permute-start.26 = (bf16[176,512]{1,0:T(8,128)(2,1)S(1)}, bf16[176,512]{1,0:T(8,128)(2,1)S(1)}, u32[]{:S(2)}, u32[]{:S(2)}) collective-permute-start(bf16[176,512]{1,0:T(8,128)(2,1)S(1)} %fusion.2), channel_id=1, source_target_pairs={{0,16},{2,18},{4,20},{6,22},{8,24},{10,26},{12,28},{14,30},{16,0},... | collective-permute-start | bytes 540680 | tf_op jit(solution)/shard_map/ppermute | solution.py:695
  (11 other events, 80.3 us)
